TPU v7x, 32 devices: a whole 2x2x4 slice. The times are simulated.
32 devices in a mesh: groups: 1, ctx: 16 (over z, y, x), exp: 2 (over core).
Axes of the slice: x: 2, y: 2, z: 4, core: 2. Of those that a mesh axis runs over, the one named last changes fastest.
Arguments:
- queries: bfloat16 [2048, 2048], P(('groups', 'ctx'), 'exp'), may hold values from -40 to 40
- key_rows: bfloat16 [2048, 256], P(('groups', 'ctx'), 'exp'), may hold values from -15 to 15
- value_rows: bfloat16 [2048, 256], P(('groups', 'ctx'), 'exp'), may hold values from -6 to 6
- hidden_in: bfloat16 [2048, 1024], P(('groups', 'ctx')), may hold values from -40 to 40
- out_proj: bfloat16 [2048, 1024], P('exp'), may hold values from -0.125 to 0.125
- norm_gain: float32 [1024], replicated, may hold values from 0.1 to 1.9
- expert_ids: int32 [2048, 8], P(('groups', 'ctx')), may hold values from 0 to 15, all different within a row; in each aligned block of 128 rows (0 to 127, 128 to 255, ...) at most 96 rows name the same one
- gate_scores: float32 [2048, 8], P(('groups', 'ctx')), may hold values from 0.05 to 1
- w_gate: bfloat16 [16, 1024, 384], P('ctx'), may hold values from -0.1875 to 0.1875
- w_up: bfloat16 [16, 1024, 384], P('ctx'), may hold values from -0.1875 to 0.1875
- w_down: bfloat16 [16, 384, 1024], P('ctx'), may hold values from -0.3125 to 0.3125
Outputs:
- layer_out: bfloat16 [2048, 1024], P(('groups', 'ctx'), 'exp')
Inputs may be any that keep to these rules, and one draw needn't show every extreme that they name: `expert_ids`: each row names 8 different experts. No expert is named by more than 96 rows of one aligned block of 128 rows, a bound that some block reaches.
All inputs are finite; a program needn't handle non-finite values.
Results may differ from a plain program's by a relative error of at most 0.0035.
Values may be sent and summed in bfloat16 or wider, within the bound.
No kernel may reach another device: no remote copies, remote signals or barrier semaphores. Data moves between devices by JAX's collectives and lax.ppermute only.
A program may use at most 64 MiB of HBM per device.

v0:
```python
import math

import jax
import jax.numpy as jnp
from jax import lax
from jax.sharding import PartitionSpec as P


def attend(queries, key_rows, value_rows, first):
    token_count = queries.shape[0]
    kv_heads = key_rows.shape[1] // 128
    q_heads = queries.shape[1] // 128
    group = q_heads // kv_heads
    grouped = queries.reshape(token_count, kv_heads, group, 128)
    query_pos = first + jnp.arange(token_count, dtype=jnp.int32)
    last_pos = first + token_count - 1
    scale = 128 ** (-0.5)
    shape_rows = (kv_heads, group, token_count)
    start_state = (
        jnp.full(shape_rows, -1e30, jnp.float32),
        jnp.zeros(shape_rows, jnp.float32),
        jnp.zeros(shape_rows + (128,), jnp.float32),
    )
    key_piece = lax.all_gather(key_rows, "ctx", axis=0, tiled=True)
    value_piece = lax.all_gather(value_rows, "ctx", axis=0, tiled=True)
    count = key_piece.shape[0]
    width = math.gcd(count, 512)

    def step(block_index, state):
        offset = block_index * width

        def compute(inner):
            running_max, running_sum, accum = inner
            key_block = lax.dynamic_slice_in_dim(key_piece, block_index * width, width, 0).reshape(
                width, kv_heads, 128
            )
            value_block = lax.dynamic_slice_in_dim(
                value_piece, block_index * width, width, 0
            ).reshape(width, kv_heads, 128)
            scores = (
                jnp.einsum("tkgd,skd->kgts", grouped, key_block, preferred_element_type=jnp.float32)
                * scale
            )
            key_pos = offset + jnp.arange(width, dtype=jnp.int32)
            allowed = key_pos[None, :] <= query_pos[:, None]
            scores = jnp.where(allowed, scores, -jnp.inf)
            new_max = jnp.maximum(running_max, jnp.max(scores, axis=-1))
            factor = jnp.exp(running_max - new_max)
            weights = jnp.exp(scores - new_max[..., None])
            new_sum = running_sum * factor + jnp.sum(weights, axis=-1)
            product = jnp.einsum(
                "kgts,skd->kgtd",
                weights.astype(jnp.bfloat16),
                value_block,
                preferred_element_type=jnp.float32,
            )
            return (new_max, new_sum, accum * factor[..., None] + product)

        return lax.cond(offset <= last_pos, compute, lambda inner: inner, state)

    _, total, accum = lax.fori_loop(0, count // width, step, start_state)
    output = accum / total[..., None]
    return (
        jnp.transpose(output, (2, 0, 1, 3)).reshape(token_count, q_heads * 128).astype(jnp.bfloat16)
    )


def place_rows(expert_ids, sent_rows, capacity, expert_count):
    top_count = expert_ids.shape[1]
    flat_ids = expert_ids.reshape(-1)
    onehot = (flat_ids[:, None] == jnp.arange(expert_count, dtype=jnp.int32)[None, :]).astype(
        jnp.int32
    )
    earlier = jnp.cumsum(onehot, axis=0) - onehot
    slot_index = jnp.sum(earlier * onehot, axis=1)
    destination = flat_ids * capacity + slot_index
    copies = jnp.repeat(sent_rows, top_count, axis=0)
    buffer = (
        jnp.zeros((expert_count * capacity, sent_rows.shape[1]), sent_rows.dtype)
        .at[destination]
        .set(copies)
    )
    return (buffer.reshape(expert_count, 2, capacity // 2, sent_rows.shape[1]), destination)


def per_device(
    queries,
    key_rows,
    value_rows,
    hidden_in,
    out_proj,
    norm_gain,
    expert_ids,
    gate_scores,
    w_gate,
    w_up,
    w_down,
):
    token_count = queries.shape[0]
    model_width = hidden_in.shape[1]
    half_width = model_width // 2
    ctx_size = lax.axis_size("ctx")
    local_experts = w_gate.shape[0]
    expert_count = local_experts * ctx_size
    top_count = expert_ids.shape[1]
    capacity = 2 * (
        min(token_count, max(2, 3 * token_count * top_count // (2 * expert_count))) // 2
    )
    half_cap = capacity // 2
    first = lax.axis_index("ctx") * token_count
    core = lax.axis_index("exp")
    side_start = core * half_width
    attended = attend(queries, key_rows, value_rows, first)
    head_part = jnp.dot(attended, out_proj, preferred_element_type=jnp.float32)
    attn_full = lax.psum(head_part.astype(jnp.bfloat16), "exp").astype(jnp.float32)
    resid = hidden_in.astype(jnp.float32) + attn_full
    inverse = lax.rsqrt(jnp.mean(resid * resid, axis=1, keepdims=True) + 1e-06)
    sent_rows = (resid * inverse * norm_gain[None, :]).astype(jnp.bfloat16)
    resid_half = lax.dynamic_slice_in_dim(resid, side_start, half_width, 1)
    buffer, destination = place_rows(expert_ids, sent_rows, capacity, expert_count)
    own_slots = lax.dynamic_slice_in_dim(buffer, core, 1, 1)
    grouped = lax.all_to_all(own_slots, "ctx", split_axis=0, concat_axis=0, tiled=True)
    gate = jnp.einsum("sxmd,xdf->sxmf", grouped, w_gate, preferred_element_type=jnp.float32)
    upper = jnp.einsum("sxmd,xdf->sxmf", grouped, w_up, preferred_element_type=jnp.float32)
    hidden = (jax.nn.silu(gate) * upper).astype(jnp.bfloat16)
    partial_value = jnp.einsum(
        "sxmf,xfd->sxmd", hidden, w_down, preferred_element_type=jnp.float32
    ).astype(jnp.bfloat16)
    returned = lax.all_to_all(partial_value, "ctx", split_axis=0, concat_axis=0, tiled=True)
    flat_back = returned.reshape(expert_count * half_cap, model_width)
    slot_of = destination % capacity
    expert_of = destination // capacity
    owned = slot_of // half_cap == core
    local_index = jnp.where(owned, expert_of * half_cap + slot_of - core * half_cap, 0)
    picked = flat_back[local_index].astype(jnp.float32)
    mixing = (gate_scores / jnp.sum(gate_scores, axis=1, keepdims=True)).reshape(-1)
    mixing = jnp.where(owned, mixing, 0.0)
    weighted = (picked * mixing[:, None]).reshape(token_count, top_count, model_width)
    mixed_part = jnp.sum(weighted, axis=1)
    moe_half = lax.psum_scatter(
        mixed_part.astype(jnp.bfloat16), "exp", scatter_dimension=1, tiled=True
    ).astype(jnp.float32)
    return (resid_half + moe_half).astype(jnp.bfloat16)


def solution(mesh):
    placed = (
        P(("groups", "ctx"), "exp"),
        P(("groups", "ctx"), "exp"),
        P(("groups", "ctx"), "exp"),
        P(("groups", "ctx"), None),
        P("exp", None),
        P(),
        P(("groups", "ctx"), None),
        P(("groups", "ctx"), None),
        P("ctx", None, None),
        P("ctx", None, None),
        P("ctx", None, None),
    )
    return jax.shard_map(
        per_device,
        mesh=mesh,
        in_specs=placed,
        out_specs=P(("groups", "ctx"), "exp"),
        check_vma=False,
    )
```

profile of v0, /device:TPU:0, one launch (start us, length us, event | category | flops | bytes accessed | tf_op | source)
XLA Modules:
  0.0 254.2 jit_solution(11516045207703964452)
XLA Ops:
  6.5 45.7 %all_gather.6 = bf16[2048,128]{1,0:T(8,128)(2,1)S(1)} all-gather(bf16[128,128]{1,0:T(8,128)(2,1)} %param.16), channel_id=1, replica_groups=mesh['groups'=1,'ctx'=16,'exp'=2] {'ctx'}, dimensions={0}, use_global_device_ids=true | all-gather | bytes 557056 | tf_op jit(solution)/shard_map/all_gather | solution.py:24
  52.2 40.9 %all_gather.7 = bf16[2048,128]{1,0:T(8,128)(2,1)} all-gather(bf16[128,128]{1,0:T(8,128)(2,1)} %param.17), channel_id=1, replica_groups=mesh['groups'=1,'ctx'=16,'exp'=2] {'ctx'}, dimensions={0}, use_global_device_ids=true | all-gather | bytes 557056 | tf_op jit(solution)/shard_map/all_gather | solution.py:25
  93.1 1.1 copy.47
  94.2 0.2 copy.48
  94.5 2.8 %while.18 = (s32[]{:T(128)}, f32[1,8,128]{2,1,0:T(8,128)S(1)}, f32[1,8,128]{2,1,0:T(8,128)S(1)}, f32[1,8,128,128]{3,2,1,0:T(8,128)S(1)}, s32[]{:T(128)}, /*index...) while((s32[]{:T(128)}, f32[1,8,128]{2,1,0:T(8,128)S(1)}, ...), condition=%wide.region_5.6_spmd.clone, body=%wide.region_0.5_spmd.clone.sunk | while | flops 272436864 | bytes 8067405 | solution.py:61
  94.5 2.6 %conditional.3 = ((f32[1,8,128]{2,1,0:T(8,128)S(1)}, f32[1,8,128]{2,1,0:T(8,128)S(1)}, f32[1,8,128,128]{3,2,1,0:T(8,128)S(1)})) conditional(s32[]{:T(128)} %convert_element_type.120, (f32[1,8,128]{2,1,0:T(8,128)S(1)}, f32[1,8,128]{2,1,0:T(8,128)S(1)}, f32[1,8,128,128]{3,2,1,0:T(8,128)S(1)}) %tuple.49, (s32[]{:T(128)}, s32[]{:T(128)}, s32[]{:T(128)}, ...), branch_computations={%region_1.0_spmd, %region_2.4_spmd} | conditional | flops 272436864 | bytes 8066654 | solution.py:59
  94.6 0.1 broadcast_compare_fusion
  94.7 0.4 fusion.55
  95.2 1.6 fusion.4
  96.8 0.3 fusion.3
  97.3 0.2 copy.49
  97.5 0.0 copy-start.3
  97.5 0.1 divide_convert_fusion
  97.6 0.0 copy-start.2
  97.6 0.0 copy-start.5
  97.6 1.2 convolution_convert_fusion.1
  98.8 0.0 all-reduce.2.cloned.1.call-update
  98.8 0.1 copy.51
  98.9 0.1 eq.51
  99.0 0.1 eq.47
  99.1 4.5 %reduce-window.6 = s32[16,8,128]{2,1,0:T(8,128)S(1)} reduce-window(s32[16,8,128]{2,1,0:T(8,128)S(1)} %fusion.51, s32[]{:T(128)} %constant.82.clone.1), window={size=1x1x128 pad=0_0x0_0x127_0}, to_apply=%region_7.8 | reduce-window | flops 2080768 | bytes 131076 | tf_op jit(solution)/shard_map/reduce-window
  103.7 0.1 slice.10
  103.7 0.1 copy.53
  103.9 0.1 copy.54
  104.0 0.1 broadcast_add_fusion.1
  104.1 0.1 copy.50
  104.2 0.1 mul.120
  104.3 0.1 compare_select_fusion
  104.4 18.4 %all-reduce.2.cloned.1.call-done = bf16[128,1024]{1,0:T(8,128)(2,1)} async-done(((bf16[128,1024]{1,0:T(8,128)(2,1)}), bf16[128,1024]{1,0:T(8,128)(2,1)}) %all-reduce.2.cloned.1.call-update) | async-done | bytes 262160 | tf_op jit(solution)/shard_map/psum | solution.py:115
  122.8 1.1 convert_add_fusion
  123.9 1.1 multiply_convert_fusion
  125.0 7.4 %scatter_custom_fusion = bf16[1536,1024]{1,0:T(8,128)(2,1)} fusion(s32[1024]{0:T(1024)S(1)} %bitcast.140, bf16[]{:T(256)} %constant.91.clone.1, bf16[128,1024]{1,0:T(8,128)(2,1)S(1)} %multiply_convert_fusion), kind=kCustom, calls=%fused_computation.27 | custom fusion | bytes 3407874 | tf_op jit(solution)/shard_map/scatter | solution.py:81
  132.4 1.6 constant_dynamic-slice_fusion
  133.9 0.0 copy-start.6
  133.9 44.7 %all_to_all.10 = bf16[16,1,48,1024]{3,2,1,0:T(8,128)(2,1)S(1)} all-to-all(bf16[16,1,48,1024]{3,2,1,0:T(8,128)(2,1)S(1)} %constant_dynamic-slice_fusion), channel_id=1, replica_groups=mesh['groups'=1,'ctx'=16,'exp'=2] {'ctx'}, dimensions={0} | all-to-all | bytes 3145728 | tf_op jit(solution)/shard_map/all_to_all | solution.py:122
  178.7 1.1 copy-done.1
  179.8 2.0 fusion.25
  181.8 5.2 %fusion.24 = bf16[16,1,48,1024]{3,2,1,0:T(8,128)(2,1)} fusion(bf16[16,1,48,1024]{3,2,1,0:T(8,128)(2,1)} %copy-done.1, f32[16,1,48,384]{3,2,0,1:T(8,128)} %fusion.25, bf16[1,384,1024]{2,1,0:T(8,128)(2,1)} %param.25, bf16[1,1024,384]{2,1,0:T(8,128)(2,1)} %param.24), kind=kOutput, calls=%fused_computation.35 | convolution fusion | flops 1210515456 | bytes 5898240 | tf_op jit(solution)/shard_map/sxmf,xfd->sxmd/dot_general | solution.py:126
  187.0 4.5 %all-to-all-start.1 = ((bf16[16,1,48,1024]{3,2,1,0:T(8,128)(2,1)}), bf16[16,1,48,1024]{3,2,1,0:T(8,128)(2,1)}, u32[]{:S(2)}, u32[]{:S(2)}) async-start(bf16[16,1,48,1024]{3,2,1,0:T(8,128)(2,1)} %fusion.24), calls=%async_computation.1 | async-start | bytes 3145728 | tf_op jit(solution)/shard_map/all_to_all | solution.py:129
  191.5 0.2 reduce-scatter.2.cloned.1.call-start
  191.8 0.1 reduce_sum.54
  192.0 0.1 copy.57
  192.1 32.7 %all-to-all-done.1 = bf16[16,1,48,1024]{3,2,1,0:T(8,128)(2,1)} async-done(((bf16[16,1,48,1024]{3,2,1,0:T(8,128)(2,1)}), bf16[16,1,48,1024]{3,2,1,0:T(8,128)(2,1)}, u32[]{:S(2)}, u32[]{:S(2)}) %all-to-all-start.1) | async-done | bytes 1572896 | tf_op jit(solution)/shard_map/all_to_all | solution.py:129
  224.8 7.6 %gather_fusion = bf16[1024,1024]{1,0:T(8,128)(2,1)} fusion(bf16[768,1024]{1,0:T(8,128)(2,1)} %bitcast.41, s32[1024]{0:T(1024)S(1)} %broadcast_clamp_fusion), kind=kCustom, calls=%fused_computation | custom fusion | bytes 4198400 | tf_op jit(solution)/shard_map/gather | solution.py:135
  232.4 3.7 %fusion.16 = bf16[128,1024]{1,0:T(8,128)(2,1)} fusion(bf16[1024,1024]{1,0:T(8,128)(2,1)} %gather_fusion, f32[128,8]{1,0:T(8,128)S(1)} %copy.57), kind=kLoop, calls=%fused_computation.26 | loop fusion | flops 3014656 | bytes 2363392 | tf_op jit(solution)/shard_map/reduce_sum | solution.py:139
  236.1 0.0 reduce-scatter.2.cloned.1.call-update
  236.1 9.7 %reduce-scatter.2.cloned.1.call-done = bf16[128,512]{1,0:T(8,128)(2,1)} async-done(((bf16[128,1024]{1,0:T(8,128)(2,1)}), bf16[128,512]{1,0:T(8,128)(2,1)}) %reduce-scatter.2.cloned.1.call-update) | async-done | bytes 131088 | tf_op jit(solution)/shard_map/reduce_scatter | solution.py:140
  245.8 1.6 add_convert_fusion
  (35 shorter events, 0.3 us)
Async XLA Ops:
  6.5 91.1 %copy-start = (bf16[1024,1024]{1,0:T(8,128)(2,1)S(1)}, bf16[1024,1024]{1,0:T(8,128)(2,1)}, u32[]{:S(2)}) copy-start(bf16[1024,1024]{1,0:T(8,128)(2,1)} %param.19) | copy-start | bytes 6291460
  6.5 116.2 %all-reduce.2.cloned.1.call-start = ((), (), s32[]{:S(2)}) async-start(), calls=%async_computation.3 | async-start | bytes 524288 | tf_op jit(solution)/shard_map/psum | solution.py:115
  97.5 1.3 copy-start.3
  97.6 25.2 %copy-start.2 = (bf16[128,1024]{1,0:T(8,128)(2,1)S(1)}, bf16[128,1024]{1,0:T(8,128)(2,1)}, u32[]{:S(2)}) copy-start(bf16[128,1024]{1,0:T(8,128)(2,1)} %param.18) | copy-start | bytes 786436
  97.6 26.3 %copy-start.5 = (f32[1024]{0:T(1024)S(1)}, f32[1024]{0:T(1024)}, u32[]{:S(2)}) copy-start(f32[1024]{0:T(1024)} %param.20) | copy-start | bytes 12292
  133.9 45.9 %copy-start.6 = (bf16[1,1024,384]{2,1,0:T(8,128)(2,1)S(1)}, bf16[1,1024,384]{2,1,0:T(8,128)(2,1)}, u32[]{:S(2)}) copy-start(bf16[1,1024,384]{2,1,0:T(8,128)(2,1)} %param.23) | copy-start | bytes 2359300
  178.7 1.1 copy-start.1
  187.0 4.9 %copy-start.4 = (f32[128,8]{0,1:T(8,128)S(1)}, f32[128,8]{0,1:T(8,128)}, u32[]{:S(2)}) copy-start(f32[128,8]{0,1:T(8,128)} %param.22) | copy-start | bytes 12292
  187.0 37.8 %all-to-all-start.1 = ((bf16[16,1,48,1024]{3,2,1,0:T(8,128)(2,1)}), bf16[16,1,48,1024]{3,2,1,0:T(8,128)(2,1)}, u32[]{:S(2)}, u32[]{:S(2)}) async-start(bf16[16,1,48,1024]{3,2,1,0:T(8,128)(2,1)} %fusion.24), calls=%async_computation.1 | async-start | bytes 3145728 | tf_op jit(solution)/shard_map/all_to_all | solution.py:129
  191.5 54.3 %reduce-scatter.2.cloned.1.call-start = ((), (), s32[]{:S(2)}) async-start(), calls=%async_computation.4 | async-start | bytes 393216 | tf_op jit(solution)/shard_map/reduce_scatter | solution.py:140
Sparse Core Ops, SparseCore 0:
  98.9 23.7 all-reduce.1
  236.3 9.4 reduce-scatter.1
where the time goes:
time: 255 us; the launch traced here: 254 us
  blocking collectives  131 us (51%)
  waiting for transfers between devices  60.8 us (24%)
  local copies, waits for them, and re-layouts  20.3 us (8%)
  between operations  13.6 us (5%)
  other arithmetic  12.8 us (5%)
  matrix products  10.4 us (4%)
  starting transfers between devices  4.76 us (2%)
    all_gather x1, blocking collectives, attend(): key_piece = lax.all_gather(key_rows, 'ctx', axis=0, tiled=True)  45.7 us
    all_to_all x1, blocking collectives, per_device(): lax.all_to_all(own_slots, 'ctx', split_axis=0, concat_axis=0, tiled=True)  44.7 us
    all_gather x1, blocking collectives, attend(): value_piece = lax.all_gather(value_rows, 'ctx', axis=0, tiled=True)  40.9 us
    all_to_all x1, waiting for transfers between devices, per_device(): lax.all_to_all(partial_value, 'ctx', split_axis=0, concat_axis=0, tiled=T...  32.7 us
    psum x1, waiting for transfers between devices, per_device(): lax.psum(head_part.astype(jnp.bfloat16), 'exp').astype(jnp.float32)  18.4 us
    reduce_scatter x1, waiting for transfers between devices, per_device(): lax.psum_scatter(mixed_part.astype(jnp.bfloat16), 'exp', scatter_dimensio...  9.66 us
    gather x1, local copies, waits for them, and re-layouts, per_device(): picked = flat_back[local_index].astype(jnp.float32)  7.65 us
    scatter x1, local copies, waits for them, and re-layouts, place_rows(): buffer = jnp.zeros((expert_count * capacity, sent_rows.shape[1]), sent_ro...  7.39 us
  transfers between devices with their start and end apart: 3, of which 3 were waited for; matrix products, arithmetic and copies ran while one was open for 2% of the time, Pallas kernels for 0%

commit v1 on v0

--- a/solution.py
+++ b/solution.py
@@ -1,9 +1,491 @@
+import functools
 import math
 
 import jax
 import jax.numpy as jnp
 from jax import lax
+from jax.experimental import pallas as pl
+from jax.experimental.pallas import tpu as pltpu
 from jax.sharding import PartitionSpec as P
+
+
+HEAD = 128
+LOG2E = 1.4426950408889634
+HIDE = -1e30
+ROOM = 20 << 20
+
+
+def whole(memory_space=pltpu.VMEM):
+    return pl.BlockSpec(memory_space=memory_space)
+
+
+def cost(flops, size, exps=0):
+    return pl.CostEstimate(flops=int(flops), bytes_accessed=int(size), transcendentals=int(exps))
+
+
+def pack_kernel(key_ref, value_ref, ids_ref, score_ref, rows_ref, mixed_ref):
+    count = key_ref.shape[0]
+    experts = mixed_ref.shape[0] - count
+    both = jnp.concatenate([key_ref[...], value_ref[...]], axis=1)
+    rows_ref[...] = both
+    mixed_ref[:count, :] = both
+    scores = score_ref[...]
+    mix = scores / jnp.sum(scores, axis=0, keepdims=True)
+    ids = ids_ref[...]
+    number = lax.broadcasted_iota(jnp.int32, (experts, count), 0)
+    turned = jnp.zeros((experts, count), jnp.float32)
+    for k in range(ids.shape[0]):
+        turned = turned + jnp.where(number == ids[k : k + 1, :], mix[k : k + 1, :], 0.0)
+    high = turned.astype(jnp.bfloat16)
+    low = (turned - high.astype(jnp.float32)).astype(jnp.bfloat16)
+    mixed_ref[count:, :] = jnp.concatenate([high, low], axis=1)
+
+
+def pack(key_rows, value_rows, expert_ids, gate_scores, experts):
+    count, width = key_rows.shape
+    return pl.pallas_call(
+        pack_kernel,
+        out_shape=(
+            jax.ShapeDtypeStruct((count, 2 * width), jnp.bfloat16),
+            jax.ShapeDtypeStruct((count + experts, 2 * width), jnp.bfloat16),
+        ),
+        in_specs=[whole()] * 4,
+        out_specs=(whole(), whole()),
+        cost_estimate=cost(1e5, 3e5),
+        compiler_params=pltpu.CompilerParams(vmem_limit_bytes=ROOM),
+        name="pack",
+    )(key_rows, value_rows, expert_ids.T, gate_scores.T)
+
+
+def join_kernel(count, *refs):
+    out_ref = refs[-1]
+    tail = None
+    for n, ref in enumerate(refs[:-1]):
+        out_ref[n * count : (n + 1) * count, :] = ref[:count, :]
+        if ref.shape[0] > count:
+            tail = ref
+    out_ref[(len(refs) - 1) * count :, :] = tail[count:, :]
+
+
+def join(parts, count):
+    total = sum(part.shape[0] for part in parts)
+    return pl.pallas_call(
+        functools.partial(join_kernel, count),
+        out_shape=jax.ShapeDtypeStruct((total, parts[0].shape[1]), parts[0].dtype),
+        in_specs=[whole()] * len(parts),
+        out_specs=whole(),
+        cost_estimate=cost(1e5, 4e5),
+        compiler_params=pltpu.CompilerParams(vmem_limit_bytes=ROOM),
+        name="join",
+    )(*parts)
+
+
+def soften(query, key_ref, value_ref, biases, state):
+    scale = HEAD ** (-0.5) * LOG2E
+    scores = lax.dot_general(
+        query, key_ref[...], (((1,), (1,)), ((), ())), preferred_element_type=jnp.float32
+    )
+    pieces = [
+        scores[:, n * HEAD : (n + 1) * HEAD] + bias for n, bias in enumerate(biases)
+    ]
+    peak = functools.reduce(jnp.maximum, pieces)
+    peak = jnp.max(peak, axis=1, keepdims=True)
+    if state is not None:
+        peak = jnp.maximum(peak, state[0][:, :1])
+    shift = peak * scale
+    weights = [jnp.exp2(piece * scale - shift) for piece in pieces]
+    total = functools.reduce(jnp.add, weights)
+    product = jnp.dot(
+        jnp.concatenate([w.astype(jnp.bfloat16) for w in weights], axis=1),
+        value_ref[...],
+        preferred_element_type=jnp.float32,
+    )
+    if state is not None:
+        factor = jnp.exp2(state[0][:, :1] * scale - shift)
+        total = total + state[1] * factor
+        product = product + state[2] * factor
+    return peak, total, product
+
+
+def near_kernel(plane, place_ref, query_ref, *refs):
+    count = query_ref.shape[0]
+    steps = len(refs) - 5
+    sources = refs[:steps]
+    peak_ref, total_ref, sum_ref, keys, values = refs[steps:]
+    for n, ref in enumerate(sources):
+        keys[n * count : (n + 1) * count, :] = ref[:count, :HEAD]
+        values[n * count : (n + 1) * count, :] = ref[:count, HEAD:]
+    me = place_ref[0]
+    row = lax.broadcasted_iota(jnp.int32, (count, count), 0)
+    column = lax.broadcasted_iota(jnp.int32, (count, count), 1)
+    biases = [jnp.where(column <= row, 0.0, HIDE)]
+    for step in range(1, plane):
+        biases.append(jnp.where((me ^ step) < me, 0.0, HIDE))
+    for step in range(1, steps - plane + 1):
+        biases.append(jnp.where(me >= step * plane, 0.0, HIDE))
+    for head in range(query_ref.shape[1] // HEAD):
+        part = slice(head * HEAD, (head + 1) * HEAD)
+        peak, total, product = soften(query_ref[:, part], keys, values, biases, None)
+        peak_ref[:, part] = jnp.broadcast_to(peak, (count, HEAD))
+        total_ref[:, part] = total
+        sum_ref[:, part] = product
+
+
+def near(place, queries, sources, plane):
+    count, width = queries.shape
+    shape = jax.ShapeDtypeStruct((count, width), jnp.float32)
+    keys = len(sources) * count
+    return pl.pallas_call(
+        functools.partial(near_kernel, plane),
+        out_shape=(shape,) * 3,
+        in_specs=[whole(pltpu.SMEM)] + [whole()] * (1 + len(sources)),
+        out_specs=(whole(),) * 3,
+        scratch_shapes=[pltpu.VMEM((keys, HEAD), jnp.bfloat16)] * 2,
+        cost_estimate=cost(4 * width * count * keys, 4e6, width * keys),
+        compiler_params=pltpu.CompilerParams(vmem_limit_bytes=ROOM),
+        name="near",
+    )(place, queries, *sources)
+
+
+def far_kernel(plane, place_ref, query_ref, peak_ref, total_ref, sum_ref, *refs):
+    steps = plane - 1
+    sources = refs[:steps]
+    weight_ref, own_ref, other_ref, keys, values, attended, weight, result, sem = refs[steps:]
+    fetch = pltpu.make_async_copy(weight_ref, weight, sem)
+    fetch.start()
+    count = query_ref.shape[0]
+    layers = sources[0].shape[0] // count
+    span = layers * count
+    for n, ref in enumerate(sources):
+        keys[n * span : (n + 1) * span, :] = ref[:span, :HEAD]
+        values[n * span : (n + 1) * span, :] = ref[:span, HEAD:]
+    me, core = place_ref[0], place_ref[1]
+    biases = [jnp.where(me >= step * plane, 0.0, HIDE) for step in range(1, layers + 1)] * steps
+    for head in range(query_ref.shape[1] // HEAD):
+        part = slice(head * HEAD, (head + 1) * HEAD)
+        state = (peak_ref[:, part], total_ref[:, part], sum_ref[:, part])
+        _, total, product = soften(query_ref[:, part], keys, values, biases, state)
+        denom = jnp.sum(total, axis=1, keepdims=True)
+        attended[:, part] = (product / denom).astype(jnp.bfloat16)
+    fetch.wait()
+    result[...] = jnp.dot(attended[...], weight[...], preferred_element_type=jnp.float32)
+    half = count // 2
+    own_ref[...] = result[pl.ds(pl.multiple_of(core * half, half), half), :]
+    other = result[pl.ds(pl.multiple_of((1 - core) * half, half), half), :]
+    other_ref[...] = other.astype(jnp.bfloat16)
+
+
+def far(place, queries, state, sources, out_proj, plane):
+    count, width = queries.shape
+    model = out_proj.shape[1]
+    keys = len(sources) * (sources[0].shape[0] // count) * count
+    return pl.pallas_call(
+        functools.partial(far_kernel, plane),
+        out_shape=(
+            jax.ShapeDtypeStruct((count // 2, model), jnp.float32),
+            jax.ShapeDtypeStruct((count // 2, model), jnp.bfloat16),
+        ),
+        in_specs=[whole(pltpu.SMEM)] + [whole()] * (4 + len(sources)) + [whole(pl.ANY)],
+        out_specs=(whole(),) * 2,
+        scratch_shapes=[
+            pltpu.VMEM((keys, HEAD), jnp.bfloat16),
+            pltpu.VMEM((keys, HEAD), jnp.bfloat16),
+            pltpu.VMEM((count, width), jnp.bfloat16),
+            pltpu.VMEM(out_proj.shape, jnp.bfloat16),
+            pltpu.VMEM((count, model), jnp.float32),
+            pltpu.SemaphoreType.DMA,
+        ],
+        cost_estimate=cost(
+            4 * width * count * keys + 2 * count * width * model, 6e6, width * keys
+        ),
+        compiler_params=pltpu.CompilerParams(vmem_limit_bytes=ROOM),
+        name="far",
+    )(place, queries, *state, *sources, out_proj)
+
+
+def norm_kernel(place_ref, hidden_ref, own_ref, other_ref, gain_ref, resid_ref, normed_ref):
+    half = own_ref.shape[0]
+    start = pl.multiple_of(place_ref[1] * half, half)
+    hidden = hidden_ref[pl.ds(start, half), :].astype(jnp.float32)
+    resid = hidden + own_ref[...] + other_ref[...].astype(jnp.float32)
+    inverse = lax.rsqrt(jnp.mean(resid * resid, axis=1, keepdims=True) + 1e-06)
+    resid_ref[...] = resid
+    normed_ref[...] = (resid * inverse * gain_ref[...]).astype(jnp.bfloat16)
+
+
+def norm(place, hidden_in, own, other, norm_gain):
+    return pl.pallas_call(
+        norm_kernel,
+        out_shape=(
+            jax.ShapeDtypeStruct(own.shape, jnp.float32),
+            jax.ShapeDtypeStruct(own.shape, jnp.bfloat16),
+        ),
+        in_specs=[whole(pltpu.SMEM)] + [whole()] * 4,
+        out_specs=(whole(),) * 2,
+        cost_estimate=cost(1e6, 1e6),
+        compiler_params=pltpu.CompilerParams(vmem_limit_bytes=ROOM),
+        name="norm",
+    )(place, hidden_in, own, other, norm_gain)
+
+
+def share_kernel(place_ref, *refs):
+    pieces, out_ref, turned = refs[:-2], refs[-2], refs[-1]
+    experts, count = pieces[0].shape[0], pieces[0].shape[1] // 2
+    half = count // 2
+    start = pl.multiple_of(place_ref[1] * half, half)
+    number = lax.broadcasted_iota(jnp.int32, (experts, count), 0)
+    lane = lax.broadcasted_iota(jnp.int32, (count, count), 1)
+    diagonal = lax.broadcasted_iota(jnp.int32, (count, count), 0) == lane
+    for n, piece in enumerate(pieces):
+        mix = piece[:, :count].astype(jnp.float32) + piece[:, count:].astype(jnp.float32)
+        columns = jnp.zeros((count, count), jnp.float32)
+        for side in range(2):
+            line = jnp.sum(
+                jnp.where(number == place_ref[2 + side], mix, 0.0), axis=0, keepdims=True
+            )
+            column = jnp.sum(jnp.where(diagonal, line, 0.0), axis=1, keepdims=True)
+            columns = jnp.where(lane == side, column, columns)
+        turned[...] = columns
+        out_ref[n * half : (n + 1) * half, :] = turned[pl.ds(start, half), :]
+
+
+def share(place, pieces, experts):
+    width = pieces[0].shape[1]
+    count = width // 2
+    specs = []
+    for piece in pieces:
+        block = piece.shape[0] // experts - 1
+        specs.append(pl.BlockSpec((experts, width), lambda i, block=block: (block, 0)))
+    rows = len(pieces) * count // 2
+    return pl.pallas_call(
+        share_kernel,
+        grid=(1,),
+        out_shape=jax.ShapeDtypeStruct((rows, count), jnp.float32),
+        in_specs=[whole(pltpu.SMEM)] + specs,
+        out_specs=pl.BlockSpec((rows, count), lambda i: (0, 0)),
+        scratch_shapes=[pltpu.VMEM((count, count), jnp.float32)],
+        cost_estimate=cost(1e6, 4e5),
+        compiler_params=pltpu.CompilerParams(vmem_limit_bytes=ROOM),
+        name="share",
+    )(place, *pieces)
+
+
+def expert_kernel(first, blocks, place_ref, share_ref, *refs):
+    inputs, refs = refs[:blocks], refs[blocks:]
+    sources = refs[:9]
+    outputs, rows, mats, sems = refs[-8 - blocks : -8], refs[-8], refs[-7:-1], refs[-1]
+    core = place_ref[1]
+    copies = [pltpu.make_async_copy(sources[n].at[0], mats[n], sems.at[n]) for n in range(3)]
+    for n in range(3):
+        half = mats[3 + n].shape[0] // 2
+        for side in range(2):
+            place = core if side == 0 else 1 - core
+            target = mats[3 + n].at[pl.ds(pl.multiple_of(place * half, half), half)]
+            order = 3 + 2 * n + side
+            copies.append(pltpu.make_async_copy(sources[order], target, sems.at[order]))
+    for copy in copies:
+        copy.start()
+    size = inputs[0].shape[0]
+    for n, ref in enumerate(inputs):
+        rows[n * size : (n + 1) * size, :] = ref[...]
+    total = None
+    for side in range(2):
+        gate_ref, up_ref, down_ref = mats[3 * side : 3 * side + 3]
+        waits = [copies[:1], copies[1:2], copies[2:3]] if side == 0 else [
+            copies[3:5], copies[5:7], copies[7:9]]
+        for copy in waits[0]:
+            copy.wait()
+        gate = jnp.dot(rows[...], gate_ref[...], preferred_element_type=jnp.float32)
+        for copy in waits[1]:
+            copy.wait()
+        upper = jnp.dot(rows[...], up_ref[...], preferred_element_type=jnp.float32)
+        hidden = (gate / (1.0 + jnp.exp(-gate)) * upper).astype(jnp.bfloat16)
+        for copy in waits[2]:
+            copy.wait()
+        part = jnp.dot(hidden, down_ref[...], preferred_element_type=jnp.float32)
+        part = part.astype(jnp.bfloat16).astype(jnp.float32)
+        factor = share_ref[first * size : (first + blocks) * size, side : side + 1]
+        total = part * factor if total is None else total + part * factor
+    for n, ref in enumerate(outputs):
+        ref[...] = total[n * size : (n + 1) * size, :].astype(ref.dtype)
+
+
+def experts_on(place, shares, inputs, weights, first, dtypes, after):
+    blocks = len(inputs)
+    size, model = inputs[0].shape
+    units = weights[0].shape[2]
+    return pl.pallas_call(
+        functools.partial(expert_kernel, first, blocks),
+        out_shape=tuple(jax.ShapeDtypeStruct((size, model), dtype) for dtype in dtypes),
+        in_specs=[whole(pltpu.SMEM)] + [whole()] * (1 + blocks) + [whole(pl.ANY)] * (9 + len(after)),
+        out_specs=tuple([whole()] * blocks),
+        scratch_shapes=[pltpu.VMEM((blocks * size, model), jnp.bfloat16)]
+        + [
+            pltpu.VMEM((model, units), jnp.bfloat16),
+            pltpu.VMEM((model, units), jnp.bfloat16),
+            pltpu.VMEM((units, model), jnp.bfloat16),
+        ]
+        * 2
+        + [pltpu.SemaphoreType.DMA((9,))],
+        cost_estimate=cost(12 * blocks * size * model * units, 12 * model * units),
+        compiler_params=pltpu.CompilerParams(vmem_limit_bytes=ROOM),
+    )(place, shares, *inputs, *weights, *after)
+
+
+def final_kernel(place_ref, resid_ref, own_ref, *refs):
+    keep_ref, send_ref, work = refs[-3:]
+    total = own_ref[...]
+    for ref in refs[:-3]:
+        total = total + ref[...].astype(jnp.float32)
+    work[...] = (resid_ref[...] + total).astype(jnp.bfloat16)
+    half = keep_ref.shape[1]
+    core = place_ref[1]
+    keep_ref[...] = work[:, pl.ds(pl.multiple_of(core * half, half), half)]
+    send_ref[...] = work[:, pl.ds(pl.multiple_of((1 - core) * half, half), half)]
+
+
+def final(place, resid, own, received):
+    rows, model = resid.shape
+    shape = jax.ShapeDtypeStruct((rows, model // 2), jnp.bfloat16)
+    return pl.pallas_call(
+        final_kernel,
+        out_shape=(shape, shape),
+        in_specs=[whole(pltpu.SMEM)] + [whole()] * (2 + len(received)),
+        out_specs=(whole(),) * 2,
+        scratch_shapes=[pltpu.VMEM((rows, model), jnp.bfloat16)],
+        cost_estimate=cost(1e6, 1e6),
+        compiler_params=pltpu.CompilerParams(vmem_limit_bytes=ROOM),
+        name="final",
+    )(place, resid, own, *received)
+
+
+def compact(
+    queries,
+    key_rows,
+    value_rows,
+    hidden_in,
+    out_proj,
+    norm_gain,
+    expert_ids,
+    gate_scores,
+    w_gate,
+    w_up,
+    w_down,
+):
+    count = queries.shape[0]
+    model = hidden_in.shape[1]
+    ctx = lax.axis_size("ctx")
+    plane = math.isqrt(ctx)
+    planes = ctx // plane
+    away = 2 * plane
+    me = lax.axis_index("ctx")
+    core = lax.axis_index("exp")
+    place = jnp.stack([me, core, me, me ^ plane]).astype(jnp.int32)
+
+    def flip(value, mask):
+        return lax.ppermute(value, "ctx", [(i, i ^ mask) for i in range(ctx)])
+
+    def upward(value, step):
+        return lax.ppermute(value, "ctx", [(i, i + step) for i in range(ctx - step)])
+
+    def across(value):
+        return lax.ppermute(value, "exp", [(0, 1), (1, 0)])
+
+    mates = range(1, plane)
+    rows, mixed = pack(key_rows, value_rows, expert_ids, gate_scores, w_gate.shape[0] * ctx)
+    column = [
+        flip(mixed, away)
+        if step == 2
+        else upward(rows, step * plane)
+        for step in range(1, planes)
+    ]
+    level = [flip(mixed, mate) for mate in mates]
+    joined = join(column, count)
+    corner = [flip(joined, mate) for mate in mates]
+
+    halves = []
+    for mat in (w_gate, w_up, w_down):
+        half = mat.shape[1] // 2
+        piece = lax.dynamic_slice_in_dim(mat[0], core * half, half, 0)
+        halves.append(flip(piece, plane))
+    weights = [w_gate, w_up, w_down]
+    for half in halves:
+        weights += [half, across(half)]
+
+    state = near(place, queries, [mixed] + level + column, plane)
+    own, other = far(place, queries, state, corner, out_proj, plane)
+    resid, normed = norm(place, hidden_in, own, across(other), norm_gain.reshape(1, model))
+
+    shares = share(place, [mixed] + level + [column[1]] + corner, w_gate.shape[0] * ctx)
+    opposite = flip(normed, away)
+    level_rows = [flip(normed, mate) for mate in mates]
+    corner_rows = [flip(opposite, mate) for mate in mates]
+    f32, bf16 = jnp.float32, jnp.bfloat16
+    near_out = experts_on(
+        place, shares, [normed] + level_rows + [opposite], weights, 0,
+        [f32] + [bf16] * len(mates) + [f32], [],
+    )
+    far_out = experts_on(
+        place, shares, corner_rows, weights, plane + 1, [bf16] * len(mates),
+        [near_out[1]],
+    )
+    passed = [flip(value, mate) for value, mate in zip(far_out, mates)]
+    direct = [flip(value, mate) for value, mate in zip(near_out[1:plane], mates)]
+    last = flip(gather_sum(near_out[plane], passed), away)
+    keep, send = final(place, resid, near_out[0], direct + [last])
+    return assemble(place, keep, across(send))
+
+
+def gather_sum_kernel(own_ref, *refs):
+    total = own_ref[...]
+    for ref in refs[:-1]:
+        total = total + ref[...].astype(jnp.float32)
+    refs[-1][...] = total.astype(jnp.bfloat16)
+
+
+def gather_sum(own, received):
+    return pl.pallas_call(
+        gather_sum_kernel,
+        out_shape=jax.ShapeDtypeStruct(own.shape, jnp.bfloat16),
+        in_specs=[whole()] * (1 + len(received)),
+        out_specs=whole(),
+        cost_estimate=cost(1e5, 8e5),
+        compiler_params=pltpu.CompilerParams(vmem_limit_bytes=ROOM),
+        name="gather_sum",
+    )(own, *received)
+
+
+def assemble_kernel(place_ref, keep_ref, received_ref, out_ref):
+    half = keep_ref.shape[0]
+    core = place_ref[1]
+    out_ref[pl.ds(pl.multiple_of(core * half, half), half), :] = keep_ref[...]
+    out_ref[pl.ds(pl.multiple_of((1 - core) * half, half), half), :] = received_ref[...]
+
+
+def assemble(place, keep, received):
+    return pl.pallas_call(
+        assemble_kernel,
+        out_shape=jax.ShapeDtypeStruct((2 * keep.shape[0], keep.shape[1]), keep.dtype),
+        in_specs=[whole(pltpu.SMEM)] + [whole()] * 2,
+        out_specs=whole(),
+        cost_estimate=cost(1e5, 3e5),
+        compiler_params=pltpu.CompilerParams(vmem_limit_bytes=ROOM),
+        name="assemble",
+    )(place, keep, received)
+
+
+def fits_compact(queries, key_rows, expert_ids, w_gate):
+    ctx = lax.axis_size("ctx")
+    plane = math.isqrt(ctx)
+    return (
+        plane * plane == ctx
+        and plane == 4
+        and lax.axis_size("exp") == 2
+        and w_gate.shape[0] == 1
+        and ctx <= 2 * expert_ids.shape[1]
+        and key_rows.shape == (HEAD, HEAD)
+        and queries.shape[0] == HEAD
+    )
 
 
 def attend(queries, key_rows, value_rows, first):
@@ -96,6 +578,11 @@
     w_up,
     w_down,
 ):
+    if fits_compact(queries, key_rows, expert_ids, w_gate):
+        return compact(
+            queries, key_rows, value_rows, hidden_in, out_proj, norm_gain,
+            expert_ids, gate_scores, w_gate, w_up, w_down,
+        )
     token_count = queries.shape[0]
     model_width = hidden_in.shape[1]
     half_width = model_width // 2

time: 255 us -> 96.5 us (0.38)
  blocking collectives: 131 us -> 0 us
  waiting for transfers between devices: 60.8 us -> 23.8 us
  starting transfers between devices: 4.76 us -> 34.8 us
  Pallas kernels: 0 us -> 24 us
  between operations: 13.6 us -> 0.24 us
  other arithmetic: 12.8 us -> 0.08 us
  matrix products: 10.4 us -> 0 us
  local copies, waits for them, and re-layouts: 20.3 us -> 12.9 us
    all_gather x2 -> x0, blocking collectives: 86.6 us -> none  [the longest x1 45.7 us: attend(): key_piece = lax.all_gather(key_rows, 'ctx', axis=0, tiled=True)]
    all_to_all x1 -> x0, blocking collectives: 44.7 us -> none  [per_device(): lax.all_to_all(own_slots, 'ctx', split_axis=0, concat_axis=0, tiled=True)]
    ppermute x0 -> x31, starting transfers between devices: none -> 34.8 us  [the longest x24 28.9 us: flip(): return lax.ppermute(value, 'ctx', [(i, i ^ mask) for i in range(ctx)])]
    all_to_all x1 -> x0, waiting for transfers between devices: 32.7 us -> none  [per_device(): lax.all_to_all(partial_value, 'ctx', split_axis=0, concat_axis=0, tiled=T...]
    pallas_call x0 -> x11, Pallas kernels: none -> 24 us  [the longest x2 8.46 us: experts_on(): pl.pallas_call(functools.partial(expert_kernel, first, blocks), out_shape...]
    ppermute x0 -> x31, waiting for transfers between devices: none -> 23.8 us  [the longest x24 22.2 us: flip(): return lax.ppermute(value, 'ctx', [(i, i ^ mask) for i in range(ctx)])]
    psum x1 -> x0, waiting for transfers between devices: 18.4 us -> none  [per_device(): lax.psum(head_part.astype(jnp.bfloat16), 'exp').astype(jnp.float32)]
    dot_general x5 -> x0, matrix products: 10.4 us -> none  [the longest x1 5.18 us: per_device(): jnp.einsum('sxmf,xfd->sxmd', hidden, w_down, preferred_element_type=jnp.f...]
  transfers between devices with their start and end apart: 3 -> 31, of which waited for: 3 -> 11; matrix products, arithmetic and copies ran while one was open for 2% -> 5% of each run, Pallas kernels for 0% -> 18%
where the time goes in v1:
time: 96.5 us; the launch traced here: 95.9 us
  starting transfers between devices  34.8 us (36%)
  Pallas kernels  24 us (25%)
  waiting for transfers between devices  23.8 us (25%)
  local copies, waits for them, and re-layouts  12.9 us (13%)
    ppermute x24, starting transfers between devices, flip(): return lax.ppermute(value, 'ctx', [(i, i ^ mask) for i in range(ctx)])  28.9 us
    ppermute x24, waiting for transfers between devices, flip(): return lax.ppermute(value, 'ctx', [(i, i ^ mask) for i in range(ctx)])  22.2 us
    pallas_call x2, Pallas kernels, experts_on(): pl.pallas_call(functools.partial(expert_kernel, first, blocks), out_shape...  8.46 us
    unnamed x36, local copies, waits for them, and re-layouts  8.38 us
    pallas_call x1, Pallas kernels, far(): pl.pallas_call(functools.partial(far_kernel, plane), out_shape=(jax.Shape...  6.49 us
    ppermute x2, starting transfers between devices, upward(): lax.ppermute(value, 'ctx', [(i, i + step) for i in range(ctx - step)])  4.76 us
    dynamic_slice x3, local copies, waits for them, and re-layouts, compact(): piece = lax.dynamic_slice_in_dim(mat[0], core * half, half, 0)  4.51 us
    pallas_call x1, Pallas kernels, near(): pl.pallas_call(functools.partial(near_kernel, plane), out_shape=(shape,)...  3.95 us
  transfers between devices with their start and end apart: 31, of which 11 were waited for; matrix products, arithmetic and copies ran while one was open for 5% of the time, Pallas kernels for 18%

profile of v1, /device:TPU:0, one launch (start us, length us, event | category | flops | bytes accessed | tf_op | source)
XLA Modules:
  0.0 95.9 jit_solution(3809249629260044848)
XLA Ops:
  0.0 0.8 copy-done.13
  0.8 0.8 copy-done.14
  1.6 0.7 copy-done.16
  2.3 0.7 copy-done.17
  3.0 0.7 pack.1
  3.6 4.1 %collective-permute-start.4 = (bf16[144,256]{1,0:T(8,128)(2,1)}, bf16[144,256]{1,0:T(8,128)(2,1)S(1)}, u32[]{:S(2)}, u32[]{:S(2)}) collective-permute-start(bf16[144,256]{1,0:T(8,128)(2,1)} %get-tuple-element.24.refs_0_), channel_id=1, source_target_pairs={{0,16},{2,18},{4,20},{6,22},{8,24},{10,26},{12,28},{14,30},{16,0},... | collective-permute-start | bytes 221192 | tf_op jit(solution)/shard_map/ppermute | solution.py:386
  7.7 1.5 %collective-permute-start = (bf16[144,256]{1,0:T(8,128)(2,1)}, bf16[144,256]{1,0:T(8,128)(2,1)}, u32[]{:S(2)}, u32[]{:S(2)}) collective-permute-start(bf16[144,256]{1,0:T(8,128)(2,1)} %get-tuple-element.24.refs_0_), channel_id=1, source_target_pairs={{0,2},{2,0},{4,6},{6,4},{8,10},{10,8},{12,14},{14,12},{16,18},{18,... | collective-permute-start | bytes 221192 | tf_op jit(solution)/shard_map/ppermute | solution.py:386
  9.2 1.5 %collective-permute-start.1 = (bf16[144,256]{1,0:T(8,128)(2,1)}, bf16[144,256]{1,0:T(8,128)(2,1)}, u32[]{:S(2)}, u32[]{:S(2)}) collective-permute-start(bf16[144,256]{1,0:T(8,128)(2,1)} %get-tuple-element.24.refs_0_), channel_id=1, source_target_pairs={{0,4},{2,6},{4,0},{6,2},{8,12},{10,14},{12,8},{14,10},{16,20},{18,... | collective-permute-start | bytes 221192 | tf_op jit(solution)/shard_map/ppermute | solution.py:386
  10.7 3.5 %collective-permute-start.3 = (bf16[128,256]{1,0:T(8,128)(2,1)S(1)}, bf16[128,256]{1,0:T(8,128)(2,1)S(1)}, u32[]{:S(2)}, u32[]{:S(2)}) collective-permute-start(bf16[128,256]{1,0:T(8,128)(2,1)S(1)} %get-tuple-element.25), channel_id=1, source_target_pairs={{0,8},{2,10},{4,12},{6,14},{8,16},{10,18},{12,20},{14,22},{16,24},... | collective-permute-start | bytes 196616 | tf_op jit(solution)/shard_map/ppermute | solution.py:389
  14.2 1.3 %collective-permute-start.5 = (bf16[128,256]{1,0:T(8,128)(2,1)S(1)}, bf16[128,256]{1,0:T(8,128)(2,1)S(1)}, u32[]{:S(2)}, u32[]{:S(2)}) collective-permute-start(bf16[128,256]{1,0:T(8,128)(2,1)S(1)} %get-tuple-element.25), channel_id=1, source_target_pairs={{0,24},{2,26},{4,28},{6,30},{1,25},{3,27},{5,29},{7,31}} | collective-permute-start | bytes 196616 | tf_op jit(solution)/shard_map/ppermute | solution.py:389
  15.5 1.9 %dynamic-slice_bitcast_fusion.2 = bf16[512,384]{1,0:T(8,128)(2,1)} fusion(bf16[1,1024,384]{2,1,0:T(8,128)(2,1)} %refs_3_.3, s32[]{:T(128)S(6)} %select_n.7), kind=kLoop, calls=%fused_computation.2 | loop fusion | bytes 786436 | tf_op jit(solution)/shard_map/dynamic_slice | solution.py:409
  17.5 1.8 %dynamic-slice_bitcast_fusion.1 = bf16[512,384]{1,0:T(8,128)(2,1)} fusion(bf16[1,1024,384]{2,1,0:T(8,128)(2,1)} %refs_4_.1, s32[]{:T(128)S(6)} %select_n.7), kind=kLoop, calls=%fused_computation.1 | loop fusion | bytes 786436 | tf_op jit(solution)/shard_map/dynamic_slice | solution.py:409
  19.3 2.0 %collective-permute-start.16 = (bf16[512,384]{1,0:T(8,128)(2,1)}, bf16[512,384]{1,0:T(8,128)(2,1)}, u32[]{:S(2)}, u32[]{:S(2)}) collective-permute-start(bf16[512,384]{1,0:T(8,128)(2,1)} %dynamic-slice_bitcast_fusion.1), channel_id=1, source_target_pairs={{0,8},{2,10},{4,12},{6,14},{8,0},{10,2},{12,4},{14,6},{16,24},{18,... | collective-permute-start | bytes 1179656 | tf_op jit(solution)/shard_map/ppermute | solution.py:386
  21.3 0.7 join.1
  23.8 0.8 dynamic-slice_bitcast_fusion
  24.6 1.4 %collective-permute-start.2 = (bf16[144,256]{1,0:T(8,128)(2,1)}, bf16[144,256]{1,0:T(8,128)(2,1)S(1)}, u32[]{:S(2)}, u32[]{:S(2)}) collective-permute-start(bf16[144,256]{1,0:T(8,128)(2,1)} %get-tuple-element.24.refs_0_), channel_id=1, source_target_pairs={{0,6},{2,4},{4,2},{6,0},{8,14},{10,12},{12,10},{14,8},{16,22},{18,... | collective-permute-start | bytes 221192 | tf_op jit(solution)/shard_map/ppermute | solution.py:386
  26.0 4.1 %collective-permute-done.2.refs_3_ = bf16[144,256]{1,0:T(8,128)(2,1)S(1)} collective-permute-done((bf16[144,256]{1,0:T(8,128)(2,1)}, bf16[144,256]{1,0:T(8,128)(2,1)S(1)}, u32[]{:S(2)}, u32[]{:S(2)}) %collective-permute-start.2) | collective-permute-done | bytes 73760 | tf_op jit(solution)/shard_map/ppermute | solution.py:386
  30.7 1.5 %collective-permute-start.7 = (bf16[400,256]{1,0:T(8,128)(2,1)}, bf16[400,256]{1,0:T(8,128)(2,1)}, u32[]{:S(2)}, u32[]{:S(2)}) collective-permute-start(bf16[400,256]{1,0:T(8,128)(2,1)} %join.1), channel_id=1, source_target_pairs={{0,4},{2,6},{4,0},{6,2},{8,12},{10,14},{12,8},{14,10},{16,20},{18,... | collective-permute-start | bytes 614408 | tf_op jit(solution)/shard_map/ppermute | solution.py:386
  32.2 1.4 %collective-permute-start.8 = (bf16[400,256]{1,0:T(8,128)(2,1)}, bf16[400,256]{1,0:T(8,128)(2,1)}, u32[]{:S(2)}, u32[]{:S(2)}) collective-permute-start(bf16[400,256]{1,0:T(8,128)(2,1)} %join.1), channel_id=1, source_target_pairs={{0,6},{2,4},{4,2},{6,0},{8,14},{10,12},{12,10},{14,8},{16,22},{18,... | collective-permute-start | bytes 614408 | tf_op jit(solution)/shard_map/ppermute | solution.py:386
  33.7 0.9 copy-done.4
  34.7 0.9 copy-done.7
  35.6 0.8 copy-done.10
  36.4 0.8 copy-done.12
  37.2 4.0 %near.1 = (f32[128,1024]{1,0:T(8,128)S(1)}, f32[128,1024]{1,0:T(8,128)S(1)}, f32[128,1024]{1,0:T(8,128)S(1)}) custom-call(s32[4]{0:T(128)S(1)} %pad_add_fusion.place_ref, bf16[128,1024]{1,0:T(8,128)(2,1)S(1)} %copy-done.4, bf16[144,256]{1,0:T(8,128)(2,1)} %get-tuple-element.24.refs_0_, bf16[144,256]{1,0:T(8,128)(2,1)} %collective-permute-done.refs_1_, ...), custom_call_target="tpu_custom_call" | custom-call | flops 469762048 | bytes 4000000 | tf_op jit(solution)/shard_map/near/pallas_call | solution.py:138
  41.3 6.5 %far.1 = (f32[64,1024]{1,0:T(8,128)S(1)}, bf16[64,1024]{1,0:T(8,128)(2,1)S(1)}) custom-call(s32[4]{0:T(128)S(1)} %pad_add_fusion.place_ref, bf16[128,1024]{1,0:T(8,128)(2,1)S(1)} %copy-done.4, f32[128,1024]{1,0:T(8,128)S(1)} %get-tuple-element.26.peak_ref, f32[128,1024]{1,0:T(8,128)S(1)} %get-tuple-element.27.total_ref, ...), custom_call_target="tpu_custom_call" | custom-call | flops 872415232 | bytes 6000000 | tf_op jit(solution)/shard_map/far/pallas_call | solution.py:182
  49.2 0.7 norm.1
  50.5 1.5 %collective-permute-start.11 = (bf16[64,1024]{1,0:T(8,128)(2,1)S(1)}, bf16[64,1024]{1,0:T(8,128)(2,1)S(1)}, u32[]{:S(2)}, u32[]{:S(2)}) collective-permute-start(bf16[64,1024]{1,0:T(8,128)(2,1)S(1)} %get-tuple-element.32.refs_0_), channel_id=1, source_target_pairs={{0,4},{2,6},{4,0},{6,2},{8,12},{10,14},{12,8},{14,10},{16,20},{18,... | collective-permute-start | bytes 393224 | tf_op jit(solution)/shard_map/ppermute | solution.py:386
  52.0 3.5 %collective-permute-done.10.refs_1_ = bf16[64,1024]{1,0:T(8,128)(2,1)S(1)} collective-permute-done((bf16[64,1024]{1,0:T(8,128)(2,1)S(1)}, bf16[64,1024]{1,0:T(8,128)(2,1)S(1)}, u32[]{:S(2)}, u32[]{:S(2)}) %collective-permute-start.10) | collective-permute-done | bytes 131104 | tf_op jit(solution)/shard_map/ppermute | solution.py:386
  55.5 0.9 collective-permute-start.13
  56.5 1.4 %collective-permute-start.12 = (bf16[64,1024]{1,0:T(8,128)(2,1)S(1)}, bf16[64,1024]{1,0:T(8,128)(2,1)S(1)}, u32[]{:S(2)}, u32[]{:S(2)}) collective-permute-start(bf16[64,1024]{1,0:T(8,128)(2,1)S(1)} %get-tuple-element.32.refs_0_), channel_id=1, source_target_pairs={{0,6},{2,4},{4,2},{6,0},{8,14},{10,12},{12,10},{14,8},{16,22},{18,... | collective-permute-start | bytes 393224 | tf_op jit(solution)/shard_map/ppermute | solution.py:386
  57.8 1.1 %share.1.share_ref = f32[512,128]{1,0:T(8,128)S(1)} custom-call(s32[4]{0:T(128)S(1)} %pad_add_fusion.place_ref, bf16[144,256]{1,0:T(8,128)(2,1)} %get-tuple-element.24.refs_0_, bf16[144,256]{1,0:T(8,128)(2,1)} %collective-permute-done.refs_1_, bf16[144,256]{1,0:T(8,128)(2,1)} %collective-permute-done.1.refs_2_, bf16[144,256]{1,0:T(8,128)(2,1)S(1)} %copy-done.8, ...), custom_call_target="tpu_custom_call" | custom-call | flops 1000000 | bytes 400000 | tf_op jit(solution)/shard_map/share/pallas_call | solution.py:260
  58.9 5.0 %collective-permute-done.13.refs_4_ = bf16[64,1024]{1,0:T(8,128)(2,1)S(1)} collective-permute-done((bf16[64,1024]{1,0:T(8,128)(2,1)S(1)}, bf16[64,1024]{1,0:T(8,128)(2,1)S(1)}, u32[]{:S(2)}, u32[]{:S(2)}) %collective-permute-start.13) | collective-permute-done | bytes 131104 | tf_op jit(solution)/shard_map/ppermute | solution.py:386
  64.5 1.5 %collective-permute-start.24 = (bf16[64,1024]{1,0:T(8,128)(2,1)S(1)}, bf16[64,1024]{1,0:T(8,128)(2,1)S(1)}, u32[]{:S(2)}, u32[]{:S(2)}) collective-permute-start(bf16[64,1024]{1,0:T(8,128)(2,1)S(1)} %collective-permute-done.13.refs_4_), channel_id=1, source_target_pairs={{0,4},{2,6},{4,0},{6,2},{8,12},{10,14},{12,8},{14,10},{16,20},{18,... | collective-permute-start | bytes 393224 | tf_op jit(solution)/shard_map/ppermute | solution.py:386
  66.0 1.4 %collective-permute-start.25 = (bf16[64,1024]{1,0:T(8,128)(2,1)S(1)}, bf16[64,1024]{1,0:T(8,128)(2,1)S(1)}, u32[]{:S(2)}, u32[]{:S(2)}) collective-permute-start(bf16[64,1024]{1,0:T(8,128)(2,1)S(1)} %collective-permute-done.13.refs_4_), channel_id=1, source_target_pairs={{0,6},{2,4},{4,2},{6,0},{8,14},{10,12},{12,10},{14,8},{16,22},{18,... | collective-permute-start | bytes 393224 | tf_op jit(solution)/shard_map/ppermute | solution.py:386
  67.4 4.6 %shard_map.109 = (f32[64,1024]{1,0:T(8,128)S(1)}, bf16[64,1024]{1,0:T(8,128)(2,1)S(1)}, bf16[64,1024]{1,0:T(8,128)(2,1)S(1)}, bf16[64,1024]{1,0:T(8,128)(2,1)S(1)}, f32[64,1024]{1,0:T(8,128)S(1)}) custom-call(s32[4]{0:T(128)S(1)} %pad_add_fusion.place_ref, f32[512,128]{1,0:T(8,128)S(1)} %share.1.share_ref, bf16[64,1024]{1,0:T(8,128)(2,1)S(1)} %get-tuple-element.32.refs_0_, ...), custom_call_target="tpu_custom_call" | custom-call | flops 1509949440 | bytes 4718592 | tf_op jit(solution)/shard_map/pallas_call | solution.py:317
  72.3 3.8 %shard_map.110 = (bf16[64,1024]{1,0:T(8,128)(2,1)S(1)}, bf16[64,1024]{1,0:T(8,128)(2,1)S(1)}, bf16[64,1024]{1,0:T(8,128)(2,1)S(1)}) custom-call(s32[4]{0:T(128)S(1)} %pad_add_fusion.place_ref, f32[512,128]{1,0:T(8,128)S(1)} %share.1.share_ref, bf16[64,1024]{1,0:T(8,128)(2,1)S(1)} %collective-permute-done.23.refs_0_, ...), custom_call_target="tpu_custom_call" | custom-call | flops 905969664 | bytes 4718592 | tf_op jit(solution)/shard_map/pallas_call | solution.py:317
  76.1 1.4 %collective-permute-start.26 = (bf16[64,1024]{1,0:T(8,128)(2,1)S(1)}, bf16[64,1024]{1,0:T(8,128)(2,1)S(1)}, u32[]{:S(2)}, u32[]{:S(2)}) collective-permute-start(bf16[64,1024]{1,0:T(8,128)(2,1)S(1)} %get-tuple-element.38), channel_id=1, source_target_pairs={{0,2},{2,0},{4,6},{6,4},{8,10},{10,8},{12,14},{14,12},{16,18},{18,... | collective-permute-start | bytes 393224 | tf_op jit(solution)/shard_map/ppermute | solution.py:386
  78.1 1.5 %collective-permute-start.28 = (bf16[64,1024]{1,0:T(8,128)(2,1)S(1)}, bf16[64,1024]{1,0:T(8,128)(2,1)S(1)}, u32[]{:S(2)}, u32[]{:S(2)}) collective-permute-start(bf16[64,1024]{1,0:T(8,128)(2,1)S(1)} %get-tuple-element.40), channel_id=1, source_target_pairs={{0,6},{2,4},{4,2},{6,0},{8,14},{10,12},{12,10},{14,8},{16,22},{18,... | collective-permute-start | bytes 393224 | tf_op jit(solution)/shard_map/ppermute | solution.py:386
  79.6 1.3 %collective-permute-start.20 = (bf16[64,1024]{1,0:T(8,128)(2,1)S(1)}, bf16[64,1024]{1,0:T(8,128)(2,1)S(1)}, u32[]{:S(2)}, u32[]{:S(2)}) collective-permute-start(bf16[64,1024]{1,0:T(8,128)(2,1)S(1)} %get-tuple-element.34.refs_12_), channel_id=1, source_target_pairs={{0,2},{2,0},{4,6},{6,4},{8,10},{10,8},{12,14},{14,12},{16,18},{18,... | collective-permute-start | bytes 393224 | tf_op jit(solution)/shard_map/ppermute | solution.py:386
  81.6 0.9 collective-permute-done.26.refs_0_
  82.5 1.4 %collective-permute-start.22 = (bf16[64,1024]{1,0:T(8,128)(2,1)S(1)}, bf16[64,1024]{1,0:T(8,128)(2,1)S(1)}, u32[]{:S(2)}, u32[]{:S(2)}) collective-permute-start(bf16[64,1024]{1,0:T(8,128)(2,1)S(1)} %get-tuple-element.36), channel_id=1, source_target_pairs={{0,6},{2,4},{4,2},{6,0},{8,14},{10,12},{12,10},{14,8},{16,22},{18,... | collective-permute-start | bytes 393224 | tf_op jit(solution)/shard_map/ppermute | solution.py:386
  83.9 2.6 %collective-permute-done.27.refs_1_ = bf16[64,1024]{1,0:T(8,128)(2,1)S(1)} collective-permute-done((bf16[64,1024]{1,0:T(8,128)(2,1)S(1)}, bf16[64,1024]{1,0:T(8,128)(2,1)S(1)}, u32[]{:S(2)}, u32[]{:S(2)}) %collective-permute-start.27) | collective-permute-done | bytes 131104 | tf_op jit(solution)/shard_map/ppermute | solution.py:386
  86.7 1.2 %collective-permute-done.20.refs_0_ = bf16[64,1024]{1,0:T(8,128)(2,1)S(1)} collective-permute-done((bf16[64,1024]{1,0:T(8,128)(2,1)S(1)}, bf16[64,1024]{1,0:T(8,128)(2,1)S(1)}, u32[]{:S(2)}, u32[]{:S(2)}) %collective-permute-start.20) | collective-permute-done | bytes 131104 | tf_op jit(solution)/shard_map/ppermute | solution.py:386
  87.9 2.0 %collective-permute-done.21.refs_1_ = bf16[64,1024]{1,0:T(8,128)(2,1)S(1)} collective-permute-done((bf16[64,1024]{1,0:T(8,128)(2,1)S(1)}, bf16[64,1024]{1,0:T(8,128)(2,1)S(1)}, u32[]{:S(2)}, u32[]{:S(2)}) %collective-permute-start.21) | collective-permute-done | bytes 131104 | tf_op jit(solution)/shard_map/ppermute | solution.py:386
  89.9 2.7 %collective-permute-done.29.refs_3_ = bf16[64,1024]{1,0:T(8,128)(2,1)S(1)} collective-permute-done((bf16[64,1024]{1,0:T(8,128)(2,1)S(1)}, bf16[64,1024]{1,0:T(8,128)(2,1)S(1)}, u32[]{:S(2)}, u32[]{:S(2)}) %collective-permute-start.29) | collective-permute-done | bytes 131104 | tf_op jit(solution)/shard_map/ppermute | solution.py:386
  92.7 0.7 final.1
  93.4 1.2 %collective-permute-done.30.received_ref = bf16[64,512]{1,0:T(8,128)(2,1)S(1)} collective-permute-done((bf16[64,512]{1,0:T(8,128)(2,1)S(1)}, bf16[64,512]{1,0:T(8,128)(2,1)S(1)}, u32[]{:S(2)}, u32[]{:S(2)}) %collective-permute-start.30) | collective-permute-done | bytes 65568 | tf_op jit(solution)/shard_map/ppermute | solution.py:392
  94.7 1.2 %assemble.1 = bf16[128,512]{1,0:T(8,128)(2,1)} custom-call(s32[4]{0:T(128)S(1)} %pad_add_fusion.place_ref, bf16[64,512]{1,0:T(8,128)(2,1)S(1)} %get-tuple-element.41.keep_ref, bf16[64,512]{1,0:T(8,128)(2,1)S(1)} %collective-permute-done.30.received_ref), custom_call_target="tpu_custom_call" | custom-call | flops 100000 | bytes 300000 | tf_op jit(solution)/shard_map/assemble/pallas_call | solution.py:466
  (65 shorter events, 6.9 us)
Async XLA Ops:
  0.0 23.8 %copy-start.2 = (bf16[1,384,1024]{2,1,0:T(8,128)(2,1)S(1)}, bf16[1,384,1024]{2,1,0:T(8,128)(2,1)}, u32[]{:S(2)}) copy-start(bf16[1,384,1024]{2,1,0:T(8,128)(2,1)} %refs_5_.3) | copy-start | bytes 2359300
  0.0 0.8 copy-start.13
  0.8 0.8 copy-start.14
  1.6 0.7 copy-start.16
  2.3 0.7 copy-start.17
  3.6 17.7 %collective-permute-start.4 = (bf16[144,256]{1,0:T(8,128)(2,1)}, bf16[144,256]{1,0:T(8,128)(2,1)S(1)}, u32[]{:S(2)}, u32[]{:S(2)}) collective-permute-start(bf16[144,256]{1,0:T(8,128)(2,1)} %get-tuple-element.24.refs_0_), channel_id=1, source_target_pairs={{0,16},{2,18},{4,20},{6,22},{8,24},{10,26},{12,28},{14,30},{16,0},... | collective-permute-start | bytes 221192 | tf_op jit(solution)/shard_map/ppermute | solution.py:386
  7.7 16.8 %collective-permute-start = (bf16[144,256]{1,0:T(8,128)(2,1)}, bf16[144,256]{1,0:T(8,128)(2,1)}, u32[]{:S(2)}, u32[]{:S(2)}) collective-permute-start(bf16[144,256]{1,0:T(8,128)(2,1)} %get-tuple-element.24.refs_0_), channel_id=1, source_target_pairs={{0,2},{2,0},{4,6},{6,4},{8,10},{10,8},{12,14},{14,12},{16,18},{18,... | collective-permute-start | bytes 221192 | tf_op jit(solution)/shard_map/ppermute | solution.py:386
  9.2 15.4 %collective-permute-start.1 = (bf16[144,256]{1,0:T(8,128)(2,1)}, bf16[144,256]{1,0:T(8,128)(2,1)}, u32[]{:S(2)}, u32[]{:S(2)}) collective-permute-start(bf16[144,256]{1,0:T(8,128)(2,1)} %get-tuple-element.24.refs_0_), channel_id=1, source_target_pairs={{0,4},{2,6},{4,0},{6,2},{8,12},{10,14},{12,8},{14,10},{16,20},{18,... | collective-permute-start | bytes 221192 | tf_op jit(solution)/shard_map/ppermute | solution.py:386
  10.7 8.5 %collective-permute-start.3 = (bf16[128,256]{1,0:T(8,128)(2,1)S(1)}, bf16[128,256]{1,0:T(8,128)(2,1)S(1)}, u32[]{:S(2)}, u32[]{:S(2)}) collective-permute-start(bf16[128,256]{1,0:T(8,128)(2,1)S(1)} %get-tuple-element.25), channel_id=1, source_target_pairs={{0,8},{2,10},{4,12},{6,14},{8,16},{10,18},{12,20},{14,22},{16,24},... | collective-permute-start | bytes 196616 | tf_op jit(solution)/shard_map/ppermute | solution.py:389
  14.2 5.1 %collective-permute-start.5 = (bf16[128,256]{1,0:T(8,128)(2,1)S(1)}, bf16[128,256]{1,0:T(8,128)(2,1)S(1)}, u32[]{:S(2)}, u32[]{:S(2)}) collective-permute-start(bf16[128,256]{1,0:T(8,128)(2,1)S(1)} %get-tuple-element.25), channel_id=1, source_target_pairs={{0,24},{2,26},{4,28},{6,30},{1,25},{3,27},{5,29},{7,31}} | collective-permute-start | bytes 196616 | tf_op jit(solution)/shard_map/ppermute | solution.py:389
  15.5 25.7 %copy-start.3 = (bf16[1024,1024]{1,0:T(8,128)(2,1)S(1)}, bf16[1024,1024]{1,0:T(8,128)(2,1)}, u32[]{:S(2)}) copy-start(bf16[1024,1024]{1,0:T(8,128)(2,1)} %refs_3_.2) | copy-start | bytes 6291460
  19.3 28.6 %collective-permute-start.14 = (bf16[512,384]{1,0:T(8,128)(2,1)}, bf16[512,384]{1,0:T(8,128)(2,1)S(1)}, u32[]{:S(2)}, u32[]{:S(2)}) collective-permute-start(bf16[512,384]{1,0:T(8,128)(2,1)} %dynamic-slice_bitcast_fusion.2), channel_id=1, source_target_pairs={{0,8},{2,10},{4,12},{6,14},{8,0},{10,2},{12,4},{14,6},{16,24},{18,... | collective-permute-start | bytes 1179656 | tf_op jit(solution)/shard_map/ppermute | solution.py:386
  19.3 29.1 %collective-permute-start.16 = (bf16[512,384]{1,0:T(8,128)(2,1)}, bf16[512,384]{1,0:T(8,128)(2,1)}, u32[]{:S(2)}, u32[]{:S(2)}) collective-permute-start(bf16[512,384]{1,0:T(8,128)(2,1)} %dynamic-slice_bitcast_fusion.1), channel_id=1, source_target_pairs={{0,8},{2,10},{4,12},{6,14},{8,0},{10,2},{12,4},{14,6},{16,24},{18,... | collective-permute-start | bytes 1179656 | tf_op jit(solution)/shard_map/ppermute | solution.py:386
  22.6 0.6 copy-start.11
  23.2 9.0 %collective-permute-start.6 = (bf16[400,256]{1,0:T(8,128)(2,1)}, bf16[400,256]{1,0:T(8,128)(2,1)S(1)}, u32[]{:S(2)}, u32[]{:S(2)}) collective-permute-start(bf16[400,256]{1,0:T(8,128)(2,1)} %join.1), channel_id=1, source_target_pairs={{0,2},{2,0},{4,6},{6,4},{8,10},{10,8},{12,14},{14,12},{16,18},{18,... | collective-permute-start | bytes 614408 | tf_op jit(solution)/shard_map/ppermute | solution.py:386
  24.5 23.9 %collective-permute-start.18 = (bf16[192,1024]{1,0:T(8,128)(2,1)}, bf16[192,1024]{1,0:T(8,128)(2,1)}, u32[]{:S(2)}, u32[]{:S(2)}) collective-permute-start(bf16[192,1024]{1,0:T(8,128)(2,1)} %dynamic-slice_bitcast_fusion), channel_id=1, source_target_pairs={{0,8},{2,10},{4,12},{6,14},{8,0},{10,2},{12,4},{14,6},{16,24},{18,... | collective-permute-start | bytes 1179656 | tf_op jit(solution)/shard_map/ppermute | solution.py:386
  24.6 5.5 %collective-permute-start.2 = (bf16[144,256]{1,0:T(8,128)(2,1)}, bf16[144,256]{1,0:T(8,128)(2,1)S(1)}, u32[]{:S(2)}, u32[]{:S(2)}) collective-permute-start(bf16[144,256]{1,0:T(8,128)(2,1)} %get-tuple-element.24.refs_0_), channel_id=1, source_target_pairs={{0,6},{2,4},{4,2},{6,0},{8,14},{10,12},{12,10},{14,8},{16,22},{18,... | collective-permute-start | bytes 221192 | tf_op jit(solution)/shard_map/ppermute | solution.py:386
  30.1 0.6 copy-start.6
  30.7 10.5 %collective-permute-start.7 = (bf16[400,256]{1,0:T(8,128)(2,1)}, bf16[400,256]{1,0:T(8,128)(2,1)}, u32[]{:S(2)}, u32[]{:S(2)}) collective-permute-start(bf16[400,256]{1,0:T(8,128)(2,1)} %join.1), channel_id=1, source_target_pairs={{0,4},{2,6},{4,0},{6,2},{8,12},{10,14},{12,8},{14,10},{16,20},{18,... | collective-permute-start | bytes 614408 | tf_op jit(solution)/shard_map/ppermute | solution.py:386
  32.2 9.0 %collective-permute-start.8 = (bf16[400,256]{1,0:T(8,128)(2,1)}, bf16[400,256]{1,0:T(8,128)(2,1)}, u32[]{:S(2)}, u32[]{:S(2)}) collective-permute-start(bf16[400,256]{1,0:T(8,128)(2,1)} %join.1), channel_id=1, source_target_pairs={{0,6},{2,4},{4,2},{6,0},{8,14},{10,12},{12,10},{14,8},{16,22},{18,... | collective-permute-start | bytes 614408 | tf_op jit(solution)/shard_map/ppermute | solution.py:386
  33.7 1.0 copy-start.4
  34.7 0.9 copy-start.7
  35.6 0.8 copy-start.10
  36.4 0.8 copy-start.12
  41.2 8.0 %copy-start.5 = (bf16[128,1024]{1,0:T(8,128)(2,1)S(1)}, bf16[128,1024]{1,0:T(8,128)(2,1)}, u32[]{:S(2)}) copy-start(bf16[128,1024]{1,0:T(8,128)(2,1)} %hidden_ref.1) | copy-start | bytes 786436
  41.2 8.0 %copy-start.15 = (f32[1024]{0:T(1024)S(1)}, f32[1024]{0:T(1024)}, u32[]{:S(2)}) copy-start(f32[1024]{0:T(1024)} %param.16) | copy-start | bytes 12292
  41.3 16.6 %copy-start.8 = (bf16[144,256]{1,0:T(8,128)(2,1)S(1)}, bf16[144,256]{1,0:T(8,128)(2,1)}, u32[]{:S(2)}) copy-start(bf16[144,256]{1,0:T(8,128)(2,1)} %copy-done.6) | copy-start | bytes 221188
  41.3 26.2 %copy-start = (bf16[1,1024,384]{2,1,0:T(8,128)(2,1)S(1)}, bf16[1,1024,384]{2,1,0:T(8,128)(2,1)}, u32[]{:S(2)}) copy-start(bf16[1,1024,384]{2,1,0:T(8,128)(2,1)} %refs_3_.3) | copy-start | bytes 2359300
  41.3 26.1 %copy-start.1 = (bf16[1,1024,384]{2,1,0:T(8,128)(2,1)S(1)}, bf16[1,1024,384]{2,1,0:T(8,128)(2,1)}, u32[]{:S(2)}) copy-start(bf16[1,1024,384]{2,1,0:T(8,128)(2,1)} %refs_4_.1) | copy-start | bytes 2359300
  47.8 1.4 %collective-permute-start.9 = (bf16[64,1024]{1,0:T(8,128)(2,1)S(1)}, bf16[64,1024]{1,0:T(8,128)(2,1)S(1)}, u32[]{:S(2)}, u32[]{:S(2)}) collective-permute-start(bf16[64,1024]{1,0:T(8,128)(2,1)S(1)} %get-tuple-element.30), channel_id=1, source_target_pairs={{0,1},{1,0},{2,3},{3,2},{4,5},{5,4},{6,7},{7,6},{8,9},{9,8},{10,11... | collective-permute-start | bytes 393224 | tf_op jit(solution)/shard_map/ppermute | solution.py:392
  47.9 18.1 %collective-permute-start.15 = (bf16[512,384]{1,0:T(8,128)(2,1)S(1)}, bf16[512,384]{1,0:T(8,128)(2,1)S(1)}, u32[]{:S(2)}, u32[]{:S(2)}) collective-permute-start(bf16[512,384]{1,0:T(8,128)(2,1)S(1)} %collective-permute-done.14.refs_8_.refs_6_), channel_id=1, source_target_pairs={{0,1},{1,0},{2,3},{3,2},{4,5},{5,4},{6,7},{7,6},{8,9},{9,8},{10,11... | collective-permute-start | bytes 1179656 | tf_op jit(solution)/shard_map/ppermute | solution.py:392
  48.4 19.0 %collective-permute-start.17 = (bf16[512,384]{1,0:T(8,128)(2,1)}, bf16[512,384]{1,0:T(8,128)(2,1)S(1)}, u32[]{:S(2)}, u32[]{:S(2)}) collective-permute-start(bf16[512,384]{1,0:T(8,128)(2,1)} %collective-permute-done.16.refs_10_.refs_8_), channel_id=1, source_target_pairs={{0,1},{1,0},{2,3},{3,2},{4,5},{5,4},{6,7},{7,6},{8,9},{9,8},{10,11... | collective-permute-start | bytes 1179656 | tf_op jit(solution)/shard_map/ppermute | solution.py:392
  48.5 19.0 %collective-permute-start.19 = (bf16[192,1024]{1,0:T(8,128)(2,1)}, bf16[192,1024]{1,0:T(8,128)(2,1)S(1)}, u32[]{:S(2)}, u32[]{:S(2)}) collective-permute-start(bf16[192,1024]{1,0:T(8,128)(2,1)} %collective-permute-done.18.refs_12_.refs_10_), channel_id=1, source_target_pairs={{0,1},{1,0},{2,3},{3,2},{4,5},{5,4},{6,7},{7,6},{8,9},{9,8},{10,11... | collective-permute-start | bytes 1179656 | tf_op jit(solution)/shard_map/ppermute | solution.py:392
  49.9 5.6 %collective-permute-start.10 = (bf16[64,1024]{1,0:T(8,128)(2,1)S(1)}, bf16[64,1024]{1,0:T(8,128)(2,1)S(1)}, u32[]{:S(2)}, u32[]{:S(2)}) collective-permute-start(bf16[64,1024]{1,0:T(8,128)(2,1)S(1)} %get-tuple-element.32.refs_0_), channel_id=1, source_target_pairs={{0,2},{2,0},{4,6},{6,4},{8,10},{10,8},{12,14},{14,12},{16,18},{18,... | collective-permute-start | bytes 393224 | tf_op jit(solution)/shard_map/ppermute | solution.py:386
  50.5 5.9 %collective-permute-start.11 = (bf16[64,1024]{1,0:T(8,128)(2,1)S(1)}, bf16[64,1024]{1,0:T(8,128)(2,1)S(1)}, u32[]{:S(2)}, u32[]{:S(2)}) collective-permute-start(bf16[64,1024]{1,0:T(8,128)(2,1)S(1)} %get-tuple-element.32.refs_0_), channel_id=1, source_target_pairs={{0,4},{2,6},{4,0},{6,2},{8,12},{10,14},{12,8},{14,10},{16,20},{18,... | collective-permute-start | bytes 393224 | tf_op jit(solution)/shard_map/ppermute | solution.py:386
  55.5 8.4 %collective-permute-start.13 = (bf16[64,1024]{1,0:T(8,128)(2,1)S(1)}, bf16[64,1024]{1,0:T(8,128)(2,1)S(1)}, u32[]{:S(2)}, u32[]{:S(2)}) collective-permute-start(bf16[64,1024]{1,0:T(8,128)(2,1)S(1)} %get-tuple-element.32.refs_0_), channel_id=1, source_target_pairs={{0,16},{2,18},{4,20},{6,22},{8,24},{10,26},{12,28},{14,30},{16,0},... | collective-permute-start | bytes 393224 | tf_op jit(solution)/shard_map/ppermute | solution.py:386
  56.5 8.0 %collective-permute-start.12 = (bf16[64,1024]{1,0:T(8,128)(2,1)S(1)}, bf16[64,1024]{1,0:T(8,128)(2,1)S(1)}, u32[]{:S(2)}, u32[]{:S(2)}) collective-permute-start(bf16[64,1024]{1,0:T(8,128)(2,1)S(1)} %get-tuple-element.32.refs_0_), channel_id=1, source_target_pairs={{0,6},{2,4},{4,2},{6,0},{8,14},{10,12},{12,10},{14,8},{16,22},{18,... | collective-permute-start | bytes 393224 | tf_op jit(solution)/shard_map/ppermute | solution.py:386
  63.9 8.2 %collective-permute-start.23 = (bf16[64,1024]{1,0:T(8,128)(2,1)S(1)}, bf16[64,1024]{1,0:T(8,128)(2,1)S(1)}, u32[]{:S(2)}, u32[]{:S(2)}) collective-permute-start(bf16[64,1024]{1,0:T(8,128)(2,1)S(1)} %collective-permute-done.13.refs_4_), channel_id=1, source_target_pairs={{0,2},{2,0},{4,6},{6,4},{8,10},{10,8},{12,14},{14,12},{16,18},{18,... | collective-permute-start | bytes 393224 | tf_op jit(solution)/shard_map/ppermute | solution.py:386
  64.5 7.8 %collective-permute-start.24 = (bf16[64,1024]{1,0:T(8,128)(2,1)S(1)}, bf16[64,1024]{1,0:T(8,128)(2,1)S(1)}, u32[]{:S(2)}, u32[]{:S(2)}) collective-permute-start(bf16[64,1024]{1,0:T(8,128)(2,1)S(1)} %collective-permute-done.13.refs_4_), channel_id=1, source_target_pairs={{0,4},{2,6},{4,0},{6,2},{8,12},{10,14},{12,8},{14,10},{16,20},{18,... | collective-permute-start | bytes 393224 | tf_op jit(solution)/shard_map/ppermute | solution.py:386
  66.0 6.3 %collective-permute-start.25 = (bf16[64,1024]{1,0:T(8,128)(2,1)S(1)}, bf16[64,1024]{1,0:T(8,128)(2,1)S(1)}, u32[]{:S(2)}, u32[]{:S(2)}) collective-permute-start(bf16[64,1024]{1,0:T(8,128)(2,1)S(1)} %collective-permute-done.13.refs_4_), channel_id=1, source_target_pairs={{0,6},{2,4},{4,2},{6,0},{8,14},{10,12},{12,10},{14,8},{16,22},{18,... | collective-permute-start | bytes 393224 | tf_op jit(solution)/shard_map/ppermute | solution.py:386
  76.1 6.4 %collective-permute-start.26 = (bf16[64,1024]{1,0:T(8,128)(2,1)S(1)}, bf16[64,1024]{1,0:T(8,128)(2,1)S(1)}, u32[]{:S(2)}, u32[]{:S(2)}) collective-permute-start(bf16[64,1024]{1,0:T(8,128)(2,1)S(1)} %get-tuple-element.38), channel_id=1, source_target_pairs={{0,2},{2,0},{4,6},{6,4},{8,10},{10,8},{12,14},{14,12},{16,18},{18,... | collective-permute-start | bytes 393224 | tf_op jit(solution)/shard_map/ppermute | solution.py:386
  77.4 9.1 %collective-permute-start.27 = (bf16[64,1024]{1,0:T(8,128)(2,1)S(1)}, bf16[64,1024]{1,0:T(8,128)(2,1)S(1)}, u32[]{:S(2)}, u32[]{:S(2)}) collective-permute-start(bf16[64,1024]{1,0:T(8,128)(2,1)S(1)} %get-tuple-element.39), channel_id=1, source_target_pairs={{0,4},{2,6},{4,0},{6,2},{8,12},{10,14},{12,8},{14,10},{16,20},{18,... | collective-permute-start | bytes 393224 | tf_op jit(solution)/shard_map/ppermute | solution.py:386
  78.1 8.4 %collective-permute-start.28 = (bf16[64,1024]{1,0:T(8,128)(2,1)S(1)}, bf16[64,1024]{1,0:T(8,128)(2,1)S(1)}, u32[]{:S(2)}, u32[]{:S(2)}) collective-permute-start(bf16[64,1024]{1,0:T(8,128)(2,1)S(1)} %get-tuple-element.40), channel_id=1, source_target_pairs={{0,6},{2,4},{4,2},{6,0},{8,14},{10,12},{12,10},{14,8},{16,22},{18,... | collective-permute-start | bytes 393224 | tf_op jit(solution)/shard_map/ppermute | solution.py:386
  79.6 8.3 %collective-permute-start.20 = (bf16[64,1024]{1,0:T(8,128)(2,1)S(1)}, bf16[64,1024]{1,0:T(8,128)(2,1)S(1)}, u32[]{:S(2)}, u32[]{:S(2)}) collective-permute-start(bf16[64,1024]{1,0:T(8,128)(2,1)S(1)} %get-tuple-element.34.refs_12_), channel_id=1, source_target_pairs={{0,2},{2,0},{4,6},{6,4},{8,10},{10,8},{12,14},{14,12},{16,18},{18,... | collective-permute-start | bytes 393224 | tf_op jit(solution)/shard_map/ppermute | solution.py:386
  80.9 9.0 %collective-permute-start.21 = (bf16[64,1024]{1,0:T(8,128)(2,1)S(1)}, bf16[64,1024]{1,0:T(8,128)(2,1)S(1)}, u32[]{:S(2)}, u32[]{:S(2)}) collective-permute-start(bf16[64,1024]{1,0:T(8,128)(2,1)S(1)} %get-tuple-element.35), channel_id=1, source_target_pairs={{0,4},{2,6},{4,0},{6,2},{8,12},{10,14},{12,8},{14,10},{16,20},{18,... | collective-permute-start | bytes 393224 | tf_op jit(solution)/shard_map/ppermute | solution.py:386
  82.5 7.4 %collective-permute-start.22 = (bf16[64,1024]{1,0:T(8,128)(2,1)S(1)}, bf16[64,1024]{1,0:T(8,128)(2,1)S(1)}, u32[]{:S(2)}, u32[]{:S(2)}) collective-permute-start(bf16[64,1024]{1,0:T(8,128)(2,1)S(1)} %get-tuple-element.36), channel_id=1, source_target_pairs={{0,6},{2,4},{4,2},{6,0},{8,14},{10,12},{12,10},{14,8},{16,22},{18,... | collective-permute-start | bytes 393224 | tf_op jit(solution)/shard_map/ppermute | solution.py:386
  86.6 6.1 %collective-permute-start.29 = (bf16[64,1024]{1,0:T(8,128)(2,1)S(1)}, bf16[64,1024]{1,0:T(8,128)(2,1)S(1)}, u32[]{:S(2)}, u32[]{:S(2)}) collective-permute-start(bf16[64,1024]{1,0:T(8,128)(2,1)S(1)} %gather_sum.1), channel_id=1, source_target_pairs={{0,16},{2,18},{4,20},{6,22},{8,24},{10,26},{12,28},{14,30},{16,0},... | collective-permute-start | bytes 393224 | tf_op jit(solution)/shard_map/ppermute | solution.py:386
  93.3 1.3 %collective-permute-start.30 = (bf16[64,512]{1,0:T(8,128)(2,1)S(1)}, bf16[64,512]{1,0:T(8,128)(2,1)S(1)}, u32[]{:S(2)}, u32[]{:S(2)}) collective-permute-start(bf16[64,512]{1,0:T(8,128)(2,1)S(1)} %get-tuple-element.42), channel_id=1, source_target_pairs={{0,1},{1,0},{2,3},{3,2},{4,5},{5,4},{6,7},{7,6},{8,9},{9,8},{10,11... | collective-permute-start | bytes 196616 | tf_op jit(solution)/shard_map/ppermute | solution.py:392
  (1 other events, 0.6 us)

commit v2 on v1

--- a/solution.py
+++ b/solution.py
@@ -13,6 +13,8 @@
 LOG2E = 1.4426950408889634
 HIDE = -1e30
 ROOM = 20 << 20
+GROUP = 512
+FULL = 62 << 20
 
 
 def whole(memory_space=pltpu.VMEM):
@@ -23,15 +25,33 @@
     return pl.CostEstimate(flops=int(flops), bytes_accessed=int(size), transcendentals=int(exps))
 
 
-def pack_kernel(key_ref, value_ref, ids_ref, score_ref, rows_ref, mixed_ref):
-    count = key_ref.shape[0]
+def fetch_all(pairs, sems):
+    copies = [
+        pltpu.make_async_copy(source, target, sems.at[n])
+        for n, (source, target) in enumerate(pairs)
+    ]
+    for copy in copies:
+        copy.start()
+    return copies
+
+
+def pack_kernel(key_ref, value_ref, ids_ref, score_ref, rows_ref, mixed_ref, both, ids, score, sems):
+    count, width = key_ref.shape
+    copies = fetch_all(
+        [
+            (key_ref, both.at[:, :width]),
+            (value_ref, both.at[:, width:]),
+            (ids_ref, ids),
+            (score_ref, score),
+        ],
+        sems,
+    )
+    for copy in copies:
+        copy.wait()
+    rows_ref[...] = both[...]
+    mixed_ref[:count, :] = both[...]
     experts = mixed_ref.shape[0] - count
-    both = jnp.concatenate([key_ref[...], value_ref[...]], axis=1)
-    rows_ref[...] = both
-    mixed_ref[:count, :] = both
-    scores = score_ref[...]
-    mix = scores / jnp.sum(scores, axis=0, keepdims=True)
-    ids = ids_ref[...]
+    mix = score[...] / jnp.sum(score[...], axis=0, keepdims=True)
     number = lax.broadcasted_iota(jnp.int32, (experts, count), 0)
     turned = jnp.zeros((experts, count), jnp.float32)
     for k in range(ids.shape[0]):
@@ -43,18 +63,53 @@
 
 def pack(key_rows, value_rows, expert_ids, gate_scores, experts):
     count, width = key_rows.shape
+    top = expert_ids.shape[1]
     return pl.pallas_call(
         pack_kernel,
         out_shape=(
             jax.ShapeDtypeStruct((count, 2 * width), jnp.bfloat16),
             jax.ShapeDtypeStruct((count + experts, 2 * width), jnp.bfloat16),
         ),
-        in_specs=[whole()] * 4,
+        in_specs=[whole(pltpu.HBM)] * 4,
         out_specs=(whole(), whole()),
+        scratch_shapes=[
+            pltpu.VMEM((count, 2 * width), jnp.bfloat16),
+            pltpu.VMEM((top, count), jnp.int32),
+            pltpu.VMEM((top, count), jnp.float32),
+            pltpu.SemaphoreType.DMA((4,)),
+        ],
         cost_estimate=cost(1e5, 3e5),
-        compiler_params=pltpu.CompilerParams(vmem_limit_bytes=ROOM),
+        compiler_params=pltpu.CompilerParams(vmem_limit_bytes=FULL),
         name="pack",
     )(key_rows, value_rows, expert_ids.T, gate_scores.T)
+
+
+def stack_kernel(place_ref, gate_ref, up_ref, mine_ref, other_ref, own_wide, swapped_wide, sems):
+    units, core = gate_ref.shape[2], place_ref[1]
+    mine = pl.ds(pl.multiple_of(core * units, units), units)
+    other = pl.ds(pl.multiple_of((1 - core) * units, units), units)
+    pairs = [
+        (gate_ref.at[0], own_wide.at[:, :units]),
+        (up_ref.at[0], own_wide.at[:, units:]),
+        (mine_ref, swapped_wide.at[:, mine]),
+        (other_ref, swapped_wide.at[:, other]),
+    ]
+    for copy in fetch_all(pairs, sems):
+        copy.wait()
+
+
+def stack(place, w_gate, w_up, mine, other):
+    _, model, units = w_gate.shape
+    return pl.pallas_call(
+        stack_kernel,
+        out_shape=(jax.ShapeDtypeStruct((model, 2 * units), jnp.bfloat16),) * 2,
+        in_specs=[whole(pltpu.SMEM)] + [whole(pl.ANY)] * 4,
+        out_specs=(whole(),) * 2,
+        scratch_shapes=[pltpu.SemaphoreType.DMA((4,))],
+        cost_estimate=cost(1e5, 6e6),
+        compiler_params=pltpu.CompilerParams(vmem_limit_bytes=ROOM),
+        name="stack",
+    )(place, w_gate, w_up, mine, other)
 
 
 def join_kernel(count, *refs):
@@ -80,14 +135,14 @@
     )(*parts)
 
 
-def soften(query, key_ref, value_ref, biases, state):
+def soften(query, keys, values, biases, state):
     scale = HEAD ** (-0.5) * LOG2E
     scores = lax.dot_general(
-        query, key_ref[...], (((1,), (1,)), ((), ())), preferred_element_type=jnp.float32
-    )
-    pieces = [
-        scores[:, n * HEAD : (n + 1) * HEAD] + bias for n, bias in enumerate(biases)
-    ]
+        query, keys, (((1,), (1,)), ((), ())), preferred_element_type=jnp.float32
+    )
+    pieces = [scores[:, n * HEAD : (n + 1) * HEAD] for n in range(keys.shape[0] // HEAD)]
+    if biases is not None:
+        pieces = [piece + bias for piece, bias in zip(pieces, biases)]
     peak = functools.reduce(jnp.maximum, pieces)
     peak = jnp.max(peak, axis=1, keepdims=True)
     if state is not None:
@@ -97,7 +152,7 @@
     total = functools.reduce(jnp.add, weights)
     product = jnp.dot(
         jnp.concatenate([w.astype(jnp.bfloat16) for w in weights], axis=1),
-        value_ref[...],
+        values,
         preferred_element_type=jnp.float32,
     )
     if state is not None:
@@ -108,99 +163,150 @@
 
 
 def near_kernel(plane, place_ref, query_ref, *refs):
+    sources, column_ref = refs[:plane], refs[plane]
+    heads_ref, peak_ref, total_ref, sum_ref, keys, values, sems = refs[plane + 1 :]
     count = query_ref.shape[0]
-    steps = len(refs) - 5
-    sources = refs[:steps]
-    peak_ref, total_ref, sum_ref, keys, values = refs[steps:]
+    pairs = []
+    for head in range(query_ref.shape[1] // HEAD):
+        part = slice(head * count, (head + 1) * count)
+        pairs.append((query_ref.at[:, head * HEAD : (head + 1) * HEAD], heads_ref.at[part]))
+    copies = fetch_all(pairs, sems)
+    layers = column_ref.shape[0] // count
     for n, ref in enumerate(sources):
         keys[n * count : (n + 1) * count, :] = ref[:count, :HEAD]
         values[n * count : (n + 1) * count, :] = ref[:count, HEAD:]
+    keys[plane * count :, :] = column_ref[: layers * count, :HEAD]
+    values[plane * count :, :] = column_ref[: layers * count, HEAD:]
     me = place_ref[0]
-    row = lax.broadcasted_iota(jnp.int32, (count, count), 0)
-    column = lax.broadcasted_iota(jnp.int32, (count, count), 1)
-    biases = [jnp.where(column <= row, 0.0, HIDE)]
+    row = lax.broadcasted_iota(jnp.int32, (GROUP, count), 0) % count
+    number = lax.broadcasted_iota(jnp.int32, (GROUP, count), 1)
+    biases = [jnp.where(number <= row, 0.0, HIDE)]
     for step in range(1, plane):
         biases.append(jnp.where((me ^ step) < me, 0.0, HIDE))
-    for step in range(1, steps - plane + 1):
+    for step in range(1, layers + 1):
         biases.append(jnp.where(me >= step * plane, 0.0, HIDE))
-    for head in range(query_ref.shape[1] // HEAD):
-        part = slice(head * HEAD, (head + 1) * HEAD)
-        peak, total, product = soften(query_ref[:, part], keys, values, biases, None)
-        peak_ref[:, part] = jnp.broadcast_to(peak, (count, HEAD))
-        total_ref[:, part] = total
-        sum_ref[:, part] = product
-
-
-def near(place, queries, sources, plane):
+    for copy in copies:
+        copy.wait()
+    for start in range(0, heads_ref.shape[0], GROUP):
+        part = slice(start, start + GROUP)
+        peak, total, product = soften(heads_ref[part], keys[...], values[...], biases, None)
+        peak_ref[part] = jnp.broadcast_to(peak, (GROUP, HEAD))
+        total_ref[part] = total
+        sum_ref[part] = product
+
+
+def near(place, queries, sources, column, plane):
     count, width = queries.shape
-    shape = jax.ShapeDtypeStruct((count, width), jnp.float32)
-    keys = len(sources) * count
+    rows = count * width // HEAD
+    shape = jax.ShapeDtypeStruct((rows, HEAD), jnp.float32)
+    keys = (plane + column.shape[0] // HEAD) * HEAD
     return pl.pallas_call(
         functools.partial(near_kernel, plane),
+        out_shape=(jax.ShapeDtypeStruct((rows, HEAD), jnp.bfloat16),) + (shape,) * 3,
+        in_specs=[whole(pltpu.SMEM), whole(pl.ANY)] + [whole()] * (1 + len(sources)),
+        out_specs=(whole(),) * 4,
+        scratch_shapes=[pltpu.VMEM((keys, HEAD), jnp.bfloat16)] * 2
+        + [pltpu.SemaphoreType.DMA((width // HEAD,))],
+        cost_estimate=cost(4 * rows * HEAD * keys, 4e6, rows * keys),
+        compiler_params=pltpu.CompilerParams(vmem_limit_bytes=ROOM),
+        name="near",
+    )(place, queries, *sources, column)
+
+
+def extend(plane, place_ref, query_ref, state, sources, keys, values, out):
+    count = HEAD
+    layers = sources[0].shape[0] // count
+    height = place_ref[0] // plane
+
+    @pl.when(height == 0)
+    def _():
+        for source, target in zip(state, out):
+            target[...] = source[...]
+
+    for used in range(1, layers + 1):
+
+        @pl.when(height == used)
+        def _(used=used):
+            span = used * count
+            for n, ref in enumerate(sources):
+                keys[n * span : (n + 1) * span, :] = ref[:span, :HEAD]
+                values[n * span : (n + 1) * span, :] = ref[:span, HEAD:]
+            size = len(sources) * span
+            for start in range(0, query_ref.shape[0], GROUP):
+                part = slice(start, start + GROUP)
+                peak, total, product = soften(
+                    query_ref[part],
+                    keys[:size],
+                    values[:size],
+                    None,
+                    [ref[part] for ref in state],
+                )
+                out[0][part] = jnp.broadcast_to(peak, (GROUP, HEAD))
+                out[1][part] = total
+                out[2][part] = product
+
+
+def more_kernel(plane, steps, place_ref, query_ref, *refs):
+    state, sources, refs = refs[:3], refs[3 : 3 + steps], refs[3 + steps :]
+    extend(plane, place_ref, query_ref, state, sources, refs[3], refs[4], refs[:3])
+
+
+def more(place, heads, state, sources, plane):
+    shape = jax.ShapeDtypeStruct(heads.shape, jnp.float32)
+    keys = len(sources) * (sources[0].shape[0] // HEAD) * HEAD
+    return pl.pallas_call(
+        functools.partial(more_kernel, plane, len(sources)),
         out_shape=(shape,) * 3,
-        in_specs=[whole(pltpu.SMEM)] + [whole()] * (1 + len(sources)),
+        in_specs=[whole(pltpu.SMEM)] + [whole()] * (4 + len(sources)),
         out_specs=(whole(),) * 3,
         scratch_shapes=[pltpu.VMEM((keys, HEAD), jnp.bfloat16)] * 2,
-        cost_estimate=cost(4 * width * count * keys, 4e6, width * keys),
-        compiler_params=pltpu.CompilerParams(vmem_limit_bytes=ROOM),
-        name="near",
-    )(place, queries, *sources)
-
-
-def far_kernel(plane, place_ref, query_ref, peak_ref, total_ref, sum_ref, *refs):
-    steps = plane - 1
-    sources = refs[:steps]
-    weight_ref, own_ref, other_ref, keys, values, attended, weight, result, sem = refs[steps:]
-    fetch = pltpu.make_async_copy(weight_ref, weight, sem)
-    fetch.start()
-    count = query_ref.shape[0]
-    layers = sources[0].shape[0] // count
-    span = layers * count
-    for n, ref in enumerate(sources):
-        keys[n * span : (n + 1) * span, :] = ref[:span, :HEAD]
-        values[n * span : (n + 1) * span, :] = ref[:span, HEAD:]
-    me, core = place_ref[0], place_ref[1]
-    biases = [jnp.where(me >= step * plane, 0.0, HIDE) for step in range(1, layers + 1)] * steps
-    for head in range(query_ref.shape[1] // HEAD):
-        part = slice(head * HEAD, (head + 1) * HEAD)
-        state = (peak_ref[:, part], total_ref[:, part], sum_ref[:, part])
-        _, total, product = soften(query_ref[:, part], keys, values, biases, state)
-        denom = jnp.sum(total, axis=1, keepdims=True)
-        attended[:, part] = (product / denom).astype(jnp.bfloat16)
-    fetch.wait()
-    result[...] = jnp.dot(attended[...], weight[...], preferred_element_type=jnp.float32)
+        cost_estimate=cost(4 * heads.size * keys, 4e6, heads.shape[0] * keys),
+        compiler_params=pltpu.CompilerParams(vmem_limit_bytes=ROOM),
+        name="more",
+    )(place, heads, *state, *sources)
+
+
+def far_kernel(plane, place_ref, query_ref, peak_ref, total_ref, sum_ref, source_ref, *refs):
+    weight_ref, own_ref, other_ref, keys, values, peak, total, product, attended, result = refs
+    state, work = (peak_ref, total_ref, sum_ref), (peak, total, product)
+    extend(plane, place_ref, query_ref, state, (source_ref,), keys, values, work)
+    count = attended.shape[0]
+    core = place_ref[1]
+    for head in range(query_ref.shape[0] // count):
+        part = slice(head * count, (head + 1) * count)
+        denom = jnp.sum(total[part], axis=1, keepdims=True)
+        attended[:, head * HEAD : (head + 1) * HEAD] = (product[part] / denom).astype(jnp.bfloat16)
+    result[...] = jnp.dot(attended[...], weight_ref[...], preferred_element_type=jnp.float32)
     half = count // 2
     own_ref[...] = result[pl.ds(pl.multiple_of(core * half, half), half), :]
     other = result[pl.ds(pl.multiple_of((1 - core) * half, half), half), :]
     other_ref[...] = other.astype(jnp.bfloat16)
 
 
-def far(place, queries, state, sources, out_proj, plane):
-    count, width = queries.shape
-    model = out_proj.shape[1]
-    keys = len(sources) * (sources[0].shape[0] // count) * count
+def far(place, heads, state, source, out_proj, plane):
+    width, model = out_proj.shape
+    count = heads.size // width
+    keys = source.shape[0] // HEAD * HEAD
     return pl.pallas_call(
         functools.partial(far_kernel, plane),
         out_shape=(
             jax.ShapeDtypeStruct((count // 2, model), jnp.float32),
             jax.ShapeDtypeStruct((count // 2, model), jnp.bfloat16),
         ),
-        in_specs=[whole(pltpu.SMEM)] + [whole()] * (4 + len(sources)) + [whole(pl.ANY)],
+        in_specs=[whole(pltpu.SMEM)] + [whole()] * 6,
         out_specs=(whole(),) * 2,
-        scratch_shapes=[
-            pltpu.VMEM((keys, HEAD), jnp.bfloat16),
-            pltpu.VMEM((keys, HEAD), jnp.bfloat16),
+        scratch_shapes=[pltpu.VMEM((keys, HEAD), jnp.bfloat16)] * 2
+        + [pltpu.VMEM(heads.shape, jnp.float32)] * 3
+        + [
             pltpu.VMEM((count, width), jnp.bfloat16),
-            pltpu.VMEM(out_proj.shape, jnp.bfloat16),
             pltpu.VMEM((count, model), jnp.float32),
-            pltpu.SemaphoreType.DMA,
         ],
         cost_estimate=cost(
-            4 * width * count * keys + 2 * count * width * model, 6e6, width * keys
+            4 * heads.size * keys + 2 * count * width * model, 6e6, heads.shape[0] * keys
         ),
         compiler_params=pltpu.CompilerParams(vmem_limit_bytes=ROOM),
         name="far",
-    )(place, queries, *state, *sources, out_proj)
+    )(place, heads, *state, source, out_proj)
 
 
 def norm_kernel(place_ref, hidden_ref, own_ref, other_ref, gain_ref, resid_ref, normed_ref):
@@ -266,70 +372,93 @@
         scratch_shapes=[pltpu.VMEM((count, count), jnp.float32)],
         cost_estimate=cost(1e6, 4e5),
         compiler_params=pltpu.CompilerParams(vmem_limit_bytes=ROOM),
-        name="share",
+        name="columns",
     )(place, *pieces)
 
 
-def expert_kernel(first, blocks, place_ref, share_ref, *refs):
-    inputs, refs = refs[:blocks], refs[blocks:]
-    sources = refs[:9]
-    outputs, rows, mats, sems = refs[-8 - blocks : -8], refs[-8], refs[-7:-1], refs[-1]
-    core = place_ref[1]
-    copies = [pltpu.make_async_copy(sources[n].at[0], mats[n], sems.at[n]) for n in range(3)]
-    for n in range(3):
-        half = mats[3 + n].shape[0] // 2
-        for side in range(2):
-            place = core if side == 0 else 1 - core
-            target = mats[3 + n].at[pl.ds(pl.multiple_of(place * half, half), half)]
-            order = 3 + 2 * n + side
-            copies.append(pltpu.make_async_copy(sources[order], target, sems.at[order]))
-    for copy in copies:
-        copy.start()
+def expert_rows(share_ref, first, inputs, wide_refs, rows, hidden):
     size = inputs[0].shape[0]
+    units = wide_refs[0].shape[1] // 2
     for n, ref in enumerate(inputs):
         rows[n * size : (n + 1) * size, :] = ref[...]
-    total = None
-    for side in range(2):
-        gate_ref, up_ref, down_ref = mats[3 * side : 3 * side + 3]
-        waits = [copies[:1], copies[1:2], copies[2:3]] if side == 0 else [
-            copies[3:5], copies[5:7], copies[7:9]]
-        for copy in waits[0]:
-            copy.wait()
-        gate = jnp.dot(rows[...], gate_ref[...], preferred_element_type=jnp.float32)
-        for copy in waits[1]:
-            copy.wait()
-        upper = jnp.dot(rows[...], up_ref[...], preferred_element_type=jnp.float32)
-        hidden = (gate / (1.0 + jnp.exp(-gate)) * upper).astype(jnp.bfloat16)
-        for copy in waits[2]:
-            copy.wait()
-        part = jnp.dot(hidden, down_ref[...], preferred_element_type=jnp.float32)
-        part = part.astype(jnp.bfloat16).astype(jnp.float32)
-        factor = share_ref[first * size : (first + blocks) * size, side : side + 1]
-        total = part * factor if total is None else total + part * factor
+    for side, wide_ref in enumerate(wide_refs):
+        both = jnp.dot(rows[...], wide_ref[...], preferred_element_type=jnp.float32)
+        gate, upper = both[:, :units], both[:, units:]
+        factor = share_ref[first * size : (first + len(inputs)) * size, side : side + 1]
+        value = gate / (1.0 + jnp.exp(-gate)) * upper * factor
+        hidden[:, side * units : (side + 1) * units] = value.astype(jnp.bfloat16)
+
+
+def expert_sums(hidden, tall_ref, outputs):
+    size = outputs[0].shape[0]
+    total = jnp.dot(hidden[...], tall_ref[...], preferred_element_type=jnp.float32)
     for n, ref in enumerate(outputs):
         ref[...] = total[n * size : (n + 1) * size, :].astype(ref.dtype)
 
 
-def experts_on(place, shares, inputs, weights, first, dtypes, after):
+def expert_near_kernel(blocks, place_ref, share_ref, *refs):
+    inputs, wide_refs, refs = refs[:blocks], refs[blocks : blocks + 2], refs[blocks + 2 :]
+    down_ref, pieces = refs[0], refs[1:5]
+    outputs, tall_ref, rows, hidden, sems = refs[5 : 5 + blocks], *refs[5 + blocks :]
+    units, core = down_ref.shape[1], place_ref[1]
+    size = pieces[0].shape[0]
+    pairs = [(down_ref.at[0], tall_ref.at[:units])]
+    for n, position in enumerate((core, 1 - core)):
+        for part, ref in enumerate(pieces[n::2]):
+            start = units + position * (units // 2) + part * size
+            pairs.append((ref, tall_ref.at[pl.ds(pl.multiple_of(start, size), size)]))
+    copies = fetch_all(pairs, sems)
+    expert_rows(share_ref, 0, inputs, wide_refs, rows, hidden)
+    for copy in copies:
+        copy.wait()
+    expert_sums(hidden, tall_ref, outputs)
+
+
+def expert_far_kernel(first, blocks, share_ref, *refs):
+    inputs, wide_refs, tall_ref = refs[:blocks], refs[blocks : blocks + 2], refs[blocks + 2]
+    outputs, rows, hidden = refs[blocks + 3 : -2], refs[-2], refs[-1]
+    expert_rows(share_ref, first, inputs, wide_refs, rows, hidden)
+    expert_sums(hidden, tall_ref, outputs)
+
+
+def experts_near(place, shares, inputs, wide, w_down, pieces, dtypes):
     blocks = len(inputs)
     size, model = inputs[0].shape
-    units = weights[0].shape[2]
-    return pl.pallas_call(
-        functools.partial(expert_kernel, first, blocks),
-        out_shape=tuple(jax.ShapeDtypeStruct((size, model), dtype) for dtype in dtypes),
-        in_specs=[whole(pltpu.SMEM)] + [whole()] * (1 + blocks) + [whole(pl.ANY)] * (9 + len(after)),
-        out_specs=tuple([whole()] * blocks),
-        scratch_shapes=[pltpu.VMEM((blocks * size, model), jnp.bfloat16)]
-        + [
-            pltpu.VMEM((model, units), jnp.bfloat16),
-            pltpu.VMEM((model, units), jnp.bfloat16),
-            pltpu.VMEM((units, model), jnp.bfloat16),
-        ]
-        * 2
-        + [pltpu.SemaphoreType.DMA((9,))],
-        cost_estimate=cost(12 * blocks * size * model * units, 12 * model * units),
-        compiler_params=pltpu.CompilerParams(vmem_limit_bytes=ROOM),
-    )(place, shares, *inputs, *weights, *after)
+    both = 2 * w_down.shape[1]
+    return pl.pallas_call(
+        functools.partial(expert_near_kernel, blocks),
+        out_shape=tuple(jax.ShapeDtypeStruct((size, model), dtype) for dtype in dtypes)
+        + (jax.ShapeDtypeStruct((both, model), jnp.bfloat16),),
+        in_specs=[whole(pltpu.SMEM)] + [whole()] * (3 + blocks) + [whole(pl.ANY)] * 5,
+        out_specs=(whole(),) * (blocks + 1),
+        scratch_shapes=[
+            pltpu.VMEM((blocks * size, model), jnp.bfloat16),
+            pltpu.VMEM((blocks * size, both), jnp.bfloat16),
+            pltpu.SemaphoreType.DMA((5,)),
+        ],
+        cost_estimate=cost(6 * blocks * size * model * both, 6 * model * both),
+        compiler_params=pltpu.CompilerParams(vmem_limit_bytes=ROOM),
+        name="experts_near",
+    )(place, shares, *inputs, *wide, w_down, *pieces)
+
+
+def experts_far(shares, inputs, wide, tall, first):
+    blocks = len(inputs)
+    size, model = inputs[0].shape
+    both = tall.shape[0]
+    return pl.pallas_call(
+        functools.partial(expert_far_kernel, first, blocks),
+        out_shape=(jax.ShapeDtypeStruct((size, model), jnp.bfloat16),) * blocks,
+        in_specs=[whole()] * (4 + blocks),
+        out_specs=(whole(),) * blocks,
+        scratch_shapes=[
+            pltpu.VMEM((blocks * size, model), jnp.bfloat16),
+            pltpu.VMEM((blocks * size, both), jnp.bfloat16),
+        ],
+        cost_estimate=cost(6 * blocks * size * model * both, 6 * model * both),
+        compiler_params=pltpu.CompilerParams(vmem_limit_bytes=ROOM),
+        name="experts_far",
+    )(shares, *inputs, *wide, tall)
 
 
 def final_kernel(place_ref, resid_ref, own_ref, *refs):
@@ -403,32 +532,39 @@
     joined = join(column, count)
     corner = [flip(joined, mate) for mate in mates]
 
-    halves = []
-    for mat in (w_gate, w_up, w_down):
-        half = mat.shape[1] // 2
-        piece = lax.dynamic_slice_in_dim(mat[0], core * half, half, 0)
-        halves.append(flip(piece, plane))
-    weights = [w_gate, w_up, w_down]
-    for half in halves:
-        weights += [half, across(half)]
-
-    state = near(place, queries, [mixed] + level + column, plane)
-    own, other = far(place, queries, state, corner, out_proj, plane)
+    units = w_gate.shape[2]
+    quarter = units // 4
+
+    def half_flip(value, side):
+        pairs = [(2 * i + side, 2 * (i ^ plane) + side) for i in range(ctx)]
+        return lax.ppermute(value, ("ctx", "exp"), pairs)
+
+    gate_swap = half_flip(w_gate[0], 0)
+    up_swap = half_flip(w_up[0], 1)
+    tall_swap = []
+    for part in range(2):
+        start = core * 2 * quarter + part * quarter
+        piece = lax.dynamic_slice_in_dim(w_down[0], start, quarter, 0)
+        tall_swap.append(flip(piece, plane))
+
+    heads, *state = near(place, queries, [mixed] + level, joined, plane)
+    state = more(place, heads, state, corner[:-1], plane)
+    own, other = far(place, heads, state, corner[-1], out_proj, plane)
     resid, normed = norm(place, hidden_in, own, across(other), norm_gain.reshape(1, model))
-
-    shares = share(place, [mixed] + level + [column[1]] + corner, w_gate.shape[0] * ctx)
+    wide_swap = gate_swap + up_swap
+    wide = stack(place, w_gate, w_up, wide_swap, across(wide_swap))
+    pieces = [value for piece in tall_swap for value in (piece, across(piece))]
+
+    shares = share(place, [mixed] + level + [joined] + corner, w_gate.shape[0] * ctx)
     opposite = flip(normed, away)
     level_rows = [flip(normed, mate) for mate in mates]
     corner_rows = [flip(opposite, mate) for mate in mates]
     f32, bf16 = jnp.float32, jnp.bfloat16
-    near_out = experts_on(
-        place, shares, [normed] + level_rows + [opposite], weights, 0,
-        [f32] + [bf16] * len(mates) + [f32], [],
-    )
-    far_out = experts_on(
-        place, shares, corner_rows, weights, plane + 1, [bf16] * len(mates),
-        [near_out[1]],
-    )
+    *near_out, tall = experts_near(
+        place, shares, [normed] + level_rows + [opposite], wide, w_down, pieces,
+        [f32] + [bf16] * len(mates) + [f32],
+    )
+    far_out = experts_far(shares, corner_rows, wide, tall, plane + 1)
     passed = [flip(value, mate) for value, mate in zip(far_out, mates)]
     direct = [flip(value, mate) for value, mate in zip(near_out[1:plane], mates)]
     last = flip(gather_sum(near_out[plane], passed), away)

time: 96.5 us -> 102 us (1.057)
  waiting for transfers between devices: 23.8 us -> 38.6 us
  local copies, waits for them, and re-layouts: 12.9 us -> 2.58 us
  starting transfers between devices: 34.8 us -> 43 us
  Pallas kernels: 24 us -> 16.5 us
    ppermute x0 -> x2, waiting for transfers between devices: none -> 17.7 us  [half_flip(): return lax.ppermute(value, ('ctx', 'exp'), pairs)]
    unnamed x36 -> x16, local copies, waits for them, and re-layouts: 8.38 us -> 1.87 us
    ppermute x0 -> x2, starting transfers between devices: none -> 5.79 us  [half_flip(): return lax.ppermute(value, ('ctx', 'exp'), pairs)]
    pallas_call x1, Pallas kernels: 6.49 us -> 1.4 us  [far(): pl.pallas_call(functools.partial(far_kernel, plane), out_shape=(jax.Shape...]
    ppermute x24 -> x23, waiting for transfers between devices: 22.2 us -> 17.6 us  [flip(): return lax.ppermute(value, 'ctx', [(i, i ^ mask) for i in range(ctx)])]
    dynamic_slice x3 -> x1, local copies, waits for them, and re-layouts: 4.51 us -> 0.71 us  [compact(): piece = lax.dynamic_slice_in_dim(w_down[0], start, quarter, 0)]
    pallas_call x3 -> x5, Pallas kernels: 12.4 us -> 10.1 us  [the longest x1 3.57 us: experts_near(): pl.pallas_call(functools.partial(expert_near_kernel, blocks), out_shape=t...]
    ppermute x24 -> x23, starting transfers between devices: 28.9 us -> 30.7 us  [flip(): return lax.ppermute(value, 'ctx', [(i, i ^ mask) for i in range(ctx)])]
  transfers between devices with their start and end apart: 31 -> 32, of which waited for: 11 -> 16; matrix products, arithmetic and copies ran while one was open for 5% -> 1% of each run, Pallas kernels for 18% -> 13%
where the time goes in v2:
time: 102 us; the launch traced here: 101 us
  starting transfers between devices  43 us (42%)
  waiting for transfers between devices  38.6 us (38%)
  Pallas kernels  16.5 us (16%)
  local copies, waits for them, and re-layouts  2.58 us (3%)
    ppermute x23, starting transfers between devices, flip(): return lax.ppermute(value, 'ctx', [(i, i ^ mask) for i in range(ctx)])  30.7 us
    ppermute x2, waiting for transfers between devices, half_flip(): return lax.ppermute(value, ('ctx', 'exp'), pairs)  17.7 us
    ppermute x23, waiting for transfers between devices, flip(): return lax.ppermute(value, 'ctx', [(i, i ^ mask) for i in range(ctx)])  17.6 us
    ppermute x2, starting transfers between devices, half_flip(): return lax.ppermute(value, ('ctx', 'exp'), pairs)  5.79 us
    ppermute x2, starting transfers between devices, upward(): lax.ppermute(value, 'ctx', [(i, i + step) for i in range(ctx - step)])  5.67 us
    pallas_call x1, Pallas kernels, experts_near(): pl.pallas_call(functools.partial(expert_near_kernel, blocks), out_shape=t...  3.57 us
    pallas_call x1, Pallas kernels, near(): pl.pallas_call(functools.partial(near_kernel, plane), out_shape=(jax.Shap...  2.74 us
    ppermute x5, waiting for transfers between devices, across(): return lax.ppermute(value, 'exp', [(0, 1), (1, 0)])  2.08 us
  transfers between devices with their start and end apart: 32, of which 16 were waited for; matrix products, arithmetic and copies ran while one was open for 1% of the time, Pallas kernels for 13%

profile of v2, /device:TPU:0, one launch (start us, length us, event | category | flops | bytes accessed | tf_op | source)
XLA Modules:
  0.0 101.3 jit_solution(372725767294962425)
XLA Ops:
  0.0 5.1 %collective-permute-start.14 = (bf16[1024,384]{1,0:T(8,128)(2,1)}, bf16[1024,384]{1,0:T(8,128)(2,1)S(1)}, u32[]{:S(2)}, u32[]{:S(2)}) collective-permute-start(bf16[1024,384]{1,0:T(8,128)(2,1)} %bitcast.12), channel_id=1, source_target_pairs={{0,8},{2,10},{4,12},{6,14},{8,0},{10,2},{12,4},{14,6},{16,24},{18,... | collective-permute-start | bytes 2359304 | tf_op jit(solution)/shard_map/ppermute | solution.py:540
  5.1 0.7 collective-permute-start.15
  5.8 17.7 %collective-permute-done.14 = bf16[1024,384]{1,0:T(8,128)(2,1)S(1)} collective-permute-done((bf16[1024,384]{1,0:T(8,128)(2,1)}, bf16[1024,384]{1,0:T(8,128)(2,1)S(1)}, u32[]{:S(2)}, u32[]{:S(2)}) %collective-permute-start.14) | collective-permute-done | bytes 786464 | tf_op jit(solution)/shard_map/ppermute | solution.py:540
  23.9 0.7 dynamic-slice_bitcast_fusion
  24.6 1.7 %collective-permute-start.17 = (bf16[96,1024]{1,0:T(8,128)(2,1)}, bf16[96,1024]{1,0:T(8,128)(2,1)S(1)}, u32[]{:S(2)}, u32[]{:S(2)}) collective-permute-start(bf16[96,1024]{1,0:T(8,128)(2,1)} %get-tuple-element.58), channel_id=1, source_target_pairs={{0,8},{2,10},{4,12},{6,14},{8,0},{10,2},{12,4},{14,6},{16,24},{18,... | collective-permute-start | bytes 589832 | tf_op jit(solution)/shard_map/ppermute | solution.py:515
  26.3 1.5 %pack.1 = (bf16[128,256]{1,0:T(8,128)(2,1)}, bf16[144,256]{1,0:T(8,128)(2,1)}) custom-call(bf16[128,128]{1,0:T(8,128)(2,1)} %key_ref.1, bf16[128,128]{1,0:T(8,128)(2,1)} %value_ref.1, s32[8,128]{1,0:T(8,128)} %bitcast.15, f32[8,128]{1,0:T(8,128)} %bitcast.16), custom_call_target="tpu_custom_call" | custom-call | flops 100000 | bytes 300000 | tf_op jit(solution)/shard_map/pack/pallas_call | solution.py:67
  27.8 2.2 %collective-permute-start.3 = (bf16[128,256]{1,0:T(8,128)(2,1)}, bf16[128,256]{1,0:T(8,128)(2,1)S(1)}, u32[]{:S(2)}, u32[]{:S(2)}) collective-permute-start(bf16[128,256]{1,0:T(8,128)(2,1)} %get-tuple-element.32), channel_id=1, source_target_pairs={{0,8},{2,10},{4,12},{6,14},{8,16},{10,18},{12,20},{14,22},{16,24},... | collective-permute-start | bytes 196616 | tf_op jit(solution)/shard_map/ppermute | solution.py:518
  30.0 3.5 %collective-permute-start.5 = (bf16[128,256]{1,0:T(8,128)(2,1)}, bf16[128,256]{1,0:T(8,128)(2,1)S(1)}, u32[]{:S(2)}, u32[]{:S(2)}) collective-permute-start(bf16[128,256]{1,0:T(8,128)(2,1)} %get-tuple-element.32), channel_id=1, source_target_pairs={{0,24},{2,26},{4,28},{6,30},{1,25},{3,27},{5,29},{7,31}} | collective-permute-start | bytes 196616 | tf_op jit(solution)/shard_map/ppermute | solution.py:518
  33.6 1.6 %collective-permute-start = (bf16[144,256]{1,0:T(8,128)(2,1)}, bf16[144,256]{1,0:T(8,128)(2,1)S(1)}, u32[]{:S(2)}, u32[]{:S(2)}) collective-permute-start(bf16[144,256]{1,0:T(8,128)(2,1)} %get-tuple-element.31.refs_0_), channel_id=1, source_target_pairs={{0,2},{2,0},{4,6},{6,4},{8,10},{10,8},{12,14},{14,12},{16,18},{18,... | collective-permute-start | bytes 221192 | tf_op jit(solution)/shard_map/ppermute | solution.py:515
  35.1 1.2 %collective-permute-done.5.refs_2_ = bf16[128,256]{1,0:T(8,128)(2,1)S(1)} collective-permute-done((bf16[128,256]{1,0:T(8,128)(2,1)}, bf16[128,256]{1,0:T(8,128)(2,1)S(1)}, u32[]{:S(2)}, u32[]{:S(2)}) %collective-permute-start.5) | collective-permute-done | bytes 65568 | tf_op jit(solution)/shard_map/ppermute | solution.py:518
  36.3 1.5 %collective-permute-start.1 = (bf16[144,256]{1,0:T(8,128)(2,1)}, bf16[144,256]{1,0:T(8,128)(2,1)S(1)}, u32[]{:S(2)}, u32[]{:S(2)}) collective-permute-start(bf16[144,256]{1,0:T(8,128)(2,1)} %get-tuple-element.31.refs_0_), channel_id=1, source_target_pairs={{0,4},{2,6},{4,0},{6,2},{8,12},{10,14},{12,8},{14,10},{16,20},{18,... | collective-permute-start | bytes 221192 | tf_op jit(solution)/shard_map/ppermute | solution.py:515
  37.8 2.0 %collective-permute-done.4.refs_1_ = bf16[144,256]{1,0:T(8,128)(2,1)S(1)} collective-permute-done((bf16[144,256]{1,0:T(8,128)(2,1)}, bf16[144,256]{1,0:T(8,128)(2,1)S(1)}, u32[]{:S(2)}, u32[]{:S(2)}) %collective-permute-start.4) | collective-permute-done | bytes 73760 | tf_op jit(solution)/shard_map/ppermute | solution.py:515
  39.8 2.4 %collective-permute-start.2 = (bf16[144,256]{1,0:T(8,128)(2,1)}, bf16[144,256]{1,0:T(8,128)(2,1)S(1)}, u32[]{:S(2)}, u32[]{:S(2)}) collective-permute-start(bf16[144,256]{1,0:T(8,128)(2,1)} %get-tuple-element.31.refs_0_), channel_id=1, source_target_pairs={{0,6},{2,4},{4,2},{6,0},{8,14},{10,12},{12,10},{14,8},{16,22},{18,... | collective-permute-start | bytes 221192 | tf_op jit(solution)/shard_map/ppermute | solution.py:515
  42.3 0.6 collective-permute-start.6
  43.4 2.7 %collective-permute-done.2.refs_3_ = bf16[144,256]{1,0:T(8,128)(2,1)S(1)} collective-permute-done((bf16[144,256]{1,0:T(8,128)(2,1)}, bf16[144,256]{1,0:T(8,128)(2,1)S(1)}, u32[]{:S(2)}, u32[]{:S(2)}) %collective-permute-start.2) | collective-permute-done | bytes 73760 | tf_op jit(solution)/shard_map/ppermute | solution.py:515
  46.1 2.4 %collective-permute-start.8 = (bf16[400,256]{1,0:T(8,128)(2,1)S(1)}, bf16[400,256]{1,0:T(8,128)(2,1)S(1)}, u32[]{:S(2)}, u32[]{:S(2)}) collective-permute-start(bf16[400,256]{1,0:T(8,128)(2,1)S(1)} %join.1.refs_4_), channel_id=1, source_target_pairs={{0,6},{2,4},{4,2},{6,0},{8,14},{10,12},{12,10},{14,8},{16,22},{18,... | collective-permute-start | bytes 614408 | tf_op jit(solution)/shard_map/ppermute | solution.py:515
  48.6 0.9 copy-done.5
  49.5 0.9 copy-done.7
  50.4 2.7 %near.1 = (bf16[1024,128]{1,0:T(8,128)(2,1)S(1)}, f32[1024,128]{1,0:T(8,128)S(1)}, f32[1024,128]{1,0:T(8,128)S(1)}, f32[1024,128]{1,0:T(8,128)S(1)}) custom-call(s32[4]{0:T(128)S(1)} %pad_add_fusion.place_ref, bf16[128,1024]{1,0:T(8,128)(2,1)S(1)} %copy-done.7, bf16[144,256]{1,0:T(8,128)(2,1)S(1)} %copy-done.5, ...), custom_call_target="tpu_custom_call" | custom-call | flops 469762048 | bytes 4000000 | tf_op jit(solution)/shard_map/near/pallas_call | solution.py:203
  53.3 0.9 collective-permute-done.7.refs_4_.refs_6_
  54.2 0.7 more.1
  54.9 1.4 %far.1 = (f32[64,1024]{1,0:T(8,128)S(1)}, bf16[64,1024]{1,0:T(8,128)(2,1)S(1)}) custom-call(s32[4]{0:T(128)S(1)} %pad_add_fusion.place_ref, bf16[1024,128]{1,0:T(8,128)(2,1)S(1)} %get-tuple-element.33.query_ref, f32[1024,128]{1,0:T(8,128)S(1)} %get-tuple-element.37.peak_ref, f32[1024,128]{1,0:T(8,128)S(1)} %get-tuple-element.38.total_ref, ...), custom_call_target="tpu_custom_call" | custom-call | flops 469762048 | bytes 6000000 | tf_op jit(solution)/shard_map/far/pallas_call | solution.py:290
  56.9 0.8 collective-permute-done.9.other_ref
  57.8 0.7 norm.1
  58.5 5.9 %collective-permute-start.13 = (bf16[64,1024]{1,0:T(8,128)(2,1)S(1)}, bf16[64,1024]{1,0:T(8,128)(2,1)S(1)}, u32[]{:S(2)}, u32[]{:S(2)}) collective-permute-start(bf16[64,1024]{1,0:T(8,128)(2,1)S(1)} %get-tuple-element.43.refs_0_), channel_id=1, source_target_pairs={{0,16},{2,18},{4,20},{6,22},{8,24},{10,26},{12,28},{14,30},{16,0},... | collective-permute-start | bytes 393224 | tf_op jit(solution)/shard_map/ppermute | solution.py:515
  64.4 0.5 collective-permute-start.10
  65.4 2.4 %collective-permute-start.12 = (bf16[64,1024]{1,0:T(8,128)(2,1)S(1)}, bf16[64,1024]{1,0:T(8,128)(2,1)S(1)}, u32[]{:S(2)}, u32[]{:S(2)}) collective-permute-start(bf16[64,1024]{1,0:T(8,128)(2,1)S(1)} %get-tuple-element.43.refs_0_), channel_id=1, source_target_pairs={{0,6},{2,4},{4,2},{6,0},{8,14},{10,12},{12,10},{14,8},{16,22},{18,... | collective-permute-start | bytes 393224 | tf_op jit(solution)/shard_map/ppermute | solution.py:515
  67.9 0.9 columns.1.share_ref
  68.8 2.0 %stack.18 = (bf16[1024,768]{1,0:T(8,128)(2,1)S(1)}, bf16[1024,768]{1,0:T(8,128)(2,1)S(1)}) custom-call(s32[4]{0:T(128)S(1)} %pad_add_fusion.place_ref, bf16[1,1024,384]{2,1,0:T(8,128)(2,1)S(1)} %copy-done.2, bf16[1,1024,384]{2,1,0:T(8,128)(2,1)S(1)} %copy-done.3, bf16[1024,384]{1,0:T(8,128)(2,1)S(1)} %add.14.mine_ref, ...), custom_call_target="tpu_custom_call" | custom-call | flops 100000 | bytes 6000000 | tf_op jit(solution)/shard_map/stack/pallas_call | solution.py:103
  71.2 0.5 collective-permute-start.24
  72.3 2.4 %collective-permute-start.26 = (bf16[64,1024]{1,0:T(8,128)(2,1)S(1)}, bf16[64,1024]{1,0:T(8,128)(2,1)S(1)}, u32[]{:S(2)}, u32[]{:S(2)}) collective-permute-start(bf16[64,1024]{1,0:T(8,128)(2,1)S(1)} %collective-permute-done.13.refs_4_), channel_id=1, source_target_pairs={{0,6},{2,4},{4,2},{6,0},{8,14},{10,12},{12,10},{14,8},{16,22},{18,... | collective-permute-start | bytes 393224 | tf_op jit(solution)/shard_map/ppermute | solution.py:515
  74.7 3.6 %experts_near.1 = (f32[64,1024]{1,0:T(8,128)S(1)}, bf16[64,1024]{1,0:T(8,128)(2,1)S(1)}, bf16[64,1024]{1,0:T(8,128)(2,1)S(1)}, bf16[64,1024]{1,0:T(8,128)(2,1)S(...) custom-call(s32[4]{0:T(128)S(1)} %pad_add_fusion.place_ref, f32[512,128]{1,0:T(8,128)S(1)} %columns.1.share_ref, ...), custom_call_target="tpu_custom_call" | custom-call | flops 1509949440 | bytes 4718592 | tf_op jit(solution)/shard_map/experts_near/pallas_call | solution.py:428
  78.3 1.2 %collective-permute-done.25.refs_1_ = bf16[64,1024]{1,0:T(8,128)(2,1)S(1)} collective-permute-done((bf16[64,1024]{1,0:T(8,128)(2,1)S(1)}, bf16[64,1024]{1,0:T(8,128)(2,1)S(1)}, u32[]{:S(2)}, u32[]{:S(2)}) %collective-permute-start.25) | collective-permute-done | bytes 131104 | tf_op jit(solution)/shard_map/ppermute | solution.py:515
  79.5 1.2 %experts_far.1 = (bf16[64,1024]{1,0:T(8,128)(2,1)S(1)}, bf16[64,1024]{1,0:T(8,128)(2,1)S(1)}, bf16[64,1024]{1,0:T(8,128)(2,1)S(1)}) custom-call(f32[512,128]{1,0:T(8,128)S(1)} %columns.1.share_ref, bf16[64,1024]{1,0:T(8,128)(2,1)S(1)} %collective-permute-done.24.refs_0_, bf16[64,1024]{1,0:T(8,128)(2,1)S(1)} %collective-permute-done.25.refs_1_, ...), custom_call_target="tpu_custom_call" | custom-call | flops 905969664 | bytes 4718592 | tf_op jit(solution)/shard_map/experts_far/pallas_call | solution.py:449
  80.7 1.6 %collective-permute-start.27 = (bf16[64,1024]{1,0:T(8,128)(2,1)S(1)}, bf16[64,1024]{1,0:T(8,128)(2,1)S(1)}, u32[]{:S(2)}, u32[]{:S(2)}) collective-permute-start(bf16[64,1024]{1,0:T(8,128)(2,1)S(1)} %get-tuple-element.52), channel_id=1, source_target_pairs={{0,2},{2,0},{4,6},{6,4},{8,10},{10,8},{12,14},{14,12},{16,18},{18,... | collective-permute-start | bytes 393224 | tf_op jit(solution)/shard_map/ppermute | solution.py:515
  82.8 1.5 %collective-permute-start.29 = (bf16[64,1024]{1,0:T(8,128)(2,1)S(1)}, bf16[64,1024]{1,0:T(8,128)(2,1)S(1)}, u32[]{:S(2)}, u32[]{:S(2)}) collective-permute-start(bf16[64,1024]{1,0:T(8,128)(2,1)S(1)} %get-tuple-element.54), channel_id=1, source_target_pairs={{0,6},{2,4},{4,2},{6,0},{8,14},{10,12},{12,10},{14,8},{16,22},{18,... | collective-permute-start | bytes 393224 | tf_op jit(solution)/shard_map/ppermute | solution.py:515
  84.3 1.5 %collective-permute-start.21 = (bf16[64,1024]{1,0:T(8,128)(2,1)S(1)}, bf16[64,1024]{1,0:T(8,128)(2,1)S(1)}, u32[]{:S(2)}, u32[]{:S(2)}) collective-permute-start(bf16[64,1024]{1,0:T(8,128)(2,1)S(1)} %get-tuple-element.47), channel_id=1, source_target_pairs={{0,2},{2,0},{4,6},{6,4},{8,10},{10,8},{12,14},{14,12},{16,18},{18,... | collective-permute-start | bytes 393224 | tf_op jit(solution)/shard_map/ppermute | solution.py:515
  86.3 0.9 collective-permute-done.27.refs_0_
  87.1 1.3 %collective-permute-start.23 = (bf16[64,1024]{1,0:T(8,128)(2,1)S(1)}, bf16[64,1024]{1,0:T(8,128)(2,1)S(1)}, u32[]{:S(2)}, u32[]{:S(2)}) collective-permute-start(bf16[64,1024]{1,0:T(8,128)(2,1)S(1)} %get-tuple-element.49), channel_id=1, source_target_pairs={{0,6},{2,4},{4,2},{6,0},{8,14},{10,12},{12,10},{14,8},{16,22},{18,... | collective-permute-start | bytes 393224 | tf_op jit(solution)/shard_map/ppermute | solution.py:515
  88.5 1.0 collective-permute-done.28.refs_1_
  89.5 1.3 %collective-permute-done.29.refs_2_ = bf16[64,1024]{1,0:T(8,128)(2,1)S(1)} collective-permute-done((bf16[64,1024]{1,0:T(8,128)(2,1)S(1)}, bf16[64,1024]{1,0:T(8,128)(2,1)S(1)}, u32[]{:S(2)}, u32[]{:S(2)}) %collective-permute-start.29) | collective-permute-done | bytes 131104 | tf_op jit(solution)/shard_map/ppermute | solution.py:515
  90.9 1.1 %collective-permute-done.21.refs_0_ = bf16[64,1024]{1,0:T(8,128)(2,1)S(1)} collective-permute-done((bf16[64,1024]{1,0:T(8,128)(2,1)S(1)}, bf16[64,1024]{1,0:T(8,128)(2,1)S(1)}, u32[]{:S(2)}, u32[]{:S(2)}) %collective-permute-start.21) | collective-permute-done | bytes 131104 | tf_op jit(solution)/shard_map/ppermute | solution.py:515
  91.9 0.9 collective-permute-done.22.refs_1_
  92.8 1.4 %collective-permute-done.23.refs_2_ = bf16[64,1024]{1,0:T(8,128)(2,1)S(1)} collective-permute-done((bf16[64,1024]{1,0:T(8,128)(2,1)S(1)}, bf16[64,1024]{1,0:T(8,128)(2,1)S(1)}, u32[]{:S(2)}, u32[]{:S(2)}) %collective-permute-start.23) | collective-permute-done | bytes 131104 | tf_op jit(solution)/shard_map/ppermute | solution.py:515
  94.3 3.8 %collective-permute-done.30.refs_3_ = bf16[64,1024]{1,0:T(8,128)(2,1)S(1)} collective-permute-done((bf16[64,1024]{1,0:T(8,128)(2,1)S(1)}, bf16[64,1024]{1,0:T(8,128)(2,1)S(1)}, u32[]{:S(2)}, u32[]{:S(2)}) %collective-permute-start.30) | collective-permute-done | bytes 131104 | tf_op jit(solution)/shard_map/ppermute | solution.py:515
  98.1 0.7 final.1
  98.9 1.2 %collective-permute-done.31.received_ref = bf16[64,512]{1,0:T(8,128)(2,1)S(1)} collective-permute-done((bf16[64,512]{1,0:T(8,128)(2,1)S(1)}, bf16[64,512]{1,0:T(8,128)(2,1)S(1)}, u32[]{:S(2)}, u32[]{:S(2)}) %collective-permute-start.31) | collective-permute-done | bytes 65568 | tf_op jit(solution)/shard_map/ppermute | solution.py:521
  100.1 1.2 %assemble.1 = bf16[128,512]{1,0:T(8,128)(2,1)} custom-call(s32[4]{0:T(128)S(1)} %pad_add_fusion.place_ref, bf16[64,512]{1,0:T(8,128)(2,1)S(1)} %get-tuple-element.55.keep_ref, bf16[64,512]{1,0:T(8,128)(2,1)S(1)} %collective-permute-done.31.received_ref), custom_call_target="tpu_custom_call" | custom-call | flops 100000 | bytes 300000 | tf_op jit(solution)/shard_map/assemble/pallas_call | solution.py:602
  (48 shorter events, 4.4 us)
Async XLA Ops:
  0.0 23.9 %copy-start.1 = (bf16[1,384,1024]{2,1,0:T(8,128)(2,1)S(1)}, bf16[1,384,1024]{2,1,0:T(8,128)(2,1)}, u32[]{:S(2)}) copy-start(bf16[1,384,1024]{2,1,0:T(8,128)(2,1)} %refs_7_.1) | copy-start | bytes 2359300
  0.0 23.5 %collective-permute-start.14 = (bf16[1024,384]{1,0:T(8,128)(2,1)}, bf16[1024,384]{1,0:T(8,128)(2,1)S(1)}, u32[]{:S(2)}, u32[]{:S(2)}) collective-permute-start(bf16[1024,384]{1,0:T(8,128)(2,1)} %bitcast.12), channel_id=1, source_target_pairs={{0,8},{2,10},{4,12},{6,14},{8,0},{10,2},{12,4},{14,6},{16,24},{18,... | collective-permute-start | bytes 2359304 | tf_op jit(solution)/shard_map/ppermute | solution.py:540
  5.1 18.5 %collective-permute-start.15 = (bf16[1024,384]{1,0:T(8,128)(2,1)}, bf16[1024,384]{1,0:T(8,128)(2,1)S(1)}, u32[]{:S(2)}, u32[]{:S(2)}) collective-permute-start(bf16[1024,384]{1,0:T(8,128)(2,1)} %bitcast.13), channel_id=1, source_target_pairs={{1,9},{3,11},{5,13},{7,15},{9,1},{11,3},{13,5},{15,7},{17,25},{19,... | collective-permute-start | bytes 2359304 | tf_op jit(solution)/shard_map/ppermute | solution.py:540
  23.8 41.7 %collective-permute-start.16 = (bf16[1024,384]{1,0:T(8,128)(2,1)S(1)}, bf16[1024,384]{1,0:T(8,128)(2,1)}, u32[]{:S(2)}, u32[]{:S(2)}) collective-permute-start(bf16[1024,384]{1,0:T(8,128)(2,1)S(1)} %add.14.mine_ref), channel_id=1, source_target_pairs={{0,1},{1,0},{2,3},{3,2},{4,5},{5,4},{6,7},{7,6},{8,9},{9,8},{10,11... | collective-permute-start | bytes 2359304 | tf_op jit(solution)/shard_map/ppermute | solution.py:521
  24.6 23.9 %collective-permute-start.17 = (bf16[96,1024]{1,0:T(8,128)(2,1)}, bf16[96,1024]{1,0:T(8,128)(2,1)S(1)}, u32[]{:S(2)}, u32[]{:S(2)}) collective-permute-start(bf16[96,1024]{1,0:T(8,128)(2,1)} %get-tuple-element.58), channel_id=1, source_target_pairs={{0,8},{2,10},{4,12},{6,14},{8,0},{10,2},{12,4},{14,6},{16,24},{18,... | collective-permute-start | bytes 589832 | tf_op jit(solution)/shard_map/ppermute | solution.py:515
  27.8 5.8 %collective-permute-start.3 = (bf16[128,256]{1,0:T(8,128)(2,1)}, bf16[128,256]{1,0:T(8,128)(2,1)S(1)}, u32[]{:S(2)}, u32[]{:S(2)}) collective-permute-start(bf16[128,256]{1,0:T(8,128)(2,1)} %get-tuple-element.32), channel_id=1, source_target_pairs={{0,8},{2,10},{4,12},{6,14},{8,16},{10,18},{12,20},{14,22},{16,24},... | collective-permute-start | bytes 196616 | tf_op jit(solution)/shard_map/ppermute | solution.py:518
  30.0 6.3 %collective-permute-start.5 = (bf16[128,256]{1,0:T(8,128)(2,1)}, bf16[128,256]{1,0:T(8,128)(2,1)S(1)}, u32[]{:S(2)}, u32[]{:S(2)}) collective-permute-start(bf16[128,256]{1,0:T(8,128)(2,1)} %get-tuple-element.32), channel_id=1, source_target_pairs={{0,24},{2,26},{4,28},{6,30},{1,25},{3,27},{5,29},{7,31}} | collective-permute-start | bytes 196616 | tf_op jit(solution)/shard_map/ppermute | solution.py:518
  33.5 6.3 %collective-permute-start.4 = (bf16[144,256]{1,0:T(8,128)(2,1)}, bf16[144,256]{1,0:T(8,128)(2,1)S(1)}, u32[]{:S(2)}, u32[]{:S(2)}) collective-permute-start(bf16[144,256]{1,0:T(8,128)(2,1)} %get-tuple-element.31.refs_0_), channel_id=1, source_target_pairs={{0,16},{2,18},{4,20},{6,22},{8,24},{10,26},{12,28},{14,30},{16,0},... | collective-permute-start | bytes 221192 | tf_op jit(solution)/shard_map/ppermute | solution.py:515
  33.6 8.7 %collective-permute-start = (bf16[144,256]{1,0:T(8,128)(2,1)}, bf16[144,256]{1,0:T(8,128)(2,1)S(1)}, u32[]{:S(2)}, u32[]{:S(2)}) collective-permute-start(bf16[144,256]{1,0:T(8,128)(2,1)} %get-tuple-element.31.refs_0_), channel_id=1, source_target_pairs={{0,2},{2,0},{4,6},{6,4},{8,10},{10,8},{12,14},{14,12},{16,18},{18,... | collective-permute-start | bytes 221192 | tf_op jit(solution)/shard_map/ppermute | solution.py:515
  36.3 6.6 %collective-permute-start.1 = (bf16[144,256]{1,0:T(8,128)(2,1)}, bf16[144,256]{1,0:T(8,128)(2,1)S(1)}, u32[]{:S(2)}, u32[]{:S(2)}) collective-permute-start(bf16[144,256]{1,0:T(8,128)(2,1)} %get-tuple-element.31.refs_0_), channel_id=1, source_target_pairs={{0,4},{2,6},{4,0},{6,2},{8,12},{10,14},{12,8},{14,10},{16,20},{18,... | collective-permute-start | bytes 221192 | tf_op jit(solution)/shard_map/ppermute | solution.py:515
  39.8 6.3 %collective-permute-start.2 = (bf16[144,256]{1,0:T(8,128)(2,1)}, bf16[144,256]{1,0:T(8,128)(2,1)S(1)}, u32[]{:S(2)}, u32[]{:S(2)}) collective-permute-start(bf16[144,256]{1,0:T(8,128)(2,1)} %get-tuple-element.31.refs_0_), channel_id=1, source_target_pairs={{0,6},{2,4},{4,2},{6,0},{8,14},{10,12},{12,10},{14,8},{16,22},{18,... | collective-permute-start | bytes 221192 | tf_op jit(solution)/shard_map/ppermute | solution.py:515
  42.3 10.9 %collective-permute-start.6 = (bf16[400,256]{1,0:T(8,128)(2,1)S(1)}, bf16[400,256]{1,0:T(8,128)(2,1)S(1)}, u32[]{:S(2)}, u32[]{:S(2)}) collective-permute-start(bf16[400,256]{1,0:T(8,128)(2,1)S(1)} %join.1.refs_4_), channel_id=1, source_target_pairs={{0,2},{2,0},{4,6},{6,4},{8,10},{10,8},{12,14},{14,12},{16,18},{18,... | collective-permute-start | bytes 614408 | tf_op jit(solution)/shard_map/ppermute | solution.py:515
  42.9 11.3 %collective-permute-start.7 = (bf16[400,256]{1,0:T(8,128)(2,1)S(1)}, bf16[400,256]{1,0:T(8,128)(2,1)S(1)}, u32[]{:S(2)}, u32[]{:S(2)}) collective-permute-start(bf16[400,256]{1,0:T(8,128)(2,1)S(1)} %join.1.refs_4_), channel_id=1, source_target_pairs={{0,4},{2,6},{4,0},{6,2},{8,12},{10,14},{12,8},{14,10},{16,20},{18,... | collective-permute-start | bytes 614408 | tf_op jit(solution)/shard_map/ppermute | solution.py:515
  46.1 8.8 %collective-permute-start.8 = (bf16[400,256]{1,0:T(8,128)(2,1)S(1)}, bf16[400,256]{1,0:T(8,128)(2,1)S(1)}, u32[]{:S(2)}, u32[]{:S(2)}) collective-permute-start(bf16[400,256]{1,0:T(8,128)(2,1)S(1)} %join.1.refs_4_), channel_id=1, source_target_pairs={{0,6},{2,4},{4,2},{6,0},{8,14},{10,12},{12,10},{14,8},{16,22},{18,... | collective-permute-start | bytes 614408 | tf_op jit(solution)/shard_map/ppermute | solution.py:515
  48.5 7.9 %collective-permute-start.19 = (bf16[96,1024]{1,0:T(8,128)(2,1)S(1)}, bf16[96,1024]{1,0:T(8,128)(2,1)S(1)}, u32[]{:S(2)}, u32[]{:S(2)}) collective-permute-start(bf16[96,1024]{1,0:T(8,128)(2,1)S(1)} %get-tuple-element.57), channel_id=1, source_target_pairs={{0,8},{2,10},{4,12},{6,14},{8,0},{10,2},{12,4},{14,6},{16,24},{18,... | collective-permute-start | bytes 589832 | tf_op jit(solution)/shard_map/ppermute | solution.py:515
  48.6 0.9 copy-start.5
  49.5 0.9 copy-start.7
  50.4 4.5 %copy-start = (bf16[1024,1024]{1,0:T(8,128)(2,1)S(1)}, bf16[1024,1024]{1,0:T(8,128)(2,1)}, u32[]{:S(2)}) copy-start(bf16[1024,1024]{1,0:T(8,128)(2,1)} %refs_0_.1) | copy-start | bytes 6291460
  53.2 11.7 %collective-permute-start.18 = (bf16[96,1024]{1,0:T(8,128)(2,1)S(1)}, bf16[96,1024]{1,0:T(8,128)(2,1)S(1)}, u32[]{:S(2)}, u32[]{:S(2)}) collective-permute-start(bf16[96,1024]{1,0:T(8,128)(2,1)S(1)} %collective-permute-done.17.refs_8_), channel_id=1, source_target_pairs={{0,1},{1,0},{2,3},{3,2},{4,5},{5,4},{6,7},{7,6},{8,9},{9,8},{10,11... | collective-permute-start | bytes 589832 | tf_op jit(solution)/shard_map/ppermute | solution.py:521
  54.9 2.9 %copy-start.4 = (bf16[128,1024]{1,0:T(8,128)(2,1)S(1)}, bf16[128,1024]{1,0:T(8,128)(2,1)}, u32[]{:S(2)}) copy-start(bf16[128,1024]{1,0:T(8,128)(2,1)} %hidden_ref.1) | copy-start | bytes 786436
  54.9 2.9 %copy-start.6 = (f32[1024]{0:T(1024)S(1)}, f32[1024]{0:T(1024)}, u32[]{:S(2)}) copy-start(f32[1024]{0:T(1024)} %param.16) | copy-start | bytes 12292
  56.3 12.5 %copy-start.2 = (bf16[1,1024,384]{2,1,0:T(8,128)(2,1)S(1)}, bf16[1,1024,384]{2,1,0:T(8,128)(2,1)}, u32[]{:S(2)}) copy-start(bf16[1,1024,384]{2,1,0:T(8,128)(2,1)} %gate_ref.1) | copy-start | bytes 2359300
  56.3 12.5 %copy-start.3 = (bf16[1,1024,384]{2,1,0:T(8,128)(2,1)S(1)}, bf16[1,1024,384]{2,1,0:T(8,128)(2,1)}, u32[]{:S(2)}) copy-start(bf16[1,1024,384]{2,1,0:T(8,128)(2,1)} %up_ref.1) | copy-start | bytes 2359300
  56.4 1.4 %collective-permute-start.9 = (bf16[64,1024]{1,0:T(8,128)(2,1)S(1)}, bf16[64,1024]{1,0:T(8,128)(2,1)S(1)}, u32[]{:S(2)}, u32[]{:S(2)}) collective-permute-start(bf16[64,1024]{1,0:T(8,128)(2,1)S(1)} %get-tuple-element.41), channel_id=1, source_target_pairs={{0,1},{1,0},{2,3},{3,2},{4,5},{5,4},{6,7},{7,6},{8,9},{9,8},{10,11... | collective-permute-start | bytes 393224 | tf_op jit(solution)/shard_map/ppermute | solution.py:521
  56.4 15.3 %collective-permute-start.20 = (bf16[96,1024]{1,0:T(8,128)(2,1)S(1)}, bf16[96,1024]{1,0:T(8,128)(2,1)S(1)}, u32[]{:S(2)}, u32[]{:S(2)}) collective-permute-start(bf16[96,1024]{1,0:T(8,128)(2,1)S(1)} %collective-permute-done.19.refs_10_), channel_id=1, source_target_pairs={{0,1},{1,0},{2,3},{3,2},{4,5},{5,4},{6,7},{7,6},{8,9},{9,8},{10,11... | collective-permute-start | bytes 589832 | tf_op jit(solution)/shard_map/ppermute | solution.py:521
  58.5 12.8 %collective-permute-start.13 = (bf16[64,1024]{1,0:T(8,128)(2,1)S(1)}, bf16[64,1024]{1,0:T(8,128)(2,1)S(1)}, u32[]{:S(2)}, u32[]{:S(2)}) collective-permute-start(bf16[64,1024]{1,0:T(8,128)(2,1)S(1)} %get-tuple-element.43.refs_0_), channel_id=1, source_target_pairs={{0,16},{2,18},{4,20},{6,22},{8,24},{10,26},{12,28},{14,30},{16,0},... | collective-permute-start | bytes 393224 | tf_op jit(solution)/shard_map/ppermute | solution.py:515
  64.4 7.9 %collective-permute-start.10 = (bf16[64,1024]{1,0:T(8,128)(2,1)S(1)}, bf16[64,1024]{1,0:T(8,128)(2,1)S(1)}, u32[]{:S(2)}, u32[]{:S(2)}) collective-permute-start(bf16[64,1024]{1,0:T(8,128)(2,1)S(1)} %get-tuple-element.43.refs_0_), channel_id=1, source_target_pairs={{0,2},{2,0},{4,6},{6,4},{8,10},{10,8},{12,14},{14,12},{16,18},{18,... | collective-permute-start | bytes 393224 | tf_op jit(solution)/shard_map/ppermute | solution.py:515
  64.9 9.8 %collective-permute-start.11 = (bf16[64,1024]{1,0:T(8,128)(2,1)S(1)}, bf16[64,1024]{1,0:T(8,128)(2,1)S(1)}, u32[]{:S(2)}, u32[]{:S(2)}) collective-permute-start(bf16[64,1024]{1,0:T(8,128)(2,1)S(1)} %get-tuple-element.43.refs_0_), channel_id=1, source_target_pairs={{0,4},{2,6},{4,0},{6,2},{8,12},{10,14},{12,8},{14,10},{16,20},{18,... | collective-permute-start | bytes 393224 | tf_op jit(solution)/shard_map/ppermute | solution.py:515
  65.4 9.3 %collective-permute-start.12 = (bf16[64,1024]{1,0:T(8,128)(2,1)S(1)}, bf16[64,1024]{1,0:T(8,128)(2,1)S(1)}, u32[]{:S(2)}, u32[]{:S(2)}) collective-permute-start(bf16[64,1024]{1,0:T(8,128)(2,1)S(1)} %get-tuple-element.43.refs_0_), channel_id=1, source_target_pairs={{0,6},{2,4},{4,2},{6,0},{8,14},{10,12},{12,10},{14,8},{16,22},{18,... | collective-permute-start | bytes 393224 | tf_op jit(solution)/shard_map/ppermute | solution.py:515
  71.2 7.1 %collective-permute-start.24 = (bf16[64,1024]{1,0:T(8,128)(2,1)S(1)}, bf16[64,1024]{1,0:T(8,128)(2,1)S(1)}, u32[]{:S(2)}, u32[]{:S(2)}) collective-permute-start(bf16[64,1024]{1,0:T(8,128)(2,1)S(1)} %collective-permute-done.13.refs_4_), channel_id=1, source_target_pairs={{0,2},{2,0},{4,6},{6,4},{8,10},{10,8},{12,14},{14,12},{16,18},{18,... | collective-permute-start | bytes 393224 | tf_op jit(solution)/shard_map/ppermute | solution.py:515
  71.8 7.8 %collective-permute-start.25 = (bf16[64,1024]{1,0:T(8,128)(2,1)S(1)}, bf16[64,1024]{1,0:T(8,128)(2,1)S(1)}, u32[]{:S(2)}, u32[]{:S(2)}) collective-permute-start(bf16[64,1024]{1,0:T(8,128)(2,1)S(1)} %collective-permute-done.13.refs_4_), channel_id=1, source_target_pairs={{0,4},{2,6},{4,0},{6,2},{8,12},{10,14},{12,8},{14,10},{16,20},{18,... | collective-permute-start | bytes 393224 | tf_op jit(solution)/shard_map/ppermute | solution.py:515
  72.3 7.2 %collective-permute-start.26 = (bf16[64,1024]{1,0:T(8,128)(2,1)S(1)}, bf16[64,1024]{1,0:T(8,128)(2,1)S(1)}, u32[]{:S(2)}, u32[]{:S(2)}) collective-permute-start(bf16[64,1024]{1,0:T(8,128)(2,1)S(1)} %collective-permute-done.13.refs_4_), channel_id=1, source_target_pairs={{0,6},{2,4},{4,2},{6,0},{8,14},{10,12},{12,10},{14,8},{16,22},{18,... | collective-permute-start | bytes 393224 | tf_op jit(solution)/shard_map/ppermute | solution.py:515
  80.7 6.4 %collective-permute-start.27 = (bf16[64,1024]{1,0:T(8,128)(2,1)S(1)}, bf16[64,1024]{1,0:T(8,128)(2,1)S(1)}, u32[]{:S(2)}, u32[]{:S(2)}) collective-permute-start(bf16[64,1024]{1,0:T(8,128)(2,1)S(1)} %get-tuple-element.52), channel_id=1, source_target_pairs={{0,2},{2,0},{4,6},{6,4},{8,10},{10,8},{12,14},{14,12},{16,18},{18,... | collective-permute-start | bytes 393224 | tf_op jit(solution)/shard_map/ppermute | solution.py:515
  82.3 7.2 %collective-permute-start.28 = (bf16[64,1024]{1,0:T(8,128)(2,1)S(1)}, bf16[64,1024]{1,0:T(8,128)(2,1)S(1)}, u32[]{:S(2)}, u32[]{:S(2)}) collective-permute-start(bf16[64,1024]{1,0:T(8,128)(2,1)S(1)} %get-tuple-element.53), channel_id=1, source_target_pairs={{0,4},{2,6},{4,0},{6,2},{8,12},{10,14},{12,8},{14,10},{16,20},{18,... | collective-permute-start | bytes 393224 | tf_op jit(solution)/shard_map/ppermute | solution.py:515
  82.8 7.9 %collective-permute-start.29 = (bf16[64,1024]{1,0:T(8,128)(2,1)S(1)}, bf16[64,1024]{1,0:T(8,128)(2,1)S(1)}, u32[]{:S(2)}, u32[]{:S(2)}) collective-permute-start(bf16[64,1024]{1,0:T(8,128)(2,1)S(1)} %get-tuple-element.54), channel_id=1, source_target_pairs={{0,6},{2,4},{4,2},{6,0},{8,14},{10,12},{12,10},{14,8},{16,22},{18,... | collective-permute-start | bytes 393224 | tf_op jit(solution)/shard_map/ppermute | solution.py:515
  84.3 7.7 %collective-permute-start.21 = (bf16[64,1024]{1,0:T(8,128)(2,1)S(1)}, bf16[64,1024]{1,0:T(8,128)(2,1)S(1)}, u32[]{:S(2)}, u32[]{:S(2)}) collective-permute-start(bf16[64,1024]{1,0:T(8,128)(2,1)S(1)} %get-tuple-element.47), channel_id=1, source_target_pairs={{0,2},{2,0},{4,6},{6,4},{8,10},{10,8},{12,14},{14,12},{16,18},{18,... | collective-permute-start | bytes 393224 | tf_op jit(solution)/shard_map/ppermute | solution.py:515
  85.8 7.1 %collective-permute-start.22 = (bf16[64,1024]{1,0:T(8,128)(2,1)S(1)}, bf16[64,1024]{1,0:T(8,128)(2,1)S(1)}, u32[]{:S(2)}, u32[]{:S(2)}) collective-permute-start(bf16[64,1024]{1,0:T(8,128)(2,1)S(1)} %get-tuple-element.48), channel_id=1, source_target_pairs={{0,4},{2,6},{4,0},{6,2},{8,12},{10,14},{12,8},{14,10},{16,20},{18,... | collective-permute-start | bytes 393224 | tf_op jit(solution)/shard_map/ppermute | solution.py:515
  87.1 7.1 %collective-permute-start.23 = (bf16[64,1024]{1,0:T(8,128)(2,1)S(1)}, bf16[64,1024]{1,0:T(8,128)(2,1)S(1)}, u32[]{:S(2)}, u32[]{:S(2)}) collective-permute-start(bf16[64,1024]{1,0:T(8,128)(2,1)S(1)} %get-tuple-element.49), channel_id=1, source_target_pairs={{0,6},{2,4},{4,2},{6,0},{8,14},{10,12},{12,10},{14,8},{16,22},{18,... | collective-permute-start | bytes 393224 | tf_op jit(solution)/shard_map/ppermute | solution.py:515
  90.8 7.3 %collective-permute-start.30 = (bf16[64,1024]{1,0:T(8,128)(2,1)S(1)}, bf16[64,1024]{1,0:T(8,128)(2,1)S(1)}, u32[]{:S(2)}, u32[]{:S(2)}) collective-permute-start(bf16[64,1024]{1,0:T(8,128)(2,1)S(1)} %gather_sum.1), channel_id=1, source_target_pairs={{0,16},{2,18},{4,20},{6,22},{8,24},{10,26},{12,28},{14,30},{16,0},... | collective-permute-start | bytes 393224 | tf_op jit(solution)/shard_map/ppermute | solution.py:515
  98.8 1.3 %collective-permute-start.31 = (bf16[64,512]{1,0:T(8,128)(2,1)S(1)}, bf16[64,512]{1,0:T(8,128)(2,1)S(1)}, u32[]{:S(2)}, u32[]{:S(2)}) collective-permute-start(bf16[64,512]{1,0:T(8,128)(2,1)S(1)} %get-tuple-element.56), channel_id=1, source_target_pairs={{0,1},{1,0},{2,3},{3,2},{4,5},{5,4},{6,7},{7,6},{8,9},{9,8},{10,11... | collective-permute-start | bytes 196616 | tf_op jit(solution)/shard_map/ppermute | solution.py:521

commit v3 on v2

--- a/solution.py
+++ b/solution.py
@@ -14,7 +14,6 @@
 HIDE = -1e30
 ROOM = 20 << 20
 GROUP = 512
-FULL = 62 << 20
 
 
 def whole(memory_space=pltpu.VMEM):
@@ -33,6 +32,10 @@
     for copy in copies:
         copy.start()
     return copies
+
+
+def held(value):
+    return pltpu.with_memory_space_constraint(value, pltpu.HBM)
 
 
 def pack_kernel(key_ref, value_ref, ids_ref, score_ref, rows_ref, mixed_ref, both, ids, score, sems):
@@ -79,13 +82,52 @@
             pltpu.SemaphoreType.DMA((4,)),
         ],
         cost_estimate=cost(1e5, 3e5),
-        compiler_params=pltpu.CompilerParams(vmem_limit_bytes=FULL),
+        compiler_params=pltpu.CompilerParams(vmem_limit_bytes=ROOM),
         name="pack",
-    )(key_rows, value_rows, expert_ids.T, gate_scores.T)
-
-
-def stack_kernel(place_ref, gate_ref, up_ref, mine_ref, other_ref, own_wide, swapped_wide, sems):
-    units, core = gate_ref.shape[2], place_ref[1]
+    )(*[held(value) for value in (key_rows, value_rows, expert_ids.T, gate_scores.T)])
+
+
+def cut_kernel(down_ref, out_ref, sem):
+    half = out_ref.shape[0]
+    start = pl.multiple_of(lax.axis_index("exp") * half, half)
+    copy = pltpu.make_async_copy(down_ref.at[0, pl.ds(start, half)], out_ref, sem)
+    copy.start()
+    copy.wait()
+
+
+def cut(w_down):
+    _, units, model = w_down.shape
+    return pl.pallas_call(
+        cut_kernel,
+        out_shape=jax.ShapeDtypeStruct((units // 2, model), w_down.dtype),
+        in_specs=[whole(pl.ANY)],
+        out_specs=whole(),
+        scratch_shapes=[pltpu.SemaphoreType.DMA],
+        cost_estimate=cost(1e3, 1e6),
+        compiler_params=pltpu.CompilerParams(vmem_limit_bytes=ROOM),
+        name="cut",
+    )(held(w_down))
+
+
+def merge_kernel(first_ref, second_ref, out_ref):
+    out_ref[...] = first_ref[...] + second_ref[...]
+
+
+def merge(first, second):
+    pair = [pltpu.with_memory_space_constraint(value, pltpu.VMEM) for value in (first, second)]
+    return pl.pallas_call(
+        merge_kernel,
+        out_shape=jax.ShapeDtypeStruct(first.shape, first.dtype),
+        in_specs=[whole()] * 2,
+        out_specs=whole(),
+        cost_estimate=cost(1e5, 3e6),
+        compiler_params=pltpu.CompilerParams(vmem_limit_bytes=ROOM),
+        name="merge",
+    )(*pair)
+
+
+def stack_kernel(gate_ref, up_ref, mine_ref, other_ref, own_wide, swapped_wide, sems):
+    units, core = gate_ref.shape[2], lax.axis_index("exp")
     mine = pl.ds(pl.multiple_of(core * units, units), units)
     other = pl.ds(pl.multiple_of((1 - core) * units, units), units)
     pairs = [
@@ -98,18 +140,18 @@
         copy.wait()
 
 
-def stack(place, w_gate, w_up, mine, other):
+def stack(w_gate, w_up, mine, other):
     _, model, units = w_gate.shape
     return pl.pallas_call(
         stack_kernel,
         out_shape=(jax.ShapeDtypeStruct((model, 2 * units), jnp.bfloat16),) * 2,
-        in_specs=[whole(pltpu.SMEM)] + [whole(pl.ANY)] * 4,
+        in_specs=[whole(pl.ANY)] * 4,
         out_specs=(whole(),) * 2,
         scratch_shapes=[pltpu.SemaphoreType.DMA((4,))],
         cost_estimate=cost(1e5, 6e6),
         compiler_params=pltpu.CompilerParams(vmem_limit_bytes=ROOM),
         name="stack",
-    )(place, w_gate, w_up, mine, other)
+    )(w_gate, w_up, mine, other)
 
 
 def join_kernel(count, *refs):
@@ -162,22 +204,17 @@
     return peak, total, product
 
 
-def near_kernel(plane, place_ref, query_ref, *refs):
+def near_kernel(plane, heads_ref, *refs):
     sources, column_ref = refs[:plane], refs[plane]
-    heads_ref, peak_ref, total_ref, sum_ref, keys, values, sems = refs[plane + 1 :]
-    count = query_ref.shape[0]
-    pairs = []
-    for head in range(query_ref.shape[1] // HEAD):
-        part = slice(head * count, (head + 1) * count)
-        pairs.append((query_ref.at[:, head * HEAD : (head + 1) * HEAD], heads_ref.at[part]))
-    copies = fetch_all(pairs, sems)
+    peak_ref, total_ref, sum_ref, keys, values = refs[plane + 1 :]
+    count = HEAD
     layers = column_ref.shape[0] // count
     for n, ref in enumerate(sources):
         keys[n * count : (n + 1) * count, :] = ref[:count, :HEAD]
         values[n * count : (n + 1) * count, :] = ref[:count, HEAD:]
     keys[plane * count :, :] = column_ref[: layers * count, :HEAD]
     values[plane * count :, :] = column_ref[: layers * count, HEAD:]
-    me = place_ref[0]
+    me = lax.axis_index("ctx")
     row = lax.broadcasted_iota(jnp.int32, (GROUP, count), 0) % count
     number = lax.broadcasted_iota(jnp.int32, (GROUP, count), 1)
     biases = [jnp.where(number <= row, 0.0, HIDE)]
@@ -185,8 +222,6 @@
         biases.append(jnp.where((me ^ step) < me, 0.0, HIDE))
     for step in range(1, layers + 1):
         biases.append(jnp.where(me >= step * plane, 0.0, HIDE))
-    for copy in copies:
-        copy.wait()
     for start in range(0, heads_ref.shape[0], GROUP):
         part = slice(start, start + GROUP)
         peak, total, product = soften(heads_ref[part], keys[...], values[...], biases, None)
@@ -195,28 +230,49 @@
         sum_ref[part] = product
 
 
-def near(place, queries, sources, column, plane):
+def turn_kernel(query_ref, heads_ref, sems):
+    count = query_ref.shape[0]
+    pairs = []
+    for head in range(query_ref.shape[1] // HEAD):
+        part = slice(head * count, (head + 1) * count)
+        pairs.append((query_ref.at[:, head * HEAD : (head + 1) * HEAD], heads_ref.at[part]))
+    for copy in fetch_all(pairs, sems):
+        copy.wait()
+
+
+def turn(queries):
     count, width = queries.shape
-    rows = count * width // HEAD
-    shape = jax.ShapeDtypeStruct((rows, HEAD), jnp.float32)
+    return pl.pallas_call(
+        turn_kernel,
+        out_shape=jax.ShapeDtypeStruct((count * width // HEAD, HEAD), queries.dtype),
+        in_specs=[whole(pl.ANY)],
+        out_specs=whole(),
+        scratch_shapes=[pltpu.SemaphoreType.DMA((width // HEAD,))],
+        cost_estimate=cost(1e5, 1e6),
+        compiler_params=pltpu.CompilerParams(vmem_limit_bytes=ROOM),
+        name="turn",
+    )(held(queries))
+
+
+def near(heads, sources, column, plane):
+    shape = jax.ShapeDtypeStruct(heads.shape, jnp.float32)
     keys = (plane + column.shape[0] // HEAD) * HEAD
     return pl.pallas_call(
         functools.partial(near_kernel, plane),
-        out_shape=(jax.ShapeDtypeStruct((rows, HEAD), jnp.bfloat16),) + (shape,) * 3,
-        in_specs=[whole(pltpu.SMEM), whole(pl.ANY)] + [whole()] * (1 + len(sources)),
-        out_specs=(whole(),) * 4,
-        scratch_shapes=[pltpu.VMEM((keys, HEAD), jnp.bfloat16)] * 2
-        + [pltpu.SemaphoreType.DMA((width // HEAD,))],
-        cost_estimate=cost(4 * rows * HEAD * keys, 4e6, rows * keys),
+        out_shape=(shape,) * 3,
+        in_specs=[whole()] * (2 + len(sources)),
+        out_specs=(whole(),) * 3,
+        scratch_shapes=[pltpu.VMEM((keys, HEAD), jnp.bfloat16)] * 2,
+        cost_estimate=cost(4 * heads.size * keys, 4e6, heads.shape[0] * keys),
         compiler_params=pltpu.CompilerParams(vmem_limit_bytes=ROOM),
         name="near",
-    )(place, queries, *sources, column)
-
-
-def extend(plane, place_ref, query_ref, state, sources, keys, values, out):
+    )(heads, *sources, column)
+
+
+def extend(plane, query_ref, state, sources, keys, values, out):
     count = HEAD
     layers = sources[0].shape[0] // count
-    height = place_ref[0] // plane
+    height = lax.axis_index("ctx") // plane
 
     @pl.when(height == 0)
     def _():
@@ -246,32 +302,32 @@
                 out[2][part] = product
 
 
-def more_kernel(plane, steps, place_ref, query_ref, *refs):
+def more_kernel(plane, steps, query_ref, *refs):
     state, sources, refs = refs[:3], refs[3 : 3 + steps], refs[3 + steps :]
-    extend(plane, place_ref, query_ref, state, sources, refs[3], refs[4], refs[:3])
-
-
-def more(place, heads, state, sources, plane):
+    extend(plane, query_ref, state, sources, refs[3], refs[4], refs[:3])
+
+
+def more(heads, state, sources, plane):
     shape = jax.ShapeDtypeStruct(heads.shape, jnp.float32)
     keys = len(sources) * (sources[0].shape[0] // HEAD) * HEAD
     return pl.pallas_call(
         functools.partial(more_kernel, plane, len(sources)),
         out_shape=(shape,) * 3,
-        in_specs=[whole(pltpu.SMEM)] + [whole()] * (4 + len(sources)),
+        in_specs=[whole()] * (4 + len(sources)),
         out_specs=(whole(),) * 3,
         scratch_shapes=[pltpu.VMEM((keys, HEAD), jnp.bfloat16)] * 2,
         cost_estimate=cost(4 * heads.size * keys, 4e6, heads.shape[0] * keys),
         compiler_params=pltpu.CompilerParams(vmem_limit_bytes=ROOM),
         name="more",
-    )(place, heads, *state, *sources)
-
-
-def far_kernel(plane, place_ref, query_ref, peak_ref, total_ref, sum_ref, source_ref, *refs):
+    )(heads, *state, *sources)
+
+
+def far_kernel(plane, query_ref, peak_ref, total_ref, sum_ref, source_ref, *refs):
     weight_ref, own_ref, other_ref, keys, values, peak, total, product, attended, result = refs
     state, work = (peak_ref, total_ref, sum_ref), (peak, total, product)
-    extend(plane, place_ref, query_ref, state, (source_ref,), keys, values, work)
+    extend(plane, query_ref, state, (source_ref,), keys, values, work)
     count = attended.shape[0]
-    core = place_ref[1]
+    core = lax.axis_index("exp")
     for head in range(query_ref.shape[0] // count):
         part = slice(head * count, (head + 1) * count)
         denom = jnp.sum(total[part], axis=1, keepdims=True)
@@ -283,7 +339,7 @@
     other_ref[...] = other.astype(jnp.bfloat16)
 
 
-def far(place, heads, state, source, out_proj, plane):
+def far(heads, state, source, out_proj, plane):
     width, model = out_proj.shape
     count = heads.size // width
     keys = source.shape[0] // HEAD * HEAD
@@ -293,7 +349,7 @@
             jax.ShapeDtypeStruct((count // 2, model), jnp.float32),
             jax.ShapeDtypeStruct((count // 2, model), jnp.bfloat16),
         ),
-        in_specs=[whole(pltpu.SMEM)] + [whole()] * 6,
+        in_specs=[whole()] * 6,
         out_specs=(whole(),) * 2,
         scratch_shapes=[pltpu.VMEM((keys, HEAD), jnp.bfloat16)] * 2
         + [pltpu.VMEM(heads.shape, jnp.float32)] * 3
@@ -306,12 +362,12 @@
         ),
         compiler_params=pltpu.CompilerParams(vmem_limit_bytes=ROOM),
         name="far",
-    )(place, heads, *state, source, out_proj)
-
-
-def norm_kernel(place_ref, hidden_ref, own_ref, other_ref, gain_ref, resid_ref, normed_ref):
+    )(heads, *state, source, out_proj)
+
+
+def norm_kernel(hidden_ref, own_ref, other_ref, gain_ref, resid_ref, normed_ref):
     half = own_ref.shape[0]
-    start = pl.multiple_of(place_ref[1] * half, half)
+    start = pl.multiple_of(lax.axis_index("exp") * half, half)
     hidden = hidden_ref[pl.ds(start, half), :].astype(jnp.float32)
     resid = hidden + own_ref[...] + other_ref[...].astype(jnp.float32)
     inverse = lax.rsqrt(jnp.mean(resid * resid, axis=1, keepdims=True) + 1e-06)
@@ -319,26 +375,27 @@
     normed_ref[...] = (resid * inverse * gain_ref[...]).astype(jnp.bfloat16)
 
 
-def norm(place, hidden_in, own, other, norm_gain):
+def norm(hidden_in, own, other, norm_gain):
     return pl.pallas_call(
         norm_kernel,
         out_shape=(
             jax.ShapeDtypeStruct(own.shape, jnp.float32),
             jax.ShapeDtypeStruct(own.shape, jnp.bfloat16),
         ),
-        in_specs=[whole(pltpu.SMEM)] + [whole()] * 4,
+        in_specs=[whole()] * 4,
         out_specs=(whole(),) * 2,
         cost_estimate=cost(1e6, 1e6),
         compiler_params=pltpu.CompilerParams(vmem_limit_bytes=ROOM),
         name="norm",
-    )(place, hidden_in, own, other, norm_gain)
-
-
-def share_kernel(place_ref, *refs):
+    )(hidden_in, own, other, norm_gain)
+
+
+def share_kernel(plane, *refs):
     pieces, out_ref, turned = refs[:-2], refs[-2], refs[-1]
+    me = lax.axis_index("ctx")
     experts, count = pieces[0].shape[0], pieces[0].shape[1] // 2
     half = count // 2
-    start = pl.multiple_of(place_ref[1] * half, half)
+    start = pl.multiple_of(lax.axis_index("exp") * half, half)
     number = lax.broadcasted_iota(jnp.int32, (experts, count), 0)
     lane = lax.broadcasted_iota(jnp.int32, (count, count), 1)
     diagonal = lax.broadcasted_iota(jnp.int32, (count, count), 0) == lane
@@ -347,7 +404,7 @@
         columns = jnp.zeros((count, count), jnp.float32)
         for side in range(2):
             line = jnp.sum(
-                jnp.where(number == place_ref[2 + side], mix, 0.0), axis=0, keepdims=True
+                jnp.where(number == (me if side == 0 else me ^ plane), mix, 0.0), axis=0, keepdims=True
             )
             column = jnp.sum(jnp.where(diagonal, line, 0.0), axis=1, keepdims=True)
             columns = jnp.where(lane == side, column, columns)
@@ -355,7 +412,7 @@
         out_ref[n * half : (n + 1) * half, :] = turned[pl.ds(start, half), :]
 
 
-def share(place, pieces, experts):
+def share(pieces, experts, plane):
     width = pieces[0].shape[1]
     count = width // 2
     specs = []
@@ -364,16 +421,16 @@
         specs.append(pl.BlockSpec((experts, width), lambda i, block=block: (block, 0)))
     rows = len(pieces) * count // 2
     return pl.pallas_call(
-        share_kernel,
+        functools.partial(share_kernel, plane),
         grid=(1,),
         out_shape=jax.ShapeDtypeStruct((rows, count), jnp.float32),
-        in_specs=[whole(pltpu.SMEM)] + specs,
+        in_specs=specs,
         out_specs=pl.BlockSpec((rows, count), lambda i: (0, 0)),
         scratch_shapes=[pltpu.VMEM((count, count), jnp.float32)],
         cost_estimate=cost(1e6, 4e5),
         compiler_params=pltpu.CompilerParams(vmem_limit_bytes=ROOM),
         name="columns",
-    )(place, *pieces)
+    )(*pieces)
 
 
 def expert_rows(share_ref, first, inputs, wide_refs, rows, hidden):
@@ -396,22 +453,58 @@
         ref[...] = total[n * size : (n + 1) * size, :].astype(ref.dtype)
 
 
-def expert_near_kernel(blocks, place_ref, share_ref, *refs):
-    inputs, wide_refs, refs = refs[:blocks], refs[blocks : blocks + 2], refs[blocks + 2 :]
-    down_ref, pieces = refs[0], refs[1:5]
-    outputs, tall_ref, rows, hidden, sems = refs[5 : 5 + blocks], *refs[5 + blocks :]
-    units, core = down_ref.shape[1], place_ref[1]
-    size = pieces[0].shape[0]
-    pairs = [(down_ref.at[0], tall_ref.at[:units])]
-    for n, position in enumerate((core, 1 - core)):
-        for part, ref in enumerate(pieces[n::2]):
-            start = units + position * (units // 2) + part * size
-            pairs.append((ref, tall_ref.at[pl.ds(pl.multiple_of(start, size), size)]))
-    copies = fetch_all(pairs, sems)
+def expand_kernel(share_ref, *refs):
+    inputs, wide_refs, hidden, rows = refs[:-4], refs[-4:-2], refs[-2], refs[-1]
     expert_rows(share_ref, 0, inputs, wide_refs, rows, hidden)
-    for copy in copies:
+
+
+def expand(shares, inputs, wide):
+    blocks = len(inputs)
+    size, model = inputs[0].shape
+    both = wide[0].shape[1]
+    return pl.pallas_call(
+        expand_kernel,
+        out_shape=jax.ShapeDtypeStruct((blocks * size, both), jnp.bfloat16),
+        in_specs=[whole()] * (3 + blocks),
+        out_specs=whole(),
+        scratch_shapes=[pltpu.VMEM((blocks * size, model), jnp.bfloat16)],
+        cost_estimate=cost(4 * blocks * size * model * both, 4 * model * both),
+        compiler_params=pltpu.CompilerParams(vmem_limit_bytes=ROOM),
+        name="expand",
+    )(shares, *inputs, *wide)
+
+
+def contract_kernel(hidden_ref, down_ref, mine_ref, other_ref, *refs):
+    outputs, tall_ref, sems = refs[:-2], refs[-2], refs[-1]
+    units, core = down_ref.shape[1], lax.axis_index("exp")
+    half = units // 2
+    mine = pl.ds(pl.multiple_of(units + core * half, half), half)
+    other = pl.ds(pl.multiple_of(units + (1 - core) * half, half), half)
+    pairs = [
+        (down_ref.at[0], tall_ref.at[:units]),
+        (mine_ref, tall_ref.at[mine]),
+        (other_ref, tall_ref.at[other]),
+    ]
+    for copy in fetch_all(pairs, sems):
         copy.wait()
-    expert_sums(hidden, tall_ref, outputs)
+    expert_sums(hidden_ref, tall_ref, outputs)
+
+
+def contract(hidden, w_down, mine, other, dtypes):
+    blocks = len(dtypes)
+    size, model = hidden.shape[0] // blocks, w_down.shape[2]
+    both = hidden.shape[1]
+    return pl.pallas_call(
+        contract_kernel,
+        out_shape=tuple(jax.ShapeDtypeStruct((size, model), dtype) for dtype in dtypes)
+        + (jax.ShapeDtypeStruct((both, model), jnp.bfloat16),),
+        in_specs=[whole()] + [whole(pl.ANY)] * 3,
+        out_specs=(whole(),) * (blocks + 1),
+        scratch_shapes=[pltpu.SemaphoreType.DMA((3,))],
+        cost_estimate=cost(2 * blocks * size * model * both, 2 * model * both),
+        compiler_params=pltpu.CompilerParams(vmem_limit_bytes=ROOM),
+        name="contract",
+    )(hidden, w_down, mine, other)
 
 
 def expert_far_kernel(first, blocks, share_ref, *refs):
@@ -419,27 +512,6 @@
     outputs, rows, hidden = refs[blocks + 3 : -2], refs[-2], refs[-1]
     expert_rows(share_ref, first, inputs, wide_refs, rows, hidden)
     expert_sums(hidden, tall_ref, outputs)
-
-
-def experts_near(place, shares, inputs, wide, w_down, pieces, dtypes):
-    blocks = len(inputs)
-    size, model = inputs[0].shape
-    both = 2 * w_down.shape[1]
-    return pl.pallas_call(
-        functools.partial(expert_near_kernel, blocks),
-        out_shape=tuple(jax.ShapeDtypeStruct((size, model), dtype) for dtype in dtypes)
-        + (jax.ShapeDtypeStruct((both, model), jnp.bfloat16),),
-        in_specs=[whole(pltpu.SMEM)] + [whole()] * (3 + blocks) + [whole(pl.ANY)] * 5,
-        out_specs=(whole(),) * (blocks + 1),
-        scratch_shapes=[
-            pltpu.VMEM((blocks * size, model), jnp.bfloat16),
-            pltpu.VMEM((blocks * size, both), jnp.bfloat16),
-            pltpu.SemaphoreType.DMA((5,)),
-        ],
-        cost_estimate=cost(6 * blocks * size * model * both, 6 * model * both),
-        compiler_params=pltpu.CompilerParams(vmem_limit_bytes=ROOM),
-        name="experts_near",
-    )(place, shares, *inputs, *wide, w_down, *pieces)
 
 
 def experts_far(shares, inputs, wide, tall, first):
@@ -461,31 +533,31 @@
     )(shares, *inputs, *wide, tall)
 
 
-def final_kernel(place_ref, resid_ref, own_ref, *refs):
+def final_kernel(resid_ref, own_ref, *refs):
     keep_ref, send_ref, work = refs[-3:]
     total = own_ref[...]
     for ref in refs[:-3]:
         total = total + ref[...].astype(jnp.float32)
     work[...] = (resid_ref[...] + total).astype(jnp.bfloat16)
     half = keep_ref.shape[1]
-    core = place_ref[1]
+    core = lax.axis_index("exp")
     keep_ref[...] = work[:, pl.ds(pl.multiple_of(core * half, half), half)]
     send_ref[...] = work[:, pl.ds(pl.multiple_of((1 - core) * half, half), half)]
 
 
-def final(place, resid, own, received):
+def final(resid, own, received):
     rows, model = resid.shape
     shape = jax.ShapeDtypeStruct((rows, model // 2), jnp.bfloat16)
     return pl.pallas_call(
         final_kernel,
         out_shape=(shape, shape),
-        in_specs=[whole(pltpu.SMEM)] + [whole()] * (2 + len(received)),
+        in_specs=[whole()] * (2 + len(received)),
         out_specs=(whole(),) * 2,
         scratch_shapes=[pltpu.VMEM((rows, model), jnp.bfloat16)],
         cost_estimate=cost(1e6, 1e6),
         compiler_params=pltpu.CompilerParams(vmem_limit_bytes=ROOM),
         name="final",
-    )(place, resid, own, *received)
+    )(resid, own, *received)
 
 
 def compact(
@@ -507,9 +579,7 @@
     plane = math.isqrt(ctx)
     planes = ctx // plane
     away = 2 * plane
-    me = lax.axis_index("ctx")
-    core = lax.axis_index("exp")
-    place = jnp.stack([me, core, me, me ^ plane]).astype(jnp.int32)
+
 
     def flip(value, mask):
         return lax.ppermute(value, "ctx", [(i, i ^ mask) for i in range(ctx)])
@@ -532,44 +602,38 @@
     joined = join(column, count)
     corner = [flip(joined, mate) for mate in mates]
 
-    units = w_gate.shape[2]
-    quarter = units // 4
-
     def half_flip(value, side):
         pairs = [(2 * i + side, 2 * (i ^ plane) + side) for i in range(ctx)]
         return lax.ppermute(value, ("ctx", "exp"), pairs)
 
     gate_swap = half_flip(w_gate[0], 0)
     up_swap = half_flip(w_up[0], 1)
-    tall_swap = []
-    for part in range(2):
-        start = core * 2 * quarter + part * quarter
-        piece = lax.dynamic_slice_in_dim(w_down[0], start, quarter, 0)
-        tall_swap.append(flip(piece, plane))
-
-    heads, *state = near(place, queries, [mixed] + level, joined, plane)
-    state = more(place, heads, state, corner[:-1], plane)
-    own, other = far(place, heads, state, corner[-1], out_proj, plane)
-    resid, normed = norm(place, hidden_in, own, across(other), norm_gain.reshape(1, model))
-    wide_swap = gate_swap + up_swap
-    wide = stack(place, w_gate, w_up, wide_swap, across(wide_swap))
-    pieces = [value for piece in tall_swap for value in (piece, across(piece))]
-
-    shares = share(place, [mixed] + level + [joined] + corner, w_gate.shape[0] * ctx)
+    tall = cut(w_down)
+    tall_swap = flip(tall, plane)
+
+    heads = turn(queries)
+    state = near(heads, [mixed] + level, joined, plane)
+    state = more(heads, state, corner[:-1], plane)
+    own, other = far(heads, state, corner[-1], out_proj, plane)
+    resid, normed = norm(hidden_in, own, across(other), norm_gain.reshape(1, model))
+    wide_swap = merge(gate_swap, up_swap)
+    wide = stack(w_gate, w_up, wide_swap, across(wide_swap))
+    shares = share([mixed] + level + [joined] + corner, w_gate.shape[0] * ctx, plane)
     opposite = flip(normed, away)
     level_rows = [flip(normed, mate) for mate in mates]
     corner_rows = [flip(opposite, mate) for mate in mates]
     f32, bf16 = jnp.float32, jnp.bfloat16
-    *near_out, tall = experts_near(
-        place, shares, [normed] + level_rows + [opposite], wide, w_down, pieces,
+    hidden = expand(shares, [normed] + level_rows + [opposite], wide)
+    *near_out, tall = contract(
+        hidden, w_down, tall_swap, across(tall_swap),
         [f32] + [bf16] * len(mates) + [f32],
     )
     far_out = experts_far(shares, corner_rows, wide, tall, plane + 1)
     passed = [flip(value, mate) for value, mate in zip(far_out, mates)]
     direct = [flip(value, mate) for value, mate in zip(near_out[1:plane], mates)]
     last = flip(gather_sum(near_out[plane], passed), away)
-    keep, send = final(place, resid, near_out[0], direct + [last])
-    return assemble(place, keep, across(send))
+    keep, send = final(resid, near_out[0], direct + [last])
+    return assemble(keep, across(send))
 
 
 def gather_sum_kernel(own_ref, *refs):
@@ -591,23 +655,23 @@
     )(own, *received)
 
 
-def assemble_kernel(place_ref, keep_ref, received_ref, out_ref):
+def assemble_kernel(keep_ref, received_ref, out_ref):
     half = keep_ref.shape[0]
-    core = place_ref[1]
+    core = lax.axis_index("exp")
     out_ref[pl.ds(pl.multiple_of(core * half, half), half), :] = keep_ref[...]
     out_ref[pl.ds(pl.multiple_of((1 - core) * half, half), half), :] = received_ref[...]
 
 
-def assemble(place, keep, received):
+def assemble(keep, received):
     return pl.pallas_call(
         assemble_kernel,
         out_shape=jax.ShapeDtypeStruct((2 * keep.shape[0], keep.shape[1]), keep.dtype),
-        in_specs=[whole(pltpu.SMEM)] + [whole()] * 2,
+        in_specs=[whole()] * 2,
         out_specs=whole(),
         cost_estimate=cost(1e5, 3e5),
         compiler_params=pltpu.CompilerParams(vmem_limit_bytes=ROOM),
         name="assemble",
-    )(place, keep, received)
+    )(keep, received)
 
 
 def fits_compact(queries, key_rows, expert_ids, w_gate):

time: 102 us -> 96.8 us (0.949)
  Pallas kernels: 16.5 us -> 11.1 us
  starting transfers between devices: 43 us -> 47.2 us
  local copies, waits for them, and re-layouts: 2.58 us -> 0.04 us
    ppermute x23 -> x22, waiting for transfers between devices: 17.6 us -> 20.7 us  [flip(): return lax.ppermute(value, 'ctx', [(i, i ^ mask) for i in range(ctx)])]
    ppermute x2, waiting for transfers between devices: 17.7 us -> 15 us  [half_flip(): return lax.ppermute(value, ('ctx', 'exp'), pairs)]
    ppermute x2, starting transfers between devices: 5.67 us -> 8 us  [upward(): lax.ppermute(value, 'ctx', [(i, i + step) for i in range(ctx - step)])]
    ppermute x23 -> x22, starting transfers between devices: 30.7 us -> 32.8 us  [flip(): return lax.ppermute(value, 'ctx', [(i, i ^ mask) for i in range(ctx)])]
    unnamed x16 -> x12, local copies, waits for them, and re-layouts: 1.87 us -> 0.04 us
    pallas_call x1, Pallas kernels: 1.96 us -> 0.37 us  [stack(): pl.pallas_call(stack_kernel, out_shape=(jax.ShapeDtypeStruct((model, 2 *...]
    ppermute x2, waiting for transfers between devices: 1.18 us -> 0.01 us  [upward(): lax.ppermute(value, 'ctx', [(i, i + step) for i in range(ctx - step)])]
    pallas_call x4 -> x8, Pallas kernels: 7.87 us -> 6.88 us  [the longest x1 1.99 us: near(): pl.pallas_call(functools.partial(near_kernel, plane), out_shape=(shape,)...]
  transfers between devices with their start and end apart: 32 -> 30, of which waited for: 16 -> 13; matrix products, arithmetic and copies ran while one was open for 1% -> 0% of each run, Pallas kernels for 13% -> 10%
where the time goes in v3:
time: 96.8 us; the launch traced here: 96.5 us
  starting transfers between devices  47.2 us (49%)
  waiting for transfers between devices  37.7 us (39%)
  Pallas kernels  11.1 us (11%)
    ppermute x22, starting transfers between devices, flip(): return lax.ppermute(value, 'ctx', [(i, i ^ mask) for i in range(ctx)])  32.8 us
    ppermute x22, waiting for transfers between devices, flip(): return lax.ppermute(value, 'ctx', [(i, i ^ mask) for i in range(ctx)])  20.7 us
    ppermute x2, waiting for transfers between devices, half_flip(): return lax.ppermute(value, ('ctx', 'exp'), pairs)  15 us
    ppermute x2, starting transfers between devices, upward(): lax.ppermute(value, 'ctx', [(i, i + step) for i in range(ctx - step)])  8 us
    ppermute x2, starting transfers between devices, half_flip(): return lax.ppermute(value, ('ctx', 'exp'), pairs)  5.66 us
    ppermute x4, waiting for transfers between devices, across(): return lax.ppermute(value, 'exp', [(0, 1), (1, 0)])  2.08 us
    pallas_call x1, Pallas kernels, near(): pl.pallas_call(functools.partial(near_kernel, plane), out_shape=(shape,)...  1.99 us
  transfers between devices with their start and end apart: 30, of which 13 were waited for; matrix products, arithmetic and copies ran while one was open for 0% of the time, Pallas kernels for 10%

profile of v3, /device:TPU:0, one launch (start us, length us, event | category | flops | bytes accessed | tf_op | source)
XLA Modules:
  0.0 96.5 jit_solution(4004596470726169259)
XLA Ops:
  0.0 5.0 %collective-permute-start.14 = (bf16[1024,384]{1,0:T(8,128)(2,1)}, bf16[1024,384]{1,0:T(8,128)(2,1)S(1)}, u32[]{:S(2)}, u32[]{:S(2)}) collective-permute-start(bf16[1024,384]{1,0:T(8,128)(2,1)} %bitcast.5), channel_id=1, source_target_pairs={{0,8},{2,10},{4,12},{6,14},{8,0},{10,2},{12,4},{14,6},{16,24},{18,... | collective-permute-start | bytes 2359304 | tf_op jit(solution)/shard_map/ppermute | solution.py:607
  5.0 0.7 collective-permute-start.15
  5.7 0.8 pack.1
  6.5 1.9 %collective-permute-start.3 = (bf16[128,256]{1,0:T(8,128)(2,1)S(1)}, bf16[128,256]{1,0:T(8,128)(2,1)S(1)}, u32[]{:S(2)}, u32[]{:S(2)}) collective-permute-start(bf16[128,256]{1,0:T(8,128)(2,1)S(1)} %get-tuple-element.31), channel_id=1, source_target_pairs={{0,8},{2,10},{4,12},{6,14},{8,16},{10,18},{12,20},{14,22},{16,24},... | collective-permute-start | bytes 196616 | tf_op jit(solution)/shard_map/ppermute | solution.py:588
  8.5 15.0 %collective-permute-done.14.first_ref = bf16[1024,384]{1,0:T(8,128)(2,1)S(1)} collective-permute-done((bf16[1024,384]{1,0:T(8,128)(2,1)}, bf16[1024,384]{1,0:T(8,128)(2,1)S(1)}, u32[]{:S(2)}, u32[]{:S(2)}) %collective-permute-start.14) | collective-permute-done | bytes 786464 | tf_op jit(solution)/shard_map/ppermute | solution.py:607
  23.6 6.1 %collective-permute-start.5 = (bf16[128,256]{1,0:T(8,128)(2,1)S(1)}, bf16[128,256]{1,0:T(8,128)(2,1)S(1)}, u32[]{:S(2)}, u32[]{:S(2)}) collective-permute-start(bf16[128,256]{1,0:T(8,128)(2,1)S(1)} %get-tuple-element.31), channel_id=1, source_target_pairs={{0,24},{2,26},{4,28},{6,30},{1,25},{3,27},{5,29},{7,31}} | collective-permute-start | bytes 196616 | tf_op jit(solution)/shard_map/ppermute | solution.py:588
  29.8 1.6 %collective-permute-start = (bf16[144,256]{1,0:T(8,128)(2,1)S(1)}, bf16[144,256]{1,0:T(8,128)(2,1)S(1)}, u32[]{:S(2)}, u32[]{:S(2)}) collective-permute-start(bf16[144,256]{1,0:T(8,128)(2,1)S(1)} %get-tuple-element.30.refs_0_), channel_id=1, source_target_pairs={{0,2},{2,0},{4,6},{6,4},{8,10},{10,8},{12,14},{14,12},{16,18},{18,... | collective-permute-start | bytes 221192 | tf_op jit(solution)/shard_map/ppermute | solution.py:585
  31.3 1.5 %collective-permute-start.1 = (bf16[144,256]{1,0:T(8,128)(2,1)S(1)}, bf16[144,256]{1,0:T(8,128)(2,1)S(1)}, u32[]{:S(2)}, u32[]{:S(2)}) collective-permute-start(bf16[144,256]{1,0:T(8,128)(2,1)S(1)} %get-tuple-element.30.refs_0_), channel_id=1, source_target_pairs={{0,4},{2,6},{4,0},{6,2},{8,12},{10,14},{12,8},{14,10},{16,20},{18,... | collective-permute-start | bytes 221192 | tf_op jit(solution)/shard_map/ppermute | solution.py:585
  32.9 1.8 %collective-permute-start.2 = (bf16[144,256]{1,0:T(8,128)(2,1)S(1)}, bf16[144,256]{1,0:T(8,128)(2,1)S(1)}, u32[]{:S(2)}, u32[]{:S(2)}) collective-permute-start(bf16[144,256]{1,0:T(8,128)(2,1)S(1)} %get-tuple-element.30.refs_0_), channel_id=1, source_target_pairs={{0,6},{2,4},{4,2},{6,0},{8,14},{10,12},{12,10},{14,8},{16,22},{18,... | collective-permute-start | bytes 221192 | tf_op jit(solution)/shard_map/ppermute | solution.py:585
  34.7 1.0 %cut.1 = bf16[192,1024]{1,0:T(8,128)(2,1)S(1)} custom-call(bf16[1,384,1024]{2,1,0:T(8,128)(2,1)} %down_ref.3), custom_call_target="tpu_custom_call" | custom-call | flops 1000 | bytes 1000000 | tf_op jit(solution)/shard_map/cut/pallas_call | solution.py:100
  35.8 0.8 collective-permute-start.6
  36.6 1.5 %collective-permute-start.7 = (bf16[400,256]{1,0:T(8,128)(2,1)S(1)}, bf16[400,256]{1,0:T(8,128)(2,1)S(1)}, u32[]{:S(2)}, u32[]{:S(2)}) collective-permute-start(bf16[400,256]{1,0:T(8,128)(2,1)S(1)} %join.1.refs_4_), channel_id=1, source_target_pairs={{0,4},{2,6},{4,0},{6,2},{8,12},{10,14},{12,8},{14,10},{16,20},{18,... | collective-permute-start | bytes 614408 | tf_op jit(solution)/shard_map/ppermute | solution.py:585
  38.2 2.2 %collective-permute-start.8 = (bf16[400,256]{1,0:T(8,128)(2,1)S(1)}, bf16[400,256]{1,0:T(8,128)(2,1)S(1)}, u32[]{:S(2)}, u32[]{:S(2)}) collective-permute-start(bf16[400,256]{1,0:T(8,128)(2,1)S(1)} %join.1.refs_4_), channel_id=1, source_target_pairs={{0,6},{2,4},{4,2},{6,0},{8,14},{10,12},{12,10},{14,8},{16,22},{18,... | collective-permute-start | bytes 614408 | tf_op jit(solution)/shard_map/ppermute | solution.py:585
  40.3 0.9 turn.1.heads_ref.query_ref
  41.3 2.0 %near.1 = (f32[1024,128]{1,0:T(8,128)S(1)}, f32[1024,128]{1,0:T(8,128)S(1)}, f32[1024,128]{1,0:T(8,128)S(1)}) custom-call(bf16[1024,128]{1,0:T(8,128)(2,1)S(1)} %turn.1.heads_ref.query_ref, bf16[144,256]{1,0:T(8,128)(2,1)S(1)} %get-tuple-element.30.refs_0_, bf16[144,256]{1,0:T(8,128)(2,1)S(1)} %collective-permute-done.refs_1_, ...), custom_call_target="tpu_custom_call" | custom-call | flops 469762048 | bytes 4000000 | tf_op jit(solution)/shard_map/near/pallas_call | solution.py:260
  43.3 0.5 collective-permute-done.6.refs_3_.refs_5_
  43.8 3.3 %collective-permute-done.7.refs_4_.refs_6_ = bf16[400,256]{1,0:T(8,128)(2,1)S(1)} collective-permute-done((bf16[400,256]{1,0:T(8,128)(2,1)S(1)}, bf16[400,256]{1,0:T(8,128)(2,1)S(1)}, u32[]{:S(2)}, u32[]{:S(2)}) %collective-permute-start.7) | collective-permute-done | bytes 204832 | tf_op jit(solution)/shard_map/ppermute | solution.py:585
  47.2 0.9 far.1
  48.2 0.5 collective-permute-start.18
  48.7 0.8 collective-permute-done.9.other_ref
  49.6 0.1 norm.1
  49.7 7.5 %collective-permute-start.13 = (bf16[64,1024]{1,0:T(8,128)(2,1)S(1)}, bf16[64,1024]{1,0:T(8,128)(2,1)S(1)}, u32[]{:S(2)}, u32[]{:S(2)}) collective-permute-start(bf16[64,1024]{1,0:T(8,128)(2,1)S(1)} %get-tuple-element.41.refs_0_), channel_id=1, source_target_pairs={{0,16},{2,18},{4,20},{6,22},{8,24},{10,26},{12,28},{14,30},{16,0},... | collective-permute-start | bytes 393224 | tf_op jit(solution)/shard_map/ppermute | solution.py:585
  57.2 1.5 %collective-permute-start.10 = (bf16[64,1024]{1,0:T(8,128)(2,1)S(1)}, bf16[64,1024]{1,0:T(8,128)(2,1)S(1)}, u32[]{:S(2)}, u32[]{:S(2)}) collective-permute-start(bf16[64,1024]{1,0:T(8,128)(2,1)S(1)} %get-tuple-element.41.refs_0_), channel_id=1, source_target_pairs={{0,2},{2,0},{4,6},{6,4},{8,10},{10,8},{12,14},{14,12},{16,18},{18,... | collective-permute-start | bytes 393224 | tf_op jit(solution)/shard_map/ppermute | solution.py:585
  58.7 0.7 collective-permute-start.11
  59.4 4.4 %collective-permute-done.13.refs_4_ = bf16[64,1024]{1,0:T(8,128)(2,1)S(1)} collective-permute-done((bf16[64,1024]{1,0:T(8,128)(2,1)S(1)}, bf16[64,1024]{1,0:T(8,128)(2,1)S(1)}, u32[]{:S(2)}, u32[]{:S(2)}) %collective-permute-start.13) | collective-permute-done | bytes 131104 | tf_op jit(solution)/shard_map/ppermute | solution.py:585
  63.8 1.7 %collective-permute-start.12 = (bf16[64,1024]{1,0:T(8,128)(2,1)S(1)}, bf16[64,1024]{1,0:T(8,128)(2,1)S(1)}, u32[]{:S(2)}, u32[]{:S(2)}) collective-permute-start(bf16[64,1024]{1,0:T(8,128)(2,1)S(1)} %get-tuple-element.41.refs_0_), channel_id=1, source_target_pairs={{0,6},{2,4},{4,2},{6,0},{8,14},{10,12},{12,10},{14,8},{16,22},{18,... | collective-permute-start | bytes 393224 | tf_op jit(solution)/shard_map/ppermute | solution.py:585
  65.5 0.4 columns.1.share_ref
  66.0 0.4 stack.1
  66.4 1.9 %collective-permute-start.23 = (bf16[64,1024]{1,0:T(8,128)(2,1)S(1)}, bf16[64,1024]{1,0:T(8,128)(2,1)S(1)}, u32[]{:S(2)}, u32[]{:S(2)}) collective-permute-start(bf16[64,1024]{1,0:T(8,128)(2,1)S(1)} %collective-permute-done.13.refs_4_), channel_id=1, source_target_pairs={{0,4},{2,6},{4,0},{6,2},{8,12},{10,14},{12,8},{14,10},{16,20},{18,... | collective-permute-start | bytes 393224 | tf_op jit(solution)/shard_map/ppermute | solution.py:585
  68.2 1.7 %collective-permute-start.24 = (bf16[64,1024]{1,0:T(8,128)(2,1)S(1)}, bf16[64,1024]{1,0:T(8,128)(2,1)S(1)}, u32[]{:S(2)}, u32[]{:S(2)}) collective-permute-start(bf16[64,1024]{1,0:T(8,128)(2,1)S(1)} %collective-permute-done.13.refs_4_), channel_id=1, source_target_pairs={{0,6},{2,4},{4,2},{6,0},{8,14},{10,12},{12,10},{14,8},{16,22},{18,... | collective-permute-start | bytes 393224 | tf_op jit(solution)/shard_map/ppermute | solution.py:585
  69.9 1.2 %collective-permute-done.12.refs_3_ = bf16[64,1024]{1,0:T(8,128)(2,1)S(1)} collective-permute-done((bf16[64,1024]{1,0:T(8,128)(2,1)S(1)}, bf16[64,1024]{1,0:T(8,128)(2,1)S(1)}, u32[]{:S(2)}, u32[]{:S(2)}) %collective-permute-start.12) | collective-permute-done | bytes 131104 | tf_op jit(solution)/shard_map/ppermute | solution.py:585
  71.1 1.2 %expand.1.hidden_ref = bf16[320,768]{1,0:T(8,128)(2,1)S(1)} custom-call(f32[512,128]{1,0:T(8,128)S(1)} %columns.1.share_ref, bf16[64,1024]{1,0:T(8,128)(2,1)S(1)} %get-tuple-element.41.refs_0_, bf16[64,1024]{1,0:T(8,128)(2,1)S(1)} %collective-permute-done.10.refs_1_, bf16[64,1024]{1,0:T(8,128)(2,1)S(1)} %collective-permute-done.11.refs_2_, ...), custom_call_target="tpu_custom_call" | custom-call | flops 1006632960 | bytes 3145728 | tf_op jit(solution)/shard_map/expand/pallas_call | solution.py:465
  72.3 1.1 %contract.1 = (f32[64,1024]{1,0:T(8,128)S(1)}, bf16[64,1024]{1,0:T(8,128)(2,1)S(1)}, bf16[64,1024]{1,0:T(8,128)(2,1)S(1)}, bf16[64,1024]{1,0:T(8,128)(2,1)S(1)},...) custom-call(bf16[320,768]{1,0:T(8,128)(2,1)S(1)} %expand.1.hidden_ref, bf16[1,384,1024]{2,1,0:T(8,128)(2,1)S(1)} %copy-done, ...), custom_call_target="tpu_custom_call" | custom-call | flops 503316480 | bytes 1572864 | tf_op jit(solution)/shard_map/contract/pallas_call | solution.py:497
  73.5 0.4 collective-permute-done.23.refs_1_
  73.9 1.8 %collective-permute-done.24.refs_2_ = bf16[64,1024]{1,0:T(8,128)(2,1)S(1)} collective-permute-done((bf16[64,1024]{1,0:T(8,128)(2,1)S(1)}, bf16[64,1024]{1,0:T(8,128)(2,1)S(1)}, u32[]{:S(2)}, u32[]{:S(2)}) %collective-permute-start.24) | collective-permute-done | bytes 131104 | tf_op jit(solution)/shard_map/ppermute | solution.py:585
  75.7 1.2 %experts_far.1 = (bf16[64,1024]{1,0:T(8,128)(2,1)S(1)}, bf16[64,1024]{1,0:T(8,128)(2,1)S(1)}, bf16[64,1024]{1,0:T(8,128)(2,1)S(1)}) custom-call(f32[512,128]{1,0:T(8,128)S(1)} %columns.1.share_ref, bf16[64,1024]{1,0:T(8,128)(2,1)S(1)} %collective-permute-done.22.refs_0_, bf16[64,1024]{1,0:T(8,128)(2,1)S(1)} %collective-permute-done.23.refs_1_, ...), custom_call_target="tpu_custom_call" | custom-call | flops 905969664 | bytes 4718592 | tf_op jit(solution)/shard_map/experts_far/pallas_call | solution.py:521
  76.9 1.5 %collective-permute-start.25 = (bf16[64,1024]{1,0:T(8,128)(2,1)S(1)}, bf16[64,1024]{1,0:T(8,128)(2,1)S(1)}, u32[]{:S(2)}, u32[]{:S(2)}) collective-permute-start(bf16[64,1024]{1,0:T(8,128)(2,1)S(1)} %get-tuple-element.50), channel_id=1, source_target_pairs={{0,2},{2,0},{4,6},{6,4},{8,10},{10,8},{12,14},{14,12},{16,18},{18,... | collective-permute-start | bytes 393224 | tf_op jit(solution)/shard_map/ppermute | solution.py:585
  78.4 0.9 collective-permute-start.26
  79.4 1.1 %collective-permute-start.27 = (bf16[64,1024]{1,0:T(8,128)(2,1)S(1)}, bf16[64,1024]{1,0:T(8,128)(2,1)S(1)}, u32[]{:S(2)}, u32[]{:S(2)}) collective-permute-start(bf16[64,1024]{1,0:T(8,128)(2,1)S(1)} %get-tuple-element.52), channel_id=1, source_target_pairs={{0,6},{2,4},{4,2},{6,0},{8,14},{10,12},{12,10},{14,8},{16,22},{18,... | collective-permute-start | bytes 393224 | tf_op jit(solution)/shard_map/ppermute | solution.py:585
  80.4 1.5 %collective-permute-start.19 = (bf16[64,1024]{1,0:T(8,128)(2,1)S(1)}, bf16[64,1024]{1,0:T(8,128)(2,1)S(1)}, u32[]{:S(2)}, u32[]{:S(2)}) collective-permute-start(bf16[64,1024]{1,0:T(8,128)(2,1)S(1)} %get-tuple-element.45), channel_id=1, source_target_pairs={{0,2},{2,0},{4,6},{6,4},{8,10},{10,8},{12,14},{14,12},{16,18},{18,... | collective-permute-start | bytes 393224 | tf_op jit(solution)/shard_map/ppermute | solution.py:585
  81.9 0.9 collective-permute-start.20
  82.9 2.3 %collective-permute-start.21 = (bf16[64,1024]{1,0:T(8,128)(2,1)S(1)}, bf16[64,1024]{1,0:T(8,128)(2,1)S(1)}, u32[]{:S(2)}, u32[]{:S(2)}) collective-permute-start(bf16[64,1024]{1,0:T(8,128)(2,1)S(1)} %get-tuple-element.47), channel_id=1, source_target_pairs={{0,6},{2,4},{4,2},{6,0},{8,14},{10,12},{12,10},{14,8},{16,22},{18,... | collective-permute-start | bytes 393224 | tf_op jit(solution)/shard_map/ppermute | solution.py:585
  85.2 2.6 %collective-permute-done.26.refs_1_ = bf16[64,1024]{1,0:T(8,128)(2,1)S(1)} collective-permute-done((bf16[64,1024]{1,0:T(8,128)(2,1)S(1)}, bf16[64,1024]{1,0:T(8,128)(2,1)S(1)}, u32[]{:S(2)}, u32[]{:S(2)}) %collective-permute-start.26) | collective-permute-done | bytes 131104 | tf_op jit(solution)/shard_map/ppermute | solution.py:585
  87.9 1.0 %collective-permute-done.19.refs_0_ = bf16[64,1024]{1,0:T(8,128)(2,1)S(1)} collective-permute-done((bf16[64,1024]{1,0:T(8,128)(2,1)S(1)}, bf16[64,1024]{1,0:T(8,128)(2,1)S(1)}, u32[]{:S(2)}, u32[]{:S(2)}) %collective-permute-start.19) | collective-permute-done | bytes 131104 | tf_op jit(solution)/shard_map/ppermute | solution.py:585
  88.9 2.3 %collective-permute-done.20.refs_1_ = bf16[64,1024]{1,0:T(8,128)(2,1)S(1)} collective-permute-done((bf16[64,1024]{1,0:T(8,128)(2,1)S(1)}, bf16[64,1024]{1,0:T(8,128)(2,1)S(1)}, u32[]{:S(2)}, u32[]{:S(2)}) %collective-permute-start.20) | collective-permute-done | bytes 131104 | tf_op jit(solution)/shard_map/ppermute | solution.py:585
  91.2 3.1 %collective-permute-done.28.refs_3_ = bf16[64,1024]{1,0:T(8,128)(2,1)S(1)} collective-permute-done((bf16[64,1024]{1,0:T(8,128)(2,1)S(1)}, bf16[64,1024]{1,0:T(8,128)(2,1)S(1)}, u32[]{:S(2)}, u32[]{:S(2)}) %collective-permute-start.28) | collective-permute-done | bytes 131104 | tf_op jit(solution)/shard_map/ppermute | solution.py:585
  94.5 1.2 %collective-permute-done.29.received_ref = bf16[64,512]{1,0:T(8,128)(2,1)S(1)} collective-permute-done((bf16[64,512]{1,0:T(8,128)(2,1)S(1)}, bf16[64,512]{1,0:T(8,128)(2,1)S(1)}, u32[]{:S(2)}, u32[]{:S(2)}) %collective-permute-start.29) | collective-permute-done | bytes 65568 | tf_op jit(solution)/shard_map/ppermute | solution.py:591
  95.8 0.7 assemble.1
  (41 shorter events, 1.0 us)
Async XLA Ops:
  0.0 23.4 %collective-permute-start.14 = (bf16[1024,384]{1,0:T(8,128)(2,1)}, bf16[1024,384]{1,0:T(8,128)(2,1)S(1)}, u32[]{:S(2)}, u32[]{:S(2)}) collective-permute-start(bf16[1024,384]{1,0:T(8,128)(2,1)} %bitcast.5), channel_id=1, source_target_pairs={{0,8},{2,10},{4,12},{6,14},{8,0},{10,2},{12,4},{14,6},{16,24},{18,... | collective-permute-start | bytes 2359304 | tf_op jit(solution)/shard_map/ppermute | solution.py:607
  5.0 18.5 %collective-permute-start.15 = (bf16[1024,384]{1,0:T(8,128)(2,1)}, bf16[1024,384]{1,0:T(8,128)(2,1)S(1)}, u32[]{:S(2)}, u32[]{:S(2)}) collective-permute-start(bf16[1024,384]{1,0:T(8,128)(2,1)} %bitcast.6), channel_id=1, source_target_pairs={{1,9},{3,11},{5,13},{7,15},{9,1},{11,3},{13,5},{15,7},{17,25},{19,... | collective-permute-start | bytes 2359304 | tf_op jit(solution)/shard_map/ppermute | solution.py:607
  6.5 24.8 %collective-permute-start.3 = (bf16[128,256]{1,0:T(8,128)(2,1)S(1)}, bf16[128,256]{1,0:T(8,128)(2,1)S(1)}, u32[]{:S(2)}, u32[]{:S(2)}) collective-permute-start(bf16[128,256]{1,0:T(8,128)(2,1)S(1)} %get-tuple-element.31), channel_id=1, source_target_pairs={{0,8},{2,10},{4,12},{6,14},{8,16},{10,18},{12,20},{14,22},{16,24},... | collective-permute-start | bytes 196616 | tf_op jit(solution)/shard_map/ppermute | solution.py:588
  23.5 42.3 %collective-permute-start.16 = (bf16[1024,384]{1,0:T(8,128)(2,1)S(1)}, bf16[1024,384]{1,0:T(8,128)(2,1)S(1)}, u32[]{:S(2)}, u32[]{:S(2)}) collective-permute-start(bf16[1024,384]{1,0:T(8,128)(2,1)S(1)} %merge.1.mine_ref), channel_id=1, source_target_pairs={{0,1},{1,0},{2,3},{3,2},{4,5},{5,4},{6,7},{7,6},{8,9},{9,8},{10,11... | collective-permute-start | bytes 2359304 | tf_op jit(solution)/shard_map/ppermute | solution.py:591
  23.6 9.2 %collective-permute-start.5 = (bf16[128,256]{1,0:T(8,128)(2,1)S(1)}, bf16[128,256]{1,0:T(8,128)(2,1)S(1)}, u32[]{:S(2)}, u32[]{:S(2)}) collective-permute-start(bf16[128,256]{1,0:T(8,128)(2,1)S(1)} %get-tuple-element.31), channel_id=1, source_target_pairs={{0,24},{2,26},{4,28},{6,30},{1,25},{3,27},{5,29},{7,31}} | collective-permute-start | bytes 196616 | tf_op jit(solution)/shard_map/ppermute | solution.py:588
  29.7 6.0 %collective-permute-start.4 = (bf16[144,256]{1,0:T(8,128)(2,1)S(1)}, bf16[144,256]{1,0:T(8,128)(2,1)S(1)}, u32[]{:S(2)}, u32[]{:S(2)}) collective-permute-start(bf16[144,256]{1,0:T(8,128)(2,1)S(1)} %get-tuple-element.30.refs_0_), channel_id=1, source_target_pairs={{0,16},{2,18},{4,20},{6,22},{8,24},{10,26},{12,28},{14,30},{16,0},... | collective-permute-start | bytes 221192 | tf_op jit(solution)/shard_map/ppermute | solution.py:585
  29.8 6.0 %collective-permute-start = (bf16[144,256]{1,0:T(8,128)(2,1)S(1)}, bf16[144,256]{1,0:T(8,128)(2,1)S(1)}, u32[]{:S(2)}, u32[]{:S(2)}) collective-permute-start(bf16[144,256]{1,0:T(8,128)(2,1)S(1)} %get-tuple-element.30.refs_0_), channel_id=1, source_target_pairs={{0,2},{2,0},{4,6},{6,4},{8,10},{10,8},{12,14},{14,12},{16,18},{18,... | collective-permute-start | bytes 221192 | tf_op jit(solution)/shard_map/ppermute | solution.py:585
  31.3 5.3 %collective-permute-start.1 = (bf16[144,256]{1,0:T(8,128)(2,1)S(1)}, bf16[144,256]{1,0:T(8,128)(2,1)S(1)}, u32[]{:S(2)}, u32[]{:S(2)}) collective-permute-start(bf16[144,256]{1,0:T(8,128)(2,1)S(1)} %get-tuple-element.30.refs_0_), channel_id=1, source_target_pairs={{0,4},{2,6},{4,0},{6,2},{8,12},{10,14},{12,8},{14,10},{16,20},{18,... | collective-permute-start | bytes 221192 | tf_op jit(solution)/shard_map/ppermute | solution.py:585
  32.9 5.3 %collective-permute-start.2 = (bf16[144,256]{1,0:T(8,128)(2,1)S(1)}, bf16[144,256]{1,0:T(8,128)(2,1)S(1)}, u32[]{:S(2)}, u32[]{:S(2)}) collective-permute-start(bf16[144,256]{1,0:T(8,128)(2,1)S(1)} %get-tuple-element.30.refs_0_), channel_id=1, source_target_pairs={{0,6},{2,4},{4,2},{6,0},{8,14},{10,12},{12,10},{14,8},{16,22},{18,... | collective-permute-start | bytes 221192 | tf_op jit(solution)/shard_map/ppermute | solution.py:585
  35.7 12.5 %collective-permute-start.17 = (bf16[192,1024]{1,0:T(8,128)(2,1)S(1)}, bf16[192,1024]{1,0:T(8,128)(2,1)S(1)}, u32[]{:S(2)}, u32[]{:S(2)}) collective-permute-start(bf16[192,1024]{1,0:T(8,128)(2,1)S(1)} %cut.1), channel_id=1, source_target_pairs={{0,8},{2,10},{4,12},{6,14},{8,0},{10,2},{12,4},{14,6},{16,24},{18,... | collective-permute-start | bytes 1179656 | tf_op jit(solution)/shard_map/ppermute | solution.py:585
  35.8 8.0 %collective-permute-start.6 = (bf16[400,256]{1,0:T(8,128)(2,1)S(1)}, bf16[400,256]{1,0:T(8,128)(2,1)S(1)}, u32[]{:S(2)}, u32[]{:S(2)}) collective-permute-start(bf16[400,256]{1,0:T(8,128)(2,1)S(1)} %join.1.refs_4_), channel_id=1, source_target_pairs={{0,2},{2,0},{4,6},{6,4},{8,10},{10,8},{12,14},{14,12},{16,18},{18,... | collective-permute-start | bytes 614408 | tf_op jit(solution)/shard_map/ppermute | solution.py:585
  36.6 10.4 %collective-permute-start.7 = (bf16[400,256]{1,0:T(8,128)(2,1)S(1)}, bf16[400,256]{1,0:T(8,128)(2,1)S(1)}, u32[]{:S(2)}, u32[]{:S(2)}) collective-permute-start(bf16[400,256]{1,0:T(8,128)(2,1)S(1)} %join.1.refs_4_), channel_id=1, source_target_pairs={{0,4},{2,6},{4,0},{6,2},{8,12},{10,14},{12,8},{14,10},{16,20},{18,... | collective-permute-start | bytes 614408 | tf_op jit(solution)/shard_map/ppermute | solution.py:585
  38.2 9.0 %collective-permute-start.8 = (bf16[400,256]{1,0:T(8,128)(2,1)S(1)}, bf16[400,256]{1,0:T(8,128)(2,1)S(1)}, u32[]{:S(2)}, u32[]{:S(2)}) collective-permute-start(bf16[400,256]{1,0:T(8,128)(2,1)S(1)} %join.1.refs_4_), channel_id=1, source_target_pairs={{0,6},{2,4},{4,2},{6,0},{8,14},{10,12},{12,10},{14,8},{16,22},{18,... | collective-permute-start | bytes 614408 | tf_op jit(solution)/shard_map/ppermute | solution.py:585
  41.3 5.9 %copy-start.1 = (bf16[1024,1024]{1,0:T(8,128)(2,1)S(1)}, bf16[1024,1024]{1,0:T(8,128)(2,1)}, u32[]{:S(2)}) copy-start(bf16[1024,1024]{1,0:T(8,128)(2,1)} %refs_0_.1) | copy-start | bytes 6291460
  47.2 2.3 %copy-start.4 = (bf16[128,1024]{1,0:T(8,128)(2,1)S(1)}, bf16[128,1024]{1,0:T(8,128)(2,1)}, u32[]{:S(2)}) copy-start(bf16[128,1024]{1,0:T(8,128)(2,1)} %hidden_ref.1) | copy-start | bytes 786436
  47.2 2.3 %copy-start.5 = (f32[1024]{0:T(1024)S(1)}, f32[1024]{0:T(1024)}, u32[]{:S(2)}) copy-start(f32[1024]{0:T(1024)} %param.16) | copy-start | bytes 12292
  48.1 17.8 %copy-start.2 = (bf16[1,1024,384]{2,1,0:T(8,128)(2,1)S(1)}, bf16[1,1024,384]{2,1,0:T(8,128)(2,1)}, u32[]{:S(2)}) copy-start(bf16[1,1024,384]{2,1,0:T(8,128)(2,1)} %gate_ref.1) | copy-start | bytes 2359300
  48.1 17.8 %copy-start.3 = (bf16[1,1024,384]{2,1,0:T(8,128)(2,1)S(1)}, bf16[1,1024,384]{2,1,0:T(8,128)(2,1)}, u32[]{:S(2)}) copy-start(bf16[1,1024,384]{2,1,0:T(8,128)(2,1)} %up_ref.1) | copy-start | bytes 2359300
  48.1 1.4 %collective-permute-start.9 = (bf16[64,1024]{1,0:T(8,128)(2,1)S(1)}, bf16[64,1024]{1,0:T(8,128)(2,1)S(1)}, u32[]{:S(2)}, u32[]{:S(2)}) collective-permute-start(bf16[64,1024]{1,0:T(8,128)(2,1)S(1)} %get-tuple-element.39), channel_id=1, source_target_pairs={{0,1},{1,0},{2,3},{3,2},{4,5},{5,4},{6,7},{7,6},{8,9},{9,8},{10,11... | collective-permute-start | bytes 393224 | tf_op jit(solution)/shard_map/ppermute | solution.py:591
  48.2 24.1 %collective-permute-start.18 = (bf16[192,1024]{1,0:T(8,128)(2,1)S(1)}, bf16[192,1024]{1,0:T(8,128)(2,1)S(1)}, u32[]{:S(2)}, u32[]{:S(2)}) collective-permute-start(bf16[192,1024]{1,0:T(8,128)(2,1)S(1)} %collective-permute-done.17.mine_ref), channel_id=1, source_target_pairs={{0,1},{1,0},{2,3},{3,2},{4,5},{5,4},{6,7},{7,6},{8,9},{9,8},{10,11... | collective-permute-start | bytes 1179656 | tf_op jit(solution)/shard_map/ppermute | solution.py:591
  49.7 14.1 %collective-permute-start.13 = (bf16[64,1024]{1,0:T(8,128)(2,1)S(1)}, bf16[64,1024]{1,0:T(8,128)(2,1)S(1)}, u32[]{:S(2)}, u32[]{:S(2)}) collective-permute-start(bf16[64,1024]{1,0:T(8,128)(2,1)S(1)} %get-tuple-element.41.refs_0_), channel_id=1, source_target_pairs={{0,16},{2,18},{4,20},{6,22},{8,24},{10,26},{12,28},{14,30},{16,0},... | collective-permute-start | bytes 393224 | tf_op jit(solution)/shard_map/ppermute | solution.py:585
  57.2 9.1 %collective-permute-start.10 = (bf16[64,1024]{1,0:T(8,128)(2,1)S(1)}, bf16[64,1024]{1,0:T(8,128)(2,1)S(1)}, u32[]{:S(2)}, u32[]{:S(2)}) collective-permute-start(bf16[64,1024]{1,0:T(8,128)(2,1)S(1)} %get-tuple-element.41.refs_0_), channel_id=1, source_target_pairs={{0,2},{2,0},{4,6},{6,4},{8,10},{10,8},{12,14},{14,12},{16,18},{18,... | collective-permute-start | bytes 393224 | tf_op jit(solution)/shard_map/ppermute | solution.py:585
  58.7 9.5 %collective-permute-start.11 = (bf16[64,1024]{1,0:T(8,128)(2,1)S(1)}, bf16[64,1024]{1,0:T(8,128)(2,1)S(1)}, u32[]{:S(2)}, u32[]{:S(2)}) collective-permute-start(bf16[64,1024]{1,0:T(8,128)(2,1)S(1)} %get-tuple-element.41.refs_0_), channel_id=1, source_target_pairs={{0,4},{2,6},{4,0},{6,2},{8,12},{10,14},{12,8},{14,10},{16,20},{18,... | collective-permute-start | bytes 393224 | tf_op jit(solution)/shard_map/ppermute | solution.py:585
  63.8 7.3 %collective-permute-start.12 = (bf16[64,1024]{1,0:T(8,128)(2,1)S(1)}, bf16[64,1024]{1,0:T(8,128)(2,1)S(1)}, u32[]{:S(2)}, u32[]{:S(2)}) collective-permute-start(bf16[64,1024]{1,0:T(8,128)(2,1)S(1)} %get-tuple-element.41.refs_0_), channel_id=1, source_target_pairs={{0,6},{2,4},{4,2},{6,0},{8,14},{10,12},{12,10},{14,8},{16,22},{18,... | collective-permute-start | bytes 393224 | tf_op jit(solution)/shard_map/ppermute | solution.py:585
  65.9 7.6 %collective-permute-start.22 = (bf16[64,1024]{1,0:T(8,128)(2,1)S(1)}, bf16[64,1024]{1,0:T(8,128)(2,1)S(1)}, u32[]{:S(2)}, u32[]{:S(2)}) collective-permute-start(bf16[64,1024]{1,0:T(8,128)(2,1)S(1)} %collective-permute-done.13.refs_4_), channel_id=1, source_target_pairs={{0,2},{2,0},{4,6},{6,4},{8,10},{10,8},{12,14},{14,12},{16,18},{18,... | collective-permute-start | bytes 393224 | tf_op jit(solution)/shard_map/ppermute | solution.py:585
  66.4 7.6 %collective-permute-start.23 = (bf16[64,1024]{1,0:T(8,128)(2,1)S(1)}, bf16[64,1024]{1,0:T(8,128)(2,1)S(1)}, u32[]{:S(2)}, u32[]{:S(2)}) collective-permute-start(bf16[64,1024]{1,0:T(8,128)(2,1)S(1)} %collective-permute-done.13.refs_4_), channel_id=1, source_target_pairs={{0,4},{2,6},{4,0},{6,2},{8,12},{10,14},{12,8},{14,10},{16,20},{18,... | collective-permute-start | bytes 393224 | tf_op jit(solution)/shard_map/ppermute | solution.py:585
  68.2 7.5 %collective-permute-start.24 = (bf16[64,1024]{1,0:T(8,128)(2,1)S(1)}, bf16[64,1024]{1,0:T(8,128)(2,1)S(1)}, u32[]{:S(2)}, u32[]{:S(2)}) collective-permute-start(bf16[64,1024]{1,0:T(8,128)(2,1)S(1)} %collective-permute-done.13.refs_4_), channel_id=1, source_target_pairs={{0,6},{2,4},{4,2},{6,0},{8,14},{10,12},{12,10},{14,8},{16,22},{18,... | collective-permute-start | bytes 393224 | tf_op jit(solution)/shard_map/ppermute | solution.py:585
  71.1 1.2 %copy-start = (bf16[1,384,1024]{2,1,0:T(8,128)(2,1)S(1)}, bf16[1,384,1024]{2,1,0:T(8,128)(2,1)}, u32[]{:S(2)}) copy-start(bf16[1,384,1024]{2,1,0:T(8,128)(2,1)} %down_ref.3) | copy-start | bytes 2359300
  76.9 6.0 %collective-permute-start.25 = (bf16[64,1024]{1,0:T(8,128)(2,1)S(1)}, bf16[64,1024]{1,0:T(8,128)(2,1)S(1)}, u32[]{:S(2)}, u32[]{:S(2)}) collective-permute-start(bf16[64,1024]{1,0:T(8,128)(2,1)S(1)} %get-tuple-element.50), channel_id=1, source_target_pairs={{0,2},{2,0},{4,6},{6,4},{8,10},{10,8},{12,14},{14,12},{16,18},{18,... | collective-permute-start | bytes 393224 | tf_op jit(solution)/shard_map/ppermute | solution.py:585
  78.4 9.4 %collective-permute-start.26 = (bf16[64,1024]{1,0:T(8,128)(2,1)S(1)}, bf16[64,1024]{1,0:T(8,128)(2,1)S(1)}, u32[]{:S(2)}, u32[]{:S(2)}) collective-permute-start(bf16[64,1024]{1,0:T(8,128)(2,1)S(1)} %get-tuple-element.51), channel_id=1, source_target_pairs={{0,4},{2,6},{4,0},{6,2},{8,12},{10,14},{12,8},{14,10},{16,20},{18,... | collective-permute-start | bytes 393224 | tf_op jit(solution)/shard_map/ppermute | solution.py:585
  79.4 8.4 %collective-permute-start.27 = (bf16[64,1024]{1,0:T(8,128)(2,1)S(1)}, bf16[64,1024]{1,0:T(8,128)(2,1)S(1)}, u32[]{:S(2)}, u32[]{:S(2)}) collective-permute-start(bf16[64,1024]{1,0:T(8,128)(2,1)S(1)} %get-tuple-element.52), channel_id=1, source_target_pairs={{0,6},{2,4},{4,2},{6,0},{8,14},{10,12},{12,10},{14,8},{16,22},{18,... | collective-permute-start | bytes 393224 | tf_op jit(solution)/shard_map/ppermute | solution.py:585
  80.4 8.5 %collective-permute-start.19 = (bf16[64,1024]{1,0:T(8,128)(2,1)S(1)}, bf16[64,1024]{1,0:T(8,128)(2,1)S(1)}, u32[]{:S(2)}, u32[]{:S(2)}) collective-permute-start(bf16[64,1024]{1,0:T(8,128)(2,1)S(1)} %get-tuple-element.45), channel_id=1, source_target_pairs={{0,2},{2,0},{4,6},{6,4},{8,10},{10,8},{12,14},{14,12},{16,18},{18,... | collective-permute-start | bytes 393224 | tf_op jit(solution)/shard_map/ppermute | solution.py:585
  81.9 9.3 %collective-permute-start.20 = (bf16[64,1024]{1,0:T(8,128)(2,1)S(1)}, bf16[64,1024]{1,0:T(8,128)(2,1)S(1)}, u32[]{:S(2)}, u32[]{:S(2)}) collective-permute-start(bf16[64,1024]{1,0:T(8,128)(2,1)S(1)} %get-tuple-element.46), channel_id=1, source_target_pairs={{0,4},{2,6},{4,0},{6,2},{8,12},{10,14},{12,8},{14,10},{16,20},{18,... | collective-permute-start | bytes 393224 | tf_op jit(solution)/shard_map/ppermute | solution.py:585
  82.9 8.3 %collective-permute-start.21 = (bf16[64,1024]{1,0:T(8,128)(2,1)S(1)}, bf16[64,1024]{1,0:T(8,128)(2,1)S(1)}, u32[]{:S(2)}, u32[]{:S(2)}) collective-permute-start(bf16[64,1024]{1,0:T(8,128)(2,1)S(1)} %get-tuple-element.47), channel_id=1, source_target_pairs={{0,6},{2,4},{4,2},{6,0},{8,14},{10,12},{12,10},{14,8},{16,22},{18,... | collective-permute-start | bytes 393224 | tf_op jit(solution)/shard_map/ppermute | solution.py:585
  87.9 6.5 %collective-permute-start.28 = (bf16[64,1024]{1,0:T(8,128)(2,1)S(1)}, bf16[64,1024]{1,0:T(8,128)(2,1)S(1)}, u32[]{:S(2)}, u32[]{:S(2)}) collective-permute-start(bf16[64,1024]{1,0:T(8,128)(2,1)S(1)} %gather_sum.1), channel_id=1, source_target_pairs={{0,16},{2,18},{4,20},{6,22},{8,24},{10,26},{12,28},{14,30},{16,0},... | collective-permute-start | bytes 393224 | tf_op jit(solution)/shard_map/ppermute | solution.py:585
  94.5 1.3 %collective-permute-start.29 = (bf16[64,512]{1,0:T(8,128)(2,1)S(1)}, bf16[64,512]{1,0:T(8,128)(2,1)S(1)}, u32[]{:S(2)}, u32[]{:S(2)}) collective-permute-start(bf16[64,512]{1,0:T(8,128)(2,1)S(1)} %get-tuple-element.54), channel_id=1, source_target_pairs={{0,1},{1,0},{2,3},{3,2},{4,5},{5,4},{6,7},{7,6},{8,9},{9,8},{10,11... | collective-permute-start | bytes 196616 | tf_op jit(solution)/shard_map/ppermute | solution.py:591

commit v4 on v3

--- a/solution.py
+++ b/solution.py
@@ -87,22 +87,29 @@
     )(*[held(value) for value in (key_rows, value_rows, expert_ids.T, gate_scores.T)])
 
 
-def cut_kernel(down_ref, out_ref, sem):
-    half = out_ref.shape[0]
-    start = pl.multiple_of(lax.axis_index("exp") * half, half)
-    copy = pltpu.make_async_copy(down_ref.at[0, pl.ds(start, half)], out_ref, sem)
-    copy.start()
-    copy.wait()
+def cut_kernel(down_ref, first_ref, second_ref, sems):
+    size = first_ref.shape[0]
+    half = size + second_ref.shape[0]
+    start = lax.axis_index("exp") * half
+    first = pl.ds(pl.multiple_of(start, size), size)
+    second = pl.ds(pl.multiple_of(start + size, size), half - size)
+    pairs = [(down_ref.at[0, first], first_ref), (down_ref.at[0, second], second_ref)]
+    for copy in fetch_all(pairs, sems):
+        copy.wait()
 
 
 def cut(w_down):
     _, units, model = w_down.shape
+    size = units // 6
     return pl.pallas_call(
         cut_kernel,
-        out_shape=jax.ShapeDtypeStruct((units // 2, model), w_down.dtype),
+        out_shape=(
+            jax.ShapeDtypeStruct((size, model), w_down.dtype),
+            jax.ShapeDtypeStruct((2 * size, model), w_down.dtype),
+        ),
         in_specs=[whole(pl.ANY)],
-        out_specs=whole(),
-        scratch_shapes=[pltpu.SemaphoreType.DMA],
+        out_specs=(whole(),) * 2,
+        scratch_shapes=[pltpu.SemaphoreType.DMA((2,))],
         cost_estimate=cost(1e3, 1e6),
         compiler_params=pltpu.CompilerParams(vmem_limit_bytes=ROOM),
         name="cut",
@@ -474,23 +481,24 @@
     )(shares, *inputs, *wide)
 
 
-def contract_kernel(hidden_ref, down_ref, mine_ref, other_ref, *refs):
-    outputs, tall_ref, sems = refs[:-2], refs[-2], refs[-1]
+def contract_kernel(hidden_ref, down_ref, *refs):
+    pieces, outputs, tall_ref, sems = refs[:4], refs[4:-2], refs[-2], refs[-1]
     units, core = down_ref.shape[1], lax.axis_index("exp")
-    half = units // 2
-    mine = pl.ds(pl.multiple_of(units + core * half, half), half)
-    other = pl.ds(pl.multiple_of(units + (1 - core) * half, half), half)
-    pairs = [
-        (down_ref.at[0], tall_ref.at[:units]),
-        (mine_ref, tall_ref.at[mine]),
-        (other_ref, tall_ref.at[other]),
-    ]
+    pairs = [(down_ref.at[0], tall_ref.at[:units])]
+    for n, position in enumerate((core, 1 - core)):
+        start = units + position * (units // 2)
+        for ref in pieces[n::2]:
+            size = ref.shape[0]
+            step = math.gcd(size, units // 6)
+            band = pl.ds(pl.multiple_of(start, step), size)
+            pairs.append((ref, tall_ref.at[band]))
+            start = start + size
     for copy in fetch_all(pairs, sems):
         copy.wait()
     expert_sums(hidden_ref, tall_ref, outputs)
 
 
-def contract(hidden, w_down, mine, other, dtypes):
+def contract(hidden, w_down, pieces, dtypes):
     blocks = len(dtypes)
     size, model = hidden.shape[0] // blocks, w_down.shape[2]
     both = hidden.shape[1]
@@ -498,13 +506,13 @@
         contract_kernel,
         out_shape=tuple(jax.ShapeDtypeStruct((size, model), dtype) for dtype in dtypes)
         + (jax.ShapeDtypeStruct((both, model), jnp.bfloat16),),
-        in_specs=[whole()] + [whole(pl.ANY)] * 3,
+        in_specs=[whole()] + [whole(pl.ANY)] * 5,
         out_specs=(whole(),) * (blocks + 1),
-        scratch_shapes=[pltpu.SemaphoreType.DMA((3,))],
+        scratch_shapes=[pltpu.SemaphoreType.DMA((5,))],
         cost_estimate=cost(2 * blocks * size * model * both, 2 * model * both),
         compiler_params=pltpu.CompilerParams(vmem_limit_bytes=ROOM),
         name="contract",
-    )(hidden, w_down, mine, other)
+    )(hidden, w_down, *pieces)
 
 
 def expert_far_kernel(first, blocks, share_ref, *refs):
@@ -608,8 +616,7 @@
 
     gate_swap = half_flip(w_gate[0], 0)
     up_swap = half_flip(w_up[0], 1)
-    tall = cut(w_down)
-    tall_swap = flip(tall, plane)
+    tall_swap = [flip(piece, plane) for piece in cut(w_down)]
 
     heads = turn(queries)
     state = near(heads, [mixed] + level, joined, plane)
@@ -624,9 +631,9 @@
     corner_rows = [flip(opposite, mate) for mate in mates]
     f32, bf16 = jnp.float32, jnp.bfloat16
     hidden = expand(shares, [normed] + level_rows + [opposite], wide)
+    pieces = [value for piece in tall_swap for value in (piece, across(piece))]
     *near_out, tall = contract(
-        hidden, w_down, tall_swap, across(tall_swap),
-        [f32] + [bf16] * len(mates) + [f32],
+        hidden, w_down, pieces, [f32] + [bf16] * len(mates) + [f32]
     )
     far_out = experts_far(shares, corner_rows, wide, tall, plane + 1)
     passed = [flip(value, mate) for value, mate in zip(far_out, mates)]

time: 96.8 us -> 105 us (1.085)
  waiting for transfers between devices: 37.7 us -> 42.7 us
  starting transfers between devices: 47.2 us -> 50.1 us
    ppermute x22 -> x23, starting transfers between devices: 32.8 us -> 39.4 us  [flip(): return lax.ppermute(value, 'ctx', [(i, i ^ mask) for i in range(ctx)])]
    ppermute x2, starting transfers between devices: 8 us -> 4.76 us  [upward(): lax.ppermute(value, 'ctx', [(i, i + step) for i in range(ctx - step)])]
    ppermute x2, waiting for transfers between devices: 15 us -> 17.7 us  [half_flip(): return lax.ppermute(value, ('ctx', 'exp'), pairs)]
    ppermute x22 -> x23, waiting for transfers between devices: 20.7 us -> 23.4 us  [flip(): return lax.ppermute(value, 'ctx', [(i, i ^ mask) for i in range(ctx)])]
  transfers between devices with their start and end apart: 30 -> 32, of which waited for: 13 -> 12; matrix products, arithmetic and copies ran while one was open for 0% -> 0% of each run, Pallas kernels for 10% -> 9%
where the time goes in v4:
time: 105 us; the launch traced here: 104 us
  starting transfers between devices  50.1 us (48%)
  waiting for transfers between devices  42.7 us (41%)
  Pallas kernels  11.2 us (11%)
    ppermute x23, starting transfers between devices, flip(): return lax.ppermute(value, 'ctx', [(i, i ^ mask) for i in range(ctx)])  39.4 us
    ppermute x23, waiting for transfers between devices, flip(): return lax.ppermute(value, 'ctx', [(i, i ^ mask) for i in range(ctx)])  23.4 us
    ppermute x2, waiting for transfers between devices, half_flip(): return lax.ppermute(value, ('ctx', 'exp'), pairs)  17.7 us
    ppermute x2, starting transfers between devices, half_flip(): return lax.ppermute(value, ('ctx', 'exp'), pairs)  5.66 us
    ppermute x2, starting transfers between devices, upward(): lax.ppermute(value, 'ctx', [(i, i + step) for i in range(ctx - step)])  4.76 us
  transfers between devices with their start and end apart: 32, of which 12 were waited for; matrix products, arithmetic and copies ran while one was open for 0% of the time, Pallas kernels for 9%

profile of v4, /device:TPU:0, one launch (start us, length us, event | category | flops | bytes accessed | tf_op | source)
XLA Modules:
  0.0 104.3 jit_solution(3466431873027620890)
XLA Ops:
  0.0 5.0 %collective-permute-start.14 = (bf16[1024,384]{1,0:T(8,128)(2,1)}, bf16[1024,384]{1,0:T(8,128)(2,1)S(1)}, u32[]{:S(2)}, u32[]{:S(2)}) collective-permute-start(bf16[1024,384]{1,0:T(8,128)(2,1)} %bitcast.5), channel_id=1, source_target_pairs={{0,8},{2,10},{4,12},{6,14},{8,0},{10,2},{12,4},{14,6},{16,24},{18,... | collective-permute-start | bytes 2359304 | tf_op jit(solution)/shard_map/ppermute | solution.py:615
  5.0 0.7 collective-permute-start.15
  5.7 17.7 %collective-permute-done.14.first_ref = bf16[1024,384]{1,0:T(8,128)(2,1)S(1)} collective-permute-done((bf16[1024,384]{1,0:T(8,128)(2,1)}, bf16[1024,384]{1,0:T(8,128)(2,1)S(1)}, u32[]{:S(2)}, u32[]{:S(2)}) %collective-permute-start.14) | collective-permute-done | bytes 786464 | tf_op jit(solution)/shard_map/ppermute | solution.py:615
  23.6 0.8 pack.1
  24.5 2.8 %collective-permute-start.4 = (bf16[144,256]{1,0:T(8,128)(2,1)S(1)}, bf16[144,256]{1,0:T(8,128)(2,1)S(1)}, u32[]{:S(2)}, u32[]{:S(2)}) collective-permute-start(bf16[144,256]{1,0:T(8,128)(2,1)S(1)} %get-tuple-element.32.refs_0_), channel_id=1, source_target_pairs={{0,16},{2,18},{4,20},{6,22},{8,24},{10,26},{12,28},{14,30},{16,0},... | collective-permute-start | bytes 221192 | tf_op jit(solution)/shard_map/ppermute | solution.py:593
  27.3 3.5 %collective-permute-start.3 = (bf16[128,256]{1,0:T(8,128)(2,1)S(1)}, bf16[128,256]{1,0:T(8,128)(2,1)S(1)}, u32[]{:S(2)}, u32[]{:S(2)}) collective-permute-start(bf16[128,256]{1,0:T(8,128)(2,1)S(1)} %get-tuple-element.33), channel_id=1, source_target_pairs={{0,8},{2,10},{4,12},{6,14},{8,16},{10,18},{12,20},{14,22},{16,24},... | collective-permute-start | bytes 196616 | tf_op jit(solution)/shard_map/ppermute | solution.py:596
  30.8 1.3 %collective-permute-start.5 = (bf16[128,256]{1,0:T(8,128)(2,1)S(1)}, bf16[128,256]{1,0:T(8,128)(2,1)S(1)}, u32[]{:S(2)}, u32[]{:S(2)}) collective-permute-start(bf16[128,256]{1,0:T(8,128)(2,1)S(1)} %get-tuple-element.33), channel_id=1, source_target_pairs={{0,24},{2,26},{4,28},{6,30},{1,25},{3,27},{5,29},{7,31}} | collective-permute-start | bytes 196616 | tf_op jit(solution)/shard_map/ppermute | solution.py:596
  32.1 1.6 %collective-permute-start = (bf16[144,256]{1,0:T(8,128)(2,1)S(1)}, bf16[144,256]{1,0:T(8,128)(2,1)S(1)}, u32[]{:S(2)}, u32[]{:S(2)}) collective-permute-start(bf16[144,256]{1,0:T(8,128)(2,1)S(1)} %get-tuple-element.32.refs_0_), channel_id=1, source_target_pairs={{0,2},{2,0},{4,6},{6,4},{8,10},{10,8},{12,14},{14,12},{16,18},{18,... | collective-permute-start | bytes 221192 | tf_op jit(solution)/shard_map/ppermute | solution.py:593
  34.0 1.6 %collective-permute-start.6 = (bf16[400,256]{1,0:T(8,128)(2,1)S(1)}, bf16[400,256]{1,0:T(8,128)(2,1)S(1)}, u32[]{:S(2)}, u32[]{:S(2)}) collective-permute-start(bf16[400,256]{1,0:T(8,128)(2,1)S(1)} %join.1.refs_4_), channel_id=1, source_target_pairs={{0,2},{2,0},{4,6},{6,4},{8,10},{10,8},{12,14},{14,12},{16,18},{18,... | collective-permute-start | bytes 614408 | tf_op jit(solution)/shard_map/ppermute | solution.py:593
  35.5 1.5 %collective-permute-start.7 = (bf16[400,256]{1,0:T(8,128)(2,1)S(1)}, bf16[400,256]{1,0:T(8,128)(2,1)S(1)}, u32[]{:S(2)}, u32[]{:S(2)}) collective-permute-start(bf16[400,256]{1,0:T(8,128)(2,1)S(1)} %join.1.refs_4_), channel_id=1, source_target_pairs={{0,4},{2,6},{4,0},{6,2},{8,12},{10,14},{12,8},{14,10},{16,20},{18,... | collective-permute-start | bytes 614408 | tf_op jit(solution)/shard_map/ppermute | solution.py:593
  37.0 0.5 collective-permute-start.1
  37.6 1.8 %collective-permute-start.8 = (bf16[400,256]{1,0:T(8,128)(2,1)S(1)}, bf16[400,256]{1,0:T(8,128)(2,1)S(1)}, u32[]{:S(2)}, u32[]{:S(2)}) collective-permute-start(bf16[400,256]{1,0:T(8,128)(2,1)S(1)} %join.1.refs_4_), channel_id=1, source_target_pairs={{0,6},{2,4},{4,2},{6,0},{8,14},{10,12},{12,10},{14,8},{16,22},{18,... | collective-permute-start | bytes 614408 | tf_op jit(solution)/shard_map/ppermute | solution.py:593
  39.4 8.2 %collective-permute-done.1.refs_2_ = bf16[144,256]{1,0:T(8,128)(2,1)S(1)} collective-permute-done((bf16[144,256]{1,0:T(8,128)(2,1)S(1)}, bf16[144,256]{1,0:T(8,128)(2,1)S(1)}, u32[]{:S(2)}, u32[]{:S(2)}) %collective-permute-start.1) | collective-permute-done | bytes 73760 | tf_op jit(solution)/shard_map/ppermute | solution.py:593
  47.6 2.3 %collective-permute-start.2 = (bf16[144,256]{1,0:T(8,128)(2,1)S(1)}, bf16[144,256]{1,0:T(8,128)(2,1)S(1)}, u32[]{:S(2)}, u32[]{:S(2)}) collective-permute-start(bf16[144,256]{1,0:T(8,128)(2,1)S(1)} %get-tuple-element.32.refs_0_), channel_id=1, source_target_pairs={{0,6},{2,4},{4,2},{6,0},{8,14},{10,12},{12,10},{14,8},{16,22},{18,... | collective-permute-start | bytes 221192 | tf_op jit(solution)/shard_map/ppermute | solution.py:593
  49.9 1.0 cut.1
  50.9 0.9 turn.1.heads_ref.query_ref
  51.9 1.0 collective-permute-done.2.refs_3_
  52.8 0.7 collective-permute-start.19
  53.6 2.0 %near.1 = (f32[1024,128]{1,0:T(8,128)S(1)}, f32[1024,128]{1,0:T(8,128)S(1)}, f32[1024,128]{1,0:T(8,128)S(1)}) custom-call(bf16[1024,128]{1,0:T(8,128)(2,1)S(1)} %turn.1.heads_ref.query_ref, bf16[144,256]{1,0:T(8,128)(2,1)S(1)} %get-tuple-element.32.refs_0_, bf16[144,256]{1,0:T(8,128)(2,1)S(1)} %collective-permute-done.refs_1_, ...), custom_call_target="tpu_custom_call" | custom-call | flops 469762048 | bytes 4000000 | tf_op jit(solution)/shard_map/near/pallas_call | solution.py:267
  55.8 0.9 far.1
  56.8 4.1 %collective-permute-start.17 = (bf16[64,1024]{1,0:T(8,128)(2,1)S(1)}, bf16[64,1024]{1,0:T(8,128)(2,1)S(1)}, u32[]{:S(2)}, u32[]{:S(2)}) collective-permute-start(bf16[64,1024]{1,0:T(8,128)(2,1)S(1)} %get-tuple-element.46), channel_id=1, source_target_pairs={{0,8},{2,10},{4,12},{6,14},{8,0},{10,2},{12,4},{14,6},{16,24},{18,... | collective-permute-start | bytes 393224 | tf_op jit(solution)/shard_map/ppermute | solution.py:593
  61.0 0.6 collective-permute-start.10
  61.6 5.2 %collective-permute-start.13 = (bf16[64,1024]{1,0:T(8,128)(2,1)S(1)}, bf16[64,1024]{1,0:T(8,128)(2,1)S(1)}, u32[]{:S(2)}, u32[]{:S(2)}) collective-permute-start(bf16[64,1024]{1,0:T(8,128)(2,1)S(1)} %get-tuple-element.43.refs_0_), channel_id=1, source_target_pairs={{0,16},{2,18},{4,20},{6,22},{8,24},{10,26},{12,28},{14,30},{16,0},... | collective-permute-start | bytes 393224 | tf_op jit(solution)/shard_map/ppermute | solution.py:593
  66.8 1.5 %collective-permute-start.11 = (bf16[64,1024]{1,0:T(8,128)(2,1)S(1)}, bf16[64,1024]{1,0:T(8,128)(2,1)S(1)}, u32[]{:S(2)}, u32[]{:S(2)}) collective-permute-start(bf16[64,1024]{1,0:T(8,128)(2,1)S(1)} %get-tuple-element.43.refs_0_), channel_id=1, source_target_pairs={{0,4},{2,6},{4,0},{6,2},{8,12},{10,14},{12,8},{14,10},{16,20},{18,... | collective-permute-start | bytes 393224 | tf_op jit(solution)/shard_map/ppermute | solution.py:593
  68.3 1.4 %collective-permute-start.12 = (bf16[64,1024]{1,0:T(8,128)(2,1)S(1)}, bf16[64,1024]{1,0:T(8,128)(2,1)S(1)}, u32[]{:S(2)}, u32[]{:S(2)}) collective-permute-start(bf16[64,1024]{1,0:T(8,128)(2,1)S(1)} %get-tuple-element.43.refs_0_), channel_id=1, source_target_pairs={{0,6},{2,4},{4,2},{6,0},{8,14},{10,12},{12,10},{14,8},{16,22},{18,... | collective-permute-start | bytes 393224 | tf_op jit(solution)/shard_map/ppermute | solution.py:593
  69.7 0.4 columns.1.share_ref
  70.1 0.4 stack.1
  70.5 3.2 %collective-permute-done.13.refs_4_ = bf16[64,1024]{1,0:T(8,128)(2,1)S(1)} collective-permute-done((bf16[64,1024]{1,0:T(8,128)(2,1)S(1)}, bf16[64,1024]{1,0:T(8,128)(2,1)S(1)}, u32[]{:S(2)}, u32[]{:S(2)}) %collective-permute-start.13) | collective-permute-done | bytes 131104 | tf_op jit(solution)/shard_map/ppermute | solution.py:593
  73.7 1.5 %collective-permute-start.24 = (bf16[64,1024]{1,0:T(8,128)(2,1)S(1)}, bf16[64,1024]{1,0:T(8,128)(2,1)S(1)}, u32[]{:S(2)}, u32[]{:S(2)}) collective-permute-start(bf16[64,1024]{1,0:T(8,128)(2,1)S(1)} %collective-permute-done.13.refs_4_), channel_id=1, source_target_pairs={{0,2},{2,0},{4,6},{6,4},{8,10},{10,8},{12,14},{14,12},{16,18},{18,... | collective-permute-start | bytes 393224 | tf_op jit(solution)/shard_map/ppermute | solution.py:593
  75.2 1.5 %collective-permute-start.25 = (bf16[64,1024]{1,0:T(8,128)(2,1)S(1)}, bf16[64,1024]{1,0:T(8,128)(2,1)S(1)}, u32[]{:S(2)}, u32[]{:S(2)}) collective-permute-start(bf16[64,1024]{1,0:T(8,128)(2,1)S(1)} %collective-permute-done.13.refs_4_), channel_id=1, source_target_pairs={{0,4},{2,6},{4,0},{6,2},{8,12},{10,14},{12,8},{14,10},{16,20},{18,... | collective-permute-start | bytes 393224 | tf_op jit(solution)/shard_map/ppermute | solution.py:593
  76.7 1.4 %collective-permute-start.26 = (bf16[64,1024]{1,0:T(8,128)(2,1)S(1)}, bf16[64,1024]{1,0:T(8,128)(2,1)S(1)}, u32[]{:S(2)}, u32[]{:S(2)}) collective-permute-start(bf16[64,1024]{1,0:T(8,128)(2,1)S(1)} %collective-permute-done.13.refs_4_), channel_id=1, source_target_pairs={{0,6},{2,4},{4,2},{6,0},{8,14},{10,12},{12,10},{14,8},{16,22},{18,... | collective-permute-start | bytes 393224 | tf_op jit(solution)/shard_map/ppermute | solution.py:593
  78.2 1.2 %expand.1.hidden_ref = bf16[320,768]{1,0:T(8,128)(2,1)S(1)} custom-call(f32[512,128]{1,0:T(8,128)S(1)} %columns.1.share_ref, bf16[64,1024]{1,0:T(8,128)(2,1)S(1)} %get-tuple-element.43.refs_0_, bf16[64,1024]{1,0:T(8,128)(2,1)S(1)} %collective-permute-done.10.refs_1_, bf16[64,1024]{1,0:T(8,128)(2,1)S(1)} %collective-permute-done.11.refs_2_, ...), custom_call_target="tpu_custom_call" | custom-call | flops 1006632960 | bytes 3145728 | tf_op jit(solution)/shard_map/expand/pallas_call | solution.py:472
  79.4 1.2 %contract.1 = (f32[64,1024]{1,0:T(8,128)S(1)}, bf16[64,1024]{1,0:T(8,128)(2,1)S(1)}, bf16[64,1024]{1,0:T(8,128)(2,1)S(1)}, bf16[64,1024]{1,0:T(8,128)(2,1)S(1)},...) custom-call(bf16[320,768]{1,0:T(8,128)(2,1)S(1)} %expand.1.hidden_ref, bf16[1,384,1024]{2,1,0:T(8,128)(2,1)S(1)} %copy-done, ...), custom_call_target="tpu_custom_call" | custom-call | flops 503316480 | bytes 1572864 | tf_op jit(solution)/shard_map/contract/pallas_call | solution.py:505
  80.6 2.5 %collective-permute-done.25.refs_1_ = bf16[64,1024]{1,0:T(8,128)(2,1)S(1)} collective-permute-done((bf16[64,1024]{1,0:T(8,128)(2,1)S(1)}, bf16[64,1024]{1,0:T(8,128)(2,1)S(1)}, u32[]{:S(2)}, u32[]{:S(2)}) %collective-permute-start.25) | collective-permute-done | bytes 131104 | tf_op jit(solution)/shard_map/ppermute | solution.py:593
  83.1 1.2 %experts_far.1 = (bf16[64,1024]{1,0:T(8,128)(2,1)S(1)}, bf16[64,1024]{1,0:T(8,128)(2,1)S(1)}, bf16[64,1024]{1,0:T(8,128)(2,1)S(1)}) custom-call(f32[512,128]{1,0:T(8,128)S(1)} %columns.1.share_ref, bf16[64,1024]{1,0:T(8,128)(2,1)S(1)} %collective-permute-done.24.refs_0_, bf16[64,1024]{1,0:T(8,128)(2,1)S(1)} %collective-permute-done.25.refs_1_, ...), custom_call_target="tpu_custom_call" | custom-call | flops 905969664 | bytes 4718592 | tf_op jit(solution)/shard_map/experts_far/pallas_call | solution.py:529
  84.2 1.4 %collective-permute-start.27 = (bf16[64,1024]{1,0:T(8,128)(2,1)S(1)}, bf16[64,1024]{1,0:T(8,128)(2,1)S(1)}, u32[]{:S(2)}, u32[]{:S(2)}) collective-permute-start(bf16[64,1024]{1,0:T(8,128)(2,1)S(1)} %get-tuple-element.54), channel_id=1, source_target_pairs={{0,2},{2,0},{4,6},{6,4},{8,10},{10,8},{12,14},{14,12},{16,18},{18,... | collective-permute-start | bytes 393224 | tf_op jit(solution)/shard_map/ppermute | solution.py:593
  85.7 1.3 %collective-permute-start.28 = (bf16[64,1024]{1,0:T(8,128)(2,1)S(1)}, bf16[64,1024]{1,0:T(8,128)(2,1)S(1)}, u32[]{:S(2)}, u32[]{:S(2)}) collective-permute-start(bf16[64,1024]{1,0:T(8,128)(2,1)S(1)} %get-tuple-element.55), channel_id=1, source_target_pairs={{0,4},{2,6},{4,0},{6,2},{8,12},{10,14},{12,8},{14,10},{16,20},{18,... | collective-permute-start | bytes 393224 | tf_op jit(solution)/shard_map/ppermute | solution.py:593
  87.0 0.8 collective-permute-start.29
  87.8 1.4 %collective-permute-start.21 = (bf16[64,1024]{1,0:T(8,128)(2,1)S(1)}, bf16[64,1024]{1,0:T(8,128)(2,1)S(1)}, u32[]{:S(2)}, u32[]{:S(2)}) collective-permute-start(bf16[64,1024]{1,0:T(8,128)(2,1)S(1)} %get-tuple-element.49), channel_id=1, source_target_pairs={{0,2},{2,0},{4,6},{6,4},{8,10},{10,8},{12,14},{14,12},{16,18},{18,... | collective-permute-start | bytes 393224 | tf_op jit(solution)/shard_map/ppermute | solution.py:593
  89.2 1.3 %collective-permute-start.22 = (bf16[64,1024]{1,0:T(8,128)(2,1)S(1)}, bf16[64,1024]{1,0:T(8,128)(2,1)S(1)}, u32[]{:S(2)}, u32[]{:S(2)}) collective-permute-start(bf16[64,1024]{1,0:T(8,128)(2,1)S(1)} %get-tuple-element.50), channel_id=1, source_target_pairs={{0,4},{2,6},{4,0},{6,2},{8,12},{10,14},{12,8},{14,10},{16,20},{18,... | collective-permute-start | bytes 393224 | tf_op jit(solution)/shard_map/ppermute | solution.py:593
  90.6 2.2 %collective-permute-start.23 = (bf16[64,1024]{1,0:T(8,128)(2,1)S(1)}, bf16[64,1024]{1,0:T(8,128)(2,1)S(1)}, u32[]{:S(2)}, u32[]{:S(2)}) collective-permute-start(bf16[64,1024]{1,0:T(8,128)(2,1)S(1)} %get-tuple-element.51), channel_id=1, source_target_pairs={{0,6},{2,4},{4,2},{6,0},{8,14},{10,12},{12,10},{14,8},{16,22},{18,... | collective-permute-start | bytes 393224 | tf_op jit(solution)/shard_map/ppermute | solution.py:593
  92.8 2.0 %collective-permute-done.28.refs_1_ = bf16[64,1024]{1,0:T(8,128)(2,1)S(1)} collective-permute-done((bf16[64,1024]{1,0:T(8,128)(2,1)S(1)}, bf16[64,1024]{1,0:T(8,128)(2,1)S(1)}, u32[]{:S(2)}, u32[]{:S(2)}) %collective-permute-start.28) | collective-permute-done | bytes 131104 | tf_op jit(solution)/shard_map/ppermute | solution.py:593
  94.9 1.0 collective-permute-start.30
  95.9 0.4 collective-permute-done.21.refs_0_
  96.3 1.7 %collective-permute-done.22.refs_1_ = bf16[64,1024]{1,0:T(8,128)(2,1)S(1)} collective-permute-done((bf16[64,1024]{1,0:T(8,128)(2,1)S(1)}, bf16[64,1024]{1,0:T(8,128)(2,1)S(1)}, u32[]{:S(2)}, u32[]{:S(2)}) %collective-permute-start.22) | collective-permute-done | bytes 131104 | tf_op jit(solution)/shard_map/ppermute | solution.py:593
  98.0 4.2 %collective-permute-done.30.refs_3_ = bf16[64,1024]{1,0:T(8,128)(2,1)S(1)} collective-permute-done((bf16[64,1024]{1,0:T(8,128)(2,1)S(1)}, bf16[64,1024]{1,0:T(8,128)(2,1)S(1)}, u32[]{:S(2)}, u32[]{:S(2)}) %collective-permute-start.30) | collective-permute-done | bytes 131104 | tf_op jit(solution)/shard_map/ppermute | solution.py:593
  102.4 1.2 %collective-permute-done.31.received_ref = bf16[64,512]{1,0:T(8,128)(2,1)S(1)} collective-permute-done((bf16[64,512]{1,0:T(8,128)(2,1)S(1)}, bf16[64,512]{1,0:T(8,128)(2,1)S(1)}, u32[]{:S(2)}, u32[]{:S(2)}) %collective-permute-start.31) | collective-permute-done | bytes 65568 | tf_op jit(solution)/shard_map/ppermute | solution.py:599
  103.7 0.7 assemble.1
  (45 shorter events, 1.3 us)
Async XLA Ops:
  0.0 23.4 %collective-permute-start.14 = (bf16[1024,384]{1,0:T(8,128)(2,1)}, bf16[1024,384]{1,0:T(8,128)(2,1)S(1)}, u32[]{:S(2)}, u32[]{:S(2)}) collective-permute-start(bf16[1024,384]{1,0:T(8,128)(2,1)} %bitcast.5), channel_id=1, source_target_pairs={{0,8},{2,10},{4,12},{6,14},{8,0},{10,2},{12,4},{14,6},{16,24},{18,... | collective-permute-start | bytes 2359304 | tf_op jit(solution)/shard_map/ppermute | solution.py:615
  5.0 18.5 %collective-permute-start.15 = (bf16[1024,384]{1,0:T(8,128)(2,1)}, bf16[1024,384]{1,0:T(8,128)(2,1)S(1)}, u32[]{:S(2)}, u32[]{:S(2)}) collective-permute-start(bf16[1024,384]{1,0:T(8,128)(2,1)} %bitcast.6), channel_id=1, source_target_pairs={{1,9},{3,11},{5,13},{7,15},{9,1},{11,3},{13,5},{15,7},{17,25},{19,... | collective-permute-start | bytes 2359304 | tf_op jit(solution)/shard_map/ppermute | solution.py:615
  23.5 46.2 %collective-permute-start.16 = (bf16[1024,384]{1,0:T(8,128)(2,1)S(1)}, bf16[1024,384]{1,0:T(8,128)(2,1)S(1)}, u32[]{:S(2)}, u32[]{:S(2)}) collective-permute-start(bf16[1024,384]{1,0:T(8,128)(2,1)S(1)} %merge.1.mine_ref), channel_id=1, source_target_pairs={{0,1},{1,0},{2,3},{3,2},{4,5},{5,4},{6,7},{7,6},{8,9},{9,8},{10,11... | collective-permute-start | bytes 2359304 | tf_op jit(solution)/shard_map/ppermute | solution.py:599
  24.5 9.5 %collective-permute-start.4 = (bf16[144,256]{1,0:T(8,128)(2,1)S(1)}, bf16[144,256]{1,0:T(8,128)(2,1)S(1)}, u32[]{:S(2)}, u32[]{:S(2)}) collective-permute-start(bf16[144,256]{1,0:T(8,128)(2,1)S(1)} %get-tuple-element.32.refs_0_), channel_id=1, source_target_pairs={{0,16},{2,18},{4,20},{6,22},{8,24},{10,26},{12,28},{14,30},{16,0},... | collective-permute-start | bytes 221192 | tf_op jit(solution)/shard_map/ppermute | solution.py:593
  27.3 6.3 %collective-permute-start.3 = (bf16[128,256]{1,0:T(8,128)(2,1)S(1)}, bf16[128,256]{1,0:T(8,128)(2,1)S(1)}, u32[]{:S(2)}, u32[]{:S(2)}) collective-permute-start(bf16[128,256]{1,0:T(8,128)(2,1)S(1)} %get-tuple-element.33), channel_id=1, source_target_pairs={{0,8},{2,10},{4,12},{6,14},{8,16},{10,18},{12,20},{14,22},{16,24},... | collective-permute-start | bytes 196616 | tf_op jit(solution)/shard_map/ppermute | solution.py:596
  30.8 3.2 %collective-permute-start.5 = (bf16[128,256]{1,0:T(8,128)(2,1)S(1)}, bf16[128,256]{1,0:T(8,128)(2,1)S(1)}, u32[]{:S(2)}, u32[]{:S(2)}) collective-permute-start(bf16[128,256]{1,0:T(8,128)(2,1)S(1)} %get-tuple-element.33), channel_id=1, source_target_pairs={{0,24},{2,26},{4,28},{6,30},{1,25},{3,27},{5,29},{7,31}} | collective-permute-start | bytes 196616 | tf_op jit(solution)/shard_map/ppermute | solution.py:596
  32.1 5.5 %collective-permute-start = (bf16[144,256]{1,0:T(8,128)(2,1)S(1)}, bf16[144,256]{1,0:T(8,128)(2,1)S(1)}, u32[]{:S(2)}, u32[]{:S(2)}) collective-permute-start(bf16[144,256]{1,0:T(8,128)(2,1)S(1)} %get-tuple-element.32.refs_0_), channel_id=1, source_target_pairs={{0,2},{2,0},{4,6},{6,4},{8,10},{10,8},{12,14},{14,12},{16,18},{18,... | collective-permute-start | bytes 221192 | tf_op jit(solution)/shard_map/ppermute | solution.py:593
  34.0 21.6 %collective-permute-start.6 = (bf16[400,256]{1,0:T(8,128)(2,1)S(1)}, bf16[400,256]{1,0:T(8,128)(2,1)S(1)}, u32[]{:S(2)}, u32[]{:S(2)}) collective-permute-start(bf16[400,256]{1,0:T(8,128)(2,1)S(1)} %join.1.refs_4_), channel_id=1, source_target_pairs={{0,2},{2,0},{4,6},{6,4},{8,10},{10,8},{12,14},{14,12},{16,18},{18,... | collective-permute-start | bytes 614408 | tf_op jit(solution)/shard_map/ppermute | solution.py:593
  35.5 20.1 %collective-permute-start.7 = (bf16[400,256]{1,0:T(8,128)(2,1)S(1)}, bf16[400,256]{1,0:T(8,128)(2,1)S(1)}, u32[]{:S(2)}, u32[]{:S(2)}) collective-permute-start(bf16[400,256]{1,0:T(8,128)(2,1)S(1)} %join.1.refs_4_), channel_id=1, source_target_pairs={{0,4},{2,6},{4,0},{6,2},{8,12},{10,14},{12,8},{14,10},{16,20},{18,... | collective-permute-start | bytes 614408 | tf_op jit(solution)/shard_map/ppermute | solution.py:593
  37.0 10.5 %collective-permute-start.1 = (bf16[144,256]{1,0:T(8,128)(2,1)S(1)}, bf16[144,256]{1,0:T(8,128)(2,1)S(1)}, u32[]{:S(2)}, u32[]{:S(2)}) collective-permute-start(bf16[144,256]{1,0:T(8,128)(2,1)S(1)} %get-tuple-element.32.refs_0_), channel_id=1, source_target_pairs={{0,4},{2,6},{4,0},{6,2},{8,12},{10,14},{12,8},{14,10},{16,20},{18,... | collective-permute-start | bytes 221192 | tf_op jit(solution)/shard_map/ppermute | solution.py:593
  37.6 18.2 %collective-permute-start.8 = (bf16[400,256]{1,0:T(8,128)(2,1)S(1)}, bf16[400,256]{1,0:T(8,128)(2,1)S(1)}, u32[]{:S(2)}, u32[]{:S(2)}) collective-permute-start(bf16[400,256]{1,0:T(8,128)(2,1)S(1)} %join.1.refs_4_), channel_id=1, source_target_pairs={{0,6},{2,4},{4,2},{6,0},{8,14},{10,12},{12,10},{14,8},{16,22},{18,... | collective-permute-start | bytes 614408 | tf_op jit(solution)/shard_map/ppermute | solution.py:593
  47.6 5.3 %collective-permute-start.2 = (bf16[144,256]{1,0:T(8,128)(2,1)S(1)}, bf16[144,256]{1,0:T(8,128)(2,1)S(1)}, u32[]{:S(2)}, u32[]{:S(2)}) collective-permute-start(bf16[144,256]{1,0:T(8,128)(2,1)S(1)} %get-tuple-element.32.refs_0_), channel_id=1, source_target_pairs={{0,6},{2,4},{4,2},{6,0},{8,14},{10,12},{12,10},{14,8},{16,22},{18,... | collective-permute-start | bytes 221192 | tf_op jit(solution)/shard_map/ppermute | solution.py:593
  52.8 2.9 %copy-start.1 = (bf16[1024,1024]{1,0:T(8,128)(2,1)S(1)}, bf16[1024,1024]{1,0:T(8,128)(2,1)}, u32[]{:S(2)}) copy-start(bf16[1024,1024]{1,0:T(8,128)(2,1)} %refs_0_.1) | copy-start | bytes 6291460
  52.8 8.8 %collective-permute-start.19 = (bf16[128,1024]{1,0:T(8,128)(2,1)S(1)}, bf16[128,1024]{1,0:T(8,128)(2,1)S(1)}, u32[]{:S(2)}, u32[]{:S(2)}) collective-permute-start(bf16[128,1024]{1,0:T(8,128)(2,1)S(1)} %get-tuple-element.47), channel_id=1, source_target_pairs={{0,8},{2,10},{4,12},{6,14},{8,0},{10,2},{12,4},{14,6},{16,24},{18,... | collective-permute-start | bytes 786440 | tf_op jit(solution)/shard_map/ppermute | solution.py:593
  55.8 5.1 %copy-start.4 = (bf16[128,1024]{1,0:T(8,128)(2,1)S(1)}, bf16[128,1024]{1,0:T(8,128)(2,1)}, u32[]{:S(2)}) copy-start(bf16[128,1024]{1,0:T(8,128)(2,1)} %hidden_ref.1) | copy-start | bytes 786436
  55.8 5.1 %copy-start.5 = (f32[1024]{0:T(1024)S(1)}, f32[1024]{0:T(1024)}, u32[]{:S(2)}) copy-start(f32[1024]{0:T(1024)} %param.16) | copy-start | bytes 12292
  56.7 13.4 %copy-start.2 = (bf16[1,1024,384]{2,1,0:T(8,128)(2,1)S(1)}, bf16[1,1024,384]{2,1,0:T(8,128)(2,1)}, u32[]{:S(2)}) copy-start(bf16[1,1024,384]{2,1,0:T(8,128)(2,1)} %gate_ref.1) | copy-start | bytes 2359300
  56.7 13.4 %copy-start.3 = (bf16[1,1024,384]{2,1,0:T(8,128)(2,1)S(1)}, bf16[1,1024,384]{2,1,0:T(8,128)(2,1)}, u32[]{:S(2)}) copy-start(bf16[1,1024,384]{2,1,0:T(8,128)(2,1)} %up_ref.1) | copy-start | bytes 2359300
  56.7 4.1 %collective-permute-start.9 = (bf16[64,1024]{1,0:T(8,128)(2,1)S(1)}, bf16[64,1024]{1,0:T(8,128)(2,1)S(1)}, u32[]{:S(2)}, u32[]{:S(2)}) collective-permute-start(bf16[64,1024]{1,0:T(8,128)(2,1)S(1)} %get-tuple-element.41), channel_id=1, source_target_pairs={{0,1},{1,0},{2,3},{3,2},{4,5},{5,4},{6,7},{7,6},{8,9},{9,8},{10,11... | collective-permute-start | bytes 393224 | tf_op jit(solution)/shard_map/ppermute | solution.py:599
  56.8 10.0 %collective-permute-start.17 = (bf16[64,1024]{1,0:T(8,128)(2,1)S(1)}, bf16[64,1024]{1,0:T(8,128)(2,1)S(1)}, u32[]{:S(2)}, u32[]{:S(2)}) collective-permute-start(bf16[64,1024]{1,0:T(8,128)(2,1)S(1)} %get-tuple-element.46), channel_id=1, source_target_pairs={{0,8},{2,10},{4,12},{6,14},{8,0},{10,2},{12,4},{14,6},{16,24},{18,... | collective-permute-start | bytes 393224 | tf_op jit(solution)/shard_map/ppermute | solution.py:593
  61.0 7.3 %collective-permute-start.10 = (bf16[64,1024]{1,0:T(8,128)(2,1)S(1)}, bf16[64,1024]{1,0:T(8,128)(2,1)S(1)}, u32[]{:S(2)}, u32[]{:S(2)}) collective-permute-start(bf16[64,1024]{1,0:T(8,128)(2,1)S(1)} %get-tuple-element.43.refs_0_), channel_id=1, source_target_pairs={{0,2},{2,0},{4,6},{6,4},{8,10},{10,8},{12,14},{14,12},{16,18},{18,... | collective-permute-start | bytes 393224 | tf_op jit(solution)/shard_map/ppermute | solution.py:593
  61.6 17.8 %collective-permute-start.20 = (bf16[128,1024]{1,0:T(8,128)(2,1)S(1)}, bf16[128,1024]{1,0:T(8,128)(2,1)S(1)}, u32[]{:S(2)}, u32[]{:S(2)}) collective-permute-start(bf16[128,1024]{1,0:T(8,128)(2,1)S(1)} %collective-permute-done.19.refs_2_), channel_id=1, source_target_pairs={{0,1},{1,0},{2,3},{3,2},{4,5},{5,4},{6,7},{7,6},{8,9},{9,8},{10,11... | collective-permute-start | bytes 786440 | tf_op jit(solution)/shard_map/ppermute | solution.py:599
  61.6 12.1 %collective-permute-start.13 = (bf16[64,1024]{1,0:T(8,128)(2,1)S(1)}, bf16[64,1024]{1,0:T(8,128)(2,1)S(1)}, u32[]{:S(2)}, u32[]{:S(2)}) collective-permute-start(bf16[64,1024]{1,0:T(8,128)(2,1)S(1)} %get-tuple-element.43.refs_0_), channel_id=1, source_target_pairs={{0,16},{2,18},{4,20},{6,22},{8,24},{10,26},{12,28},{14,30},{16,0},... | collective-permute-start | bytes 393224 | tf_op jit(solution)/shard_map/ppermute | solution.py:593
  66.8 8.5 %collective-permute-start.11 = (bf16[64,1024]{1,0:T(8,128)(2,1)S(1)}, bf16[64,1024]{1,0:T(8,128)(2,1)S(1)}, u32[]{:S(2)}, u32[]{:S(2)}) collective-permute-start(bf16[64,1024]{1,0:T(8,128)(2,1)S(1)} %get-tuple-element.43.refs_0_), channel_id=1, source_target_pairs={{0,4},{2,6},{4,0},{6,2},{8,12},{10,14},{12,8},{14,10},{16,20},{18,... | collective-permute-start | bytes 393224 | tf_op jit(solution)/shard_map/ppermute | solution.py:593
  68.3 8.5 %collective-permute-start.12 = (bf16[64,1024]{1,0:T(8,128)(2,1)S(1)}, bf16[64,1024]{1,0:T(8,128)(2,1)S(1)}, u32[]{:S(2)}, u32[]{:S(2)}) collective-permute-start(bf16[64,1024]{1,0:T(8,128)(2,1)S(1)} %get-tuple-element.43.refs_0_), channel_id=1, source_target_pairs={{0,6},{2,4},{4,2},{6,0},{8,14},{10,12},{12,10},{14,8},{16,22},{18,... | collective-permute-start | bytes 393224 | tf_op jit(solution)/shard_map/ppermute | solution.py:593
  69.7 9.7 %collective-permute-start.18 = (bf16[64,1024]{1,0:T(8,128)(2,1)S(1)}, bf16[64,1024]{1,0:T(8,128)(2,1)S(1)}, u32[]{:S(2)}, u32[]{:S(2)}) collective-permute-start(bf16[64,1024]{1,0:T(8,128)(2,1)S(1)} %collective-permute-done.17.refs_0_), channel_id=1, source_target_pairs={{0,1},{1,0},{2,3},{3,2},{4,5},{5,4},{6,7},{7,6},{8,9},{9,8},{10,11... | collective-permute-start | bytes 393224 | tf_op jit(solution)/shard_map/ppermute | solution.py:599
  73.7 6.9 %collective-permute-start.24 = (bf16[64,1024]{1,0:T(8,128)(2,1)S(1)}, bf16[64,1024]{1,0:T(8,128)(2,1)S(1)}, u32[]{:S(2)}, u32[]{:S(2)}) collective-permute-start(bf16[64,1024]{1,0:T(8,128)(2,1)S(1)} %collective-permute-done.13.refs_4_), channel_id=1, source_target_pairs={{0,2},{2,0},{4,6},{6,4},{8,10},{10,8},{12,14},{14,12},{16,18},{18,... | collective-permute-start | bytes 393224 | tf_op jit(solution)/shard_map/ppermute | solution.py:593
  75.2 7.9 %collective-permute-start.25 = (bf16[64,1024]{1,0:T(8,128)(2,1)S(1)}, bf16[64,1024]{1,0:T(8,128)(2,1)S(1)}, u32[]{:S(2)}, u32[]{:S(2)}) collective-permute-start(bf16[64,1024]{1,0:T(8,128)(2,1)S(1)} %collective-permute-done.13.refs_4_), channel_id=1, source_target_pairs={{0,4},{2,6},{4,0},{6,2},{8,12},{10,14},{12,8},{14,10},{16,20},{18,... | collective-permute-start | bytes 393224 | tf_op jit(solution)/shard_map/ppermute | solution.py:593
  76.7 6.3 %collective-permute-start.26 = (bf16[64,1024]{1,0:T(8,128)(2,1)S(1)}, bf16[64,1024]{1,0:T(8,128)(2,1)S(1)}, u32[]{:S(2)}, u32[]{:S(2)}) collective-permute-start(bf16[64,1024]{1,0:T(8,128)(2,1)S(1)} %collective-permute-done.13.refs_4_), channel_id=1, source_target_pairs={{0,6},{2,4},{4,2},{6,0},{8,14},{10,12},{12,10},{14,8},{16,22},{18,... | collective-permute-start | bytes 393224 | tf_op jit(solution)/shard_map/ppermute | solution.py:593
  78.2 1.3 %copy-start = (bf16[1,384,1024]{2,1,0:T(8,128)(2,1)S(1)}, bf16[1,384,1024]{2,1,0:T(8,128)(2,1)}, u32[]{:S(2)}) copy-start(bf16[1,384,1024]{2,1,0:T(8,128)(2,1)} %down_ref.3) | copy-start | bytes 2359300
  84.2 6.3 %collective-permute-start.27 = (bf16[64,1024]{1,0:T(8,128)(2,1)S(1)}, bf16[64,1024]{1,0:T(8,128)(2,1)S(1)}, u32[]{:S(2)}, u32[]{:S(2)}) collective-permute-start(bf16[64,1024]{1,0:T(8,128)(2,1)S(1)} %get-tuple-element.54), channel_id=1, source_target_pairs={{0,2},{2,0},{4,6},{6,4},{8,10},{10,8},{12,14},{14,12},{16,18},{18,... | collective-permute-start | bytes 393224 | tf_op jit(solution)/shard_map/ppermute | solution.py:593
  85.7 9.1 %collective-permute-start.28 = (bf16[64,1024]{1,0:T(8,128)(2,1)S(1)}, bf16[64,1024]{1,0:T(8,128)(2,1)S(1)}, u32[]{:S(2)}, u32[]{:S(2)}) collective-permute-start(bf16[64,1024]{1,0:T(8,128)(2,1)S(1)} %get-tuple-element.55), channel_id=1, source_target_pairs={{0,4},{2,6},{4,0},{6,2},{8,12},{10,14},{12,8},{14,10},{16,20},{18,... | collective-permute-start | bytes 393224 | tf_op jit(solution)/shard_map/ppermute | solution.py:593
  87.0 7.8 %collective-permute-start.29 = (bf16[64,1024]{1,0:T(8,128)(2,1)S(1)}, bf16[64,1024]{1,0:T(8,128)(2,1)S(1)}, u32[]{:S(2)}, u32[]{:S(2)}) collective-permute-start(bf16[64,1024]{1,0:T(8,128)(2,1)S(1)} %get-tuple-element.56), channel_id=1, source_target_pairs={{0,6},{2,4},{4,2},{6,0},{8,14},{10,12},{12,10},{14,8},{16,22},{18,... | collective-permute-start | bytes 393224 | tf_op jit(solution)/shard_map/ppermute | solution.py:593
  87.8 8.5 %collective-permute-start.21 = (bf16[64,1024]{1,0:T(8,128)(2,1)S(1)}, bf16[64,1024]{1,0:T(8,128)(2,1)S(1)}, u32[]{:S(2)}, u32[]{:S(2)}) collective-permute-start(bf16[64,1024]{1,0:T(8,128)(2,1)S(1)} %get-tuple-element.49), channel_id=1, source_target_pairs={{0,2},{2,0},{4,6},{6,4},{8,10},{10,8},{12,14},{14,12},{16,18},{18,... | collective-permute-start | bytes 393224 | tf_op jit(solution)/shard_map/ppermute | solution.py:593
  89.2 8.9 %collective-permute-start.22 = (bf16[64,1024]{1,0:T(8,128)(2,1)S(1)}, bf16[64,1024]{1,0:T(8,128)(2,1)S(1)}, u32[]{:S(2)}, u32[]{:S(2)}) collective-permute-start(bf16[64,1024]{1,0:T(8,128)(2,1)S(1)} %get-tuple-element.50), channel_id=1, source_target_pairs={{0,4},{2,6},{4,0},{6,2},{8,12},{10,14},{12,8},{14,10},{16,20},{18,... | collective-permute-start | bytes 393224 | tf_op jit(solution)/shard_map/ppermute | solution.py:593
  90.6 7.5 %collective-permute-start.23 = (bf16[64,1024]{1,0:T(8,128)(2,1)S(1)}, bf16[64,1024]{1,0:T(8,128)(2,1)S(1)}, u32[]{:S(2)}, u32[]{:S(2)}) collective-permute-start(bf16[64,1024]{1,0:T(8,128)(2,1)S(1)} %get-tuple-element.51), channel_id=1, source_target_pairs={{0,6},{2,4},{4,2},{6,0},{8,14},{10,12},{12,10},{14,8},{16,22},{18,... | collective-permute-start | bytes 393224 | tf_op jit(solution)/shard_map/ppermute | solution.py:593
  94.9 7.3 %collective-permute-start.30 = (bf16[64,1024]{1,0:T(8,128)(2,1)S(1)}, bf16[64,1024]{1,0:T(8,128)(2,1)S(1)}, u32[]{:S(2)}, u32[]{:S(2)}) collective-permute-start(bf16[64,1024]{1,0:T(8,128)(2,1)S(1)} %gather_sum.1), channel_id=1, source_target_pairs={{0,16},{2,18},{4,20},{6,22},{8,24},{10,26},{12,28},{14,30},{16,0},... | collective-permute-start | bytes 393224 | tf_op jit(solution)/shard_map/ppermute | solution.py:593
  102.4 1.3 %collective-permute-start.31 = (bf16[64,512]{1,0:T(8,128)(2,1)S(1)}, bf16[64,512]{1,0:T(8,128)(2,1)S(1)}, u32[]{:S(2)}, u32[]{:S(2)}) collective-permute-start(bf16[64,512]{1,0:T(8,128)(2,1)S(1)} %get-tuple-element.58), channel_id=1, source_target_pairs={{0,1},{1,0},{2,3},{3,2},{4,5},{5,4},{6,7},{7,6},{8,9},{9,8},{10,11... | collective-permute-start | bytes 196616 | tf_op jit(solution)/shard_map/ppermute | solution.py:599

commit v5 on v4

--- a/solution.py
+++ b/solution.py
@@ -196,8 +196,7 @@
     peak = jnp.max(peak, axis=1, keepdims=True)
     if state is not None:
         peak = jnp.maximum(peak, state[0][:, :1])
-    shift = peak * scale
-    weights = [jnp.exp2(piece * scale - shift) for piece in pieces]
+    weights = [jnp.exp2((piece - peak) * scale) for piece in pieces]
     total = functools.reduce(jnp.add, weights)
     product = jnp.dot(
         jnp.concatenate([w.astype(jnp.bfloat16) for w in weights], axis=1),
@@ -205,7 +204,7 @@
         preferred_element_type=jnp.float32,
     )
     if state is not None:
-        factor = jnp.exp2(state[0][:, :1] * scale - shift)
+        factor = jnp.exp2((state[0][:, :1] - peak) * scale)
         total = total + state[1] * factor
         product = product + state[2] * factor
     return peak, total, product

time: 105 us -> 104 us (level)
  no operation moved by 1% of the time
where the time goes in v5:
time: 104 us
  starting transfers between devices  49.7 us (48%)
  waiting for transfers between devices  42.7 us (41%)
  Pallas kernels  11.2 us (11%)
    ppermute x23, starting transfers between devices, flip(): return lax.ppermute(value, 'ctx', [(i, i ^ mask) for i in range(ctx)])  39.1 us
    ppermute x23, waiting for transfers between devices, flip(): return lax.ppermute(value, 'ctx', [(i, i ^ mask) for i in range(ctx)])  23.4 us
    ppermute x2, waiting for transfers between devices, half_flip(): return lax.ppermute(value, ('ctx', 'exp'), pairs)  17.7 us
    ppermute x2, starting transfers between devices, half_flip(): return lax.ppermute(value, ('ctx', 'exp'), pairs)  5.66 us
    ppermute x2, starting transfers between devices, upward(): lax.ppermute(value, 'ctx', [(i, i + step) for i in range(ctx - step)])  4.76 us
  transfers between devices with their start and end apart: 32, of which 12 were waited for; matrix products, arithmetic and copies ran while one was open for 0% of the time, Pallas kernels for 9%

profile of v5, /device:TPU:0, one launch (start us, length us, event | category | flops | bytes accessed | tf_op | source)
XLA Modules:
  0.0 103.9 jit_solution(12371397858270930723)
XLA Ops:
  0.0 5.0 %collective-permute-start.14 = (bf16[1024,384]{1,0:T(8,128)(2,1)}, bf16[1024,384]{1,0:T(8,128)(2,1)S(1)}, u32[]{:S(2)}, u32[]{:S(2)}) collective-permute-start(bf16[1024,384]{1,0:T(8,128)(2,1)} %bitcast.5), channel_id=1, source_target_pairs={{0,8},{2,10},{4,12},{6,14},{8,0},{10,2},{12,4},{14,6},{16,24},{18,... | collective-permute-start | bytes 2359304 | tf_op jit(solution)/shard_map/ppermute | solution.py:614
  5.0 0.7 collective-permute-start.15
  5.7 17.7 %collective-permute-done.14.first_ref = bf16[1024,384]{1,0:T(8,128)(2,1)S(1)} collective-permute-done((bf16[1024,384]{1,0:T(8,128)(2,1)}, bf16[1024,384]{1,0:T(8,128)(2,1)S(1)}, u32[]{:S(2)}, u32[]{:S(2)}) %collective-permute-start.14) | collective-permute-done | bytes 786464 | tf_op jit(solution)/shard_map/ppermute | solution.py:614
  23.6 0.8 pack.1
  24.5 2.8 %collective-permute-start.4 = (bf16[144,256]{1,0:T(8,128)(2,1)S(1)}, bf16[144,256]{1,0:T(8,128)(2,1)S(1)}, u32[]{:S(2)}, u32[]{:S(2)}) collective-permute-start(bf16[144,256]{1,0:T(8,128)(2,1)S(1)} %get-tuple-element.32.refs_0_), channel_id=1, source_target_pairs={{0,16},{2,18},{4,20},{6,22},{8,24},{10,26},{12,28},{14,30},{16,0},... | collective-permute-start | bytes 221192 | tf_op jit(solution)/shard_map/ppermute | solution.py:592
  27.3 3.5 %collective-permute-start.3 = (bf16[128,256]{1,0:T(8,128)(2,1)S(1)}, bf16[128,256]{1,0:T(8,128)(2,1)S(1)}, u32[]{:S(2)}, u32[]{:S(2)}) collective-permute-start(bf16[128,256]{1,0:T(8,128)(2,1)S(1)} %get-tuple-element.33), channel_id=1, source_target_pairs={{0,8},{2,10},{4,12},{6,14},{8,16},{10,18},{12,20},{14,22},{16,24},... | collective-permute-start | bytes 196616 | tf_op jit(solution)/shard_map/ppermute | solution.py:595
  30.8 1.3 %collective-permute-start.5 = (bf16[128,256]{1,0:T(8,128)(2,1)S(1)}, bf16[128,256]{1,0:T(8,128)(2,1)S(1)}, u32[]{:S(2)}, u32[]{:S(2)}) collective-permute-start(bf16[128,256]{1,0:T(8,128)(2,1)S(1)} %get-tuple-element.33), channel_id=1, source_target_pairs={{0,24},{2,26},{4,28},{6,30},{1,25},{3,27},{5,29},{7,31}} | collective-permute-start | bytes 196616 | tf_op jit(solution)/shard_map/ppermute | solution.py:595
  32.1 1.6 %collective-permute-start = (bf16[144,256]{1,0:T(8,128)(2,1)S(1)}, bf16[144,256]{1,0:T(8,128)(2,1)S(1)}, u32[]{:S(2)}, u32[]{:S(2)}) collective-permute-start(bf16[144,256]{1,0:T(8,128)(2,1)S(1)} %get-tuple-element.32.refs_0_), channel_id=1, source_target_pairs={{0,2},{2,0},{4,6},{6,4},{8,10},{10,8},{12,14},{14,12},{16,18},{18,... | collective-permute-start | bytes 221192 | tf_op jit(solution)/shard_map/ppermute | solution.py:592
  34.0 1.6 %collective-permute-start.6 = (bf16[400,256]{1,0:T(8,128)(2,1)S(1)}, bf16[400,256]{1,0:T(8,128)(2,1)S(1)}, u32[]{:S(2)}, u32[]{:S(2)}) collective-permute-start(bf16[400,256]{1,0:T(8,128)(2,1)S(1)} %join.1.refs_4_), channel_id=1, source_target_pairs={{0,2},{2,0},{4,6},{6,4},{8,10},{10,8},{12,14},{14,12},{16,18},{18,... | collective-permute-start | bytes 614408 | tf_op jit(solution)/shard_map/ppermute | solution.py:592
  35.5 1.5 %collective-permute-start.7 = (bf16[400,256]{1,0:T(8,128)(2,1)S(1)}, bf16[400,256]{1,0:T(8,128)(2,1)S(1)}, u32[]{:S(2)}, u32[]{:S(2)}) collective-permute-start(bf16[400,256]{1,0:T(8,128)(2,1)S(1)} %join.1.refs_4_), channel_id=1, source_target_pairs={{0,4},{2,6},{4,0},{6,2},{8,12},{10,14},{12,8},{14,10},{16,20},{18,... | collective-permute-start | bytes 614408 | tf_op jit(solution)/shard_map/ppermute | solution.py:592
  37.0 0.5 collective-permute-start.1
  37.6 1.8 %collective-permute-start.8 = (bf16[400,256]{1,0:T(8,128)(2,1)S(1)}, bf16[400,256]{1,0:T(8,128)(2,1)S(1)}, u32[]{:S(2)}, u32[]{:S(2)}) collective-permute-start(bf16[400,256]{1,0:T(8,128)(2,1)S(1)} %join.1.refs_4_), channel_id=1, source_target_pairs={{0,6},{2,4},{4,2},{6,0},{8,14},{10,12},{12,10},{14,8},{16,22},{18,... | collective-permute-start | bytes 614408 | tf_op jit(solution)/shard_map/ppermute | solution.py:592
  39.4 8.2 %collective-permute-done.1.refs_2_ = bf16[144,256]{1,0:T(8,128)(2,1)S(1)} collective-permute-done((bf16[144,256]{1,0:T(8,128)(2,1)S(1)}, bf16[144,256]{1,0:T(8,128)(2,1)S(1)}, u32[]{:S(2)}, u32[]{:S(2)}) %collective-permute-start.1) | collective-permute-done | bytes 73760 | tf_op jit(solution)/shard_map/ppermute | solution.py:592
  47.6 2.3 %collective-permute-start.2 = (bf16[144,256]{1,0:T(8,128)(2,1)S(1)}, bf16[144,256]{1,0:T(8,128)(2,1)S(1)}, u32[]{:S(2)}, u32[]{:S(2)}) collective-permute-start(bf16[144,256]{1,0:T(8,128)(2,1)S(1)} %get-tuple-element.32.refs_0_), channel_id=1, source_target_pairs={{0,6},{2,4},{4,2},{6,0},{8,14},{10,12},{12,10},{14,8},{16,22},{18,... | collective-permute-start | bytes 221192 | tf_op jit(solution)/shard_map/ppermute | solution.py:592
  49.9 1.0 cut.1
  50.9 0.9 turn.1.heads_ref.query_ref
  51.9 1.0 collective-permute-done.2.refs_3_
  52.8 0.7 collective-permute-start.19
  53.6 2.0 %near.1 = (f32[1024,128]{1,0:T(8,128)S(1)}, f32[1024,128]{1,0:T(8,128)S(1)}, f32[1024,128]{1,0:T(8,128)S(1)}) custom-call(bf16[1024,128]{1,0:T(8,128)(2,1)S(1)} %turn.1.heads_ref.query_ref, bf16[144,256]{1,0:T(8,128)(2,1)S(1)} %get-tuple-element.32.refs_0_, bf16[144,256]{1,0:T(8,128)(2,1)S(1)} %collective-permute-done.refs_1_, ...), custom_call_target="tpu_custom_call" | custom-call | flops 469762048 | bytes 4000000 | tf_op jit(solution)/shard_map/near/pallas_call | solution.py:266
  55.7 0.9 far.1
  56.7 3.9 %collective-permute-start.17 = (bf16[64,1024]{1,0:T(8,128)(2,1)S(1)}, bf16[64,1024]{1,0:T(8,128)(2,1)S(1)}, u32[]{:S(2)}, u32[]{:S(2)}) collective-permute-start(bf16[64,1024]{1,0:T(8,128)(2,1)S(1)} %get-tuple-element.46), channel_id=1, source_target_pairs={{0,8},{2,10},{4,12},{6,14},{8,0},{10,2},{12,4},{14,6},{16,24},{18,... | collective-permute-start | bytes 393224 | tf_op jit(solution)/shard_map/ppermute | solution.py:592
  60.8 0.6 collective-permute-start.10
  61.4 5.0 %collective-permute-start.13 = (bf16[64,1024]{1,0:T(8,128)(2,1)S(1)}, bf16[64,1024]{1,0:T(8,128)(2,1)S(1)}, u32[]{:S(2)}, u32[]{:S(2)}) collective-permute-start(bf16[64,1024]{1,0:T(8,128)(2,1)S(1)} %get-tuple-element.43.refs_0_), channel_id=1, source_target_pairs={{0,16},{2,18},{4,20},{6,22},{8,24},{10,26},{12,28},{14,30},{16,0},... | collective-permute-start | bytes 393224 | tf_op jit(solution)/shard_map/ppermute | solution.py:592
  66.3 1.5 %collective-permute-start.11 = (bf16[64,1024]{1,0:T(8,128)(2,1)S(1)}, bf16[64,1024]{1,0:T(8,128)(2,1)S(1)}, u32[]{:S(2)}, u32[]{:S(2)}) collective-permute-start(bf16[64,1024]{1,0:T(8,128)(2,1)S(1)} %get-tuple-element.43.refs_0_), channel_id=1, source_target_pairs={{0,4},{2,6},{4,0},{6,2},{8,12},{10,14},{12,8},{14,10},{16,20},{18,... | collective-permute-start | bytes 393224 | tf_op jit(solution)/shard_map/ppermute | solution.py:592
  67.9 1.4 %collective-permute-start.12 = (bf16[64,1024]{1,0:T(8,128)(2,1)S(1)}, bf16[64,1024]{1,0:T(8,128)(2,1)S(1)}, u32[]{:S(2)}, u32[]{:S(2)}) collective-permute-start(bf16[64,1024]{1,0:T(8,128)(2,1)S(1)} %get-tuple-element.43.refs_0_), channel_id=1, source_target_pairs={{0,6},{2,4},{4,2},{6,0},{8,14},{10,12},{12,10},{14,8},{16,22},{18,... | collective-permute-start | bytes 393224 | tf_op jit(solution)/shard_map/ppermute | solution.py:592
  69.3 0.4 columns.1.share_ref
  69.7 0.4 stack.1
  70.1 3.2 %collective-permute-done.13.refs_4_ = bf16[64,1024]{1,0:T(8,128)(2,1)S(1)} collective-permute-done((bf16[64,1024]{1,0:T(8,128)(2,1)S(1)}, bf16[64,1024]{1,0:T(8,128)(2,1)S(1)}, u32[]{:S(2)}, u32[]{:S(2)}) %collective-permute-start.13) | collective-permute-done | bytes 131104 | tf_op jit(solution)/shard_map/ppermute | solution.py:592
  73.3 1.5 %collective-permute-start.24 = (bf16[64,1024]{1,0:T(8,128)(2,1)S(1)}, bf16[64,1024]{1,0:T(8,128)(2,1)S(1)}, u32[]{:S(2)}, u32[]{:S(2)}) collective-permute-start(bf16[64,1024]{1,0:T(8,128)(2,1)S(1)} %collective-permute-done.13.refs_4_), channel_id=1, source_target_pairs={{0,2},{2,0},{4,6},{6,4},{8,10},{10,8},{12,14},{14,12},{16,18},{18,... | collective-permute-start | bytes 393224 | tf_op jit(solution)/shard_map/ppermute | solution.py:592
  74.8 1.5 %collective-permute-start.25 = (bf16[64,1024]{1,0:T(8,128)(2,1)S(1)}, bf16[64,1024]{1,0:T(8,128)(2,1)S(1)}, u32[]{:S(2)}, u32[]{:S(2)}) collective-permute-start(bf16[64,1024]{1,0:T(8,128)(2,1)S(1)} %collective-permute-done.13.refs_4_), channel_id=1, source_target_pairs={{0,4},{2,6},{4,0},{6,2},{8,12},{10,14},{12,8},{14,10},{16,20},{18,... | collective-permute-start | bytes 393224 | tf_op jit(solution)/shard_map/ppermute | solution.py:592
  76.3 1.4 %collective-permute-start.26 = (bf16[64,1024]{1,0:T(8,128)(2,1)S(1)}, bf16[64,1024]{1,0:T(8,128)(2,1)S(1)}, u32[]{:S(2)}, u32[]{:S(2)}) collective-permute-start(bf16[64,1024]{1,0:T(8,128)(2,1)S(1)} %collective-permute-done.13.refs_4_), channel_id=1, source_target_pairs={{0,6},{2,4},{4,2},{6,0},{8,14},{10,12},{12,10},{14,8},{16,22},{18,... | collective-permute-start | bytes 393224 | tf_op jit(solution)/shard_map/ppermute | solution.py:592
  77.7 1.2 %expand.1.hidden_ref = bf16[320,768]{1,0:T(8,128)(2,1)S(1)} custom-call(f32[512,128]{1,0:T(8,128)S(1)} %columns.1.share_ref, bf16[64,1024]{1,0:T(8,128)(2,1)S(1)} %get-tuple-element.43.refs_0_, bf16[64,1024]{1,0:T(8,128)(2,1)S(1)} %collective-permute-done.10.refs_1_, bf16[64,1024]{1,0:T(8,128)(2,1)S(1)} %collective-permute-done.11.refs_2_, ...), custom_call_target="tpu_custom_call" | custom-call | flops 1006632960 | bytes 3145728 | tf_op jit(solution)/shard_map/expand/pallas_call | solution.py:471
  79.0 1.2 %contract.1 = (f32[64,1024]{1,0:T(8,128)S(1)}, bf16[64,1024]{1,0:T(8,128)(2,1)S(1)}, bf16[64,1024]{1,0:T(8,128)(2,1)S(1)}, bf16[64,1024]{1,0:T(8,128)(2,1)S(1)},...) custom-call(bf16[320,768]{1,0:T(8,128)(2,1)S(1)} %expand.1.hidden_ref, bf16[1,384,1024]{2,1,0:T(8,128)(2,1)S(1)} %copy-done, ...), custom_call_target="tpu_custom_call" | custom-call | flops 503316480 | bytes 1572864 | tf_op jit(solution)/shard_map/contract/pallas_call | solution.py:504
  80.2 2.5 %collective-permute-done.25.refs_1_ = bf16[64,1024]{1,0:T(8,128)(2,1)S(1)} collective-permute-done((bf16[64,1024]{1,0:T(8,128)(2,1)S(1)}, bf16[64,1024]{1,0:T(8,128)(2,1)S(1)}, u32[]{:S(2)}, u32[]{:S(2)}) %collective-permute-start.25) | collective-permute-done | bytes 131104 | tf_op jit(solution)/shard_map/ppermute | solution.py:592
  82.7 1.2 %experts_far.1 = (bf16[64,1024]{1,0:T(8,128)(2,1)S(1)}, bf16[64,1024]{1,0:T(8,128)(2,1)S(1)}, bf16[64,1024]{1,0:T(8,128)(2,1)S(1)}) custom-call(f32[512,128]{1,0:T(8,128)S(1)} %columns.1.share_ref, bf16[64,1024]{1,0:T(8,128)(2,1)S(1)} %collective-permute-done.24.refs_0_, bf16[64,1024]{1,0:T(8,128)(2,1)S(1)} %collective-permute-done.25.refs_1_, ...), custom_call_target="tpu_custom_call" | custom-call | flops 905969664 | bytes 4718592 | tf_op jit(solution)/shard_map/experts_far/pallas_call | solution.py:528
  83.8 1.4 %collective-permute-start.27 = (bf16[64,1024]{1,0:T(8,128)(2,1)S(1)}, bf16[64,1024]{1,0:T(8,128)(2,1)S(1)}, u32[]{:S(2)}, u32[]{:S(2)}) collective-permute-start(bf16[64,1024]{1,0:T(8,128)(2,1)S(1)} %get-tuple-element.54), channel_id=1, source_target_pairs={{0,2},{2,0},{4,6},{6,4},{8,10},{10,8},{12,14},{14,12},{16,18},{18,... | collective-permute-start | bytes 393224 | tf_op jit(solution)/shard_map/ppermute | solution.py:592
  85.3 1.3 %collective-permute-start.28 = (bf16[64,1024]{1,0:T(8,128)(2,1)S(1)}, bf16[64,1024]{1,0:T(8,128)(2,1)S(1)}, u32[]{:S(2)}, u32[]{:S(2)}) collective-permute-start(bf16[64,1024]{1,0:T(8,128)(2,1)S(1)} %get-tuple-element.55), channel_id=1, source_target_pairs={{0,4},{2,6},{4,0},{6,2},{8,12},{10,14},{12,8},{14,10},{16,20},{18,... | collective-permute-start | bytes 393224 | tf_op jit(solution)/shard_map/ppermute | solution.py:592
  86.6 0.8 collective-permute-start.29
  87.4 1.4 %collective-permute-start.21 = (bf16[64,1024]{1,0:T(8,128)(2,1)S(1)}, bf16[64,1024]{1,0:T(8,128)(2,1)S(1)}, u32[]{:S(2)}, u32[]{:S(2)}) collective-permute-start(bf16[64,1024]{1,0:T(8,128)(2,1)S(1)} %get-tuple-element.49), channel_id=1, source_target_pairs={{0,2},{2,0},{4,6},{6,4},{8,10},{10,8},{12,14},{14,12},{16,18},{18,... | collective-permute-start | bytes 393224 | tf_op jit(solution)/shard_map/ppermute | solution.py:592
  88.8 1.3 %collective-permute-start.22 = (bf16[64,1024]{1,0:T(8,128)(2,1)S(1)}, bf16[64,1024]{1,0:T(8,128)(2,1)S(1)}, u32[]{:S(2)}, u32[]{:S(2)}) collective-permute-start(bf16[64,1024]{1,0:T(8,128)(2,1)S(1)} %get-tuple-element.50), channel_id=1, source_target_pairs={{0,4},{2,6},{4,0},{6,2},{8,12},{10,14},{12,8},{14,10},{16,20},{18,... | collective-permute-start | bytes 393224 | tf_op jit(solution)/shard_map/ppermute | solution.py:592
  90.2 2.2 %collective-permute-start.23 = (bf16[64,1024]{1,0:T(8,128)(2,1)S(1)}, bf16[64,1024]{1,0:T(8,128)(2,1)S(1)}, u32[]{:S(2)}, u32[]{:S(2)}) collective-permute-start(bf16[64,1024]{1,0:T(8,128)(2,1)S(1)} %get-tuple-element.51), channel_id=1, source_target_pairs={{0,6},{2,4},{4,2},{6,0},{8,14},{10,12},{12,10},{14,8},{16,22},{18,... | collective-permute-start | bytes 393224 | tf_op jit(solution)/shard_map/ppermute | solution.py:592
  92.4 2.0 %collective-permute-done.28.refs_1_ = bf16[64,1024]{1,0:T(8,128)(2,1)S(1)} collective-permute-done((bf16[64,1024]{1,0:T(8,128)(2,1)S(1)}, bf16[64,1024]{1,0:T(8,128)(2,1)S(1)}, u32[]{:S(2)}, u32[]{:S(2)}) %collective-permute-start.28) | collective-permute-done | bytes 131104 | tf_op jit(solution)/shard_map/ppermute | solution.py:592
  94.5 1.0 collective-permute-start.30
  95.4 0.4 collective-permute-done.21.refs_0_
  95.9 1.7 %collective-permute-done.22.refs_1_ = bf16[64,1024]{1,0:T(8,128)(2,1)S(1)} collective-permute-done((bf16[64,1024]{1,0:T(8,128)(2,1)S(1)}, bf16[64,1024]{1,0:T(8,128)(2,1)S(1)}, u32[]{:S(2)}, u32[]{:S(2)}) %collective-permute-start.22) | collective-permute-done | bytes 131104 | tf_op jit(solution)/shard_map/ppermute | solution.py:592
  97.6 4.2 %collective-permute-done.30.refs_3_ = bf16[64,1024]{1,0:T(8,128)(2,1)S(1)} collective-permute-done((bf16[64,1024]{1,0:T(8,128)(2,1)S(1)}, bf16[64,1024]{1,0:T(8,128)(2,1)S(1)}, u32[]{:S(2)}, u32[]{:S(2)}) %collective-permute-start.30) | collective-permute-done | bytes 131104 | tf_op jit(solution)/shard_map/ppermute | solution.py:592
  102.0 1.2 %collective-permute-done.31.received_ref = bf16[64,512]{1,0:T(8,128)(2,1)S(1)} collective-permute-done((bf16[64,512]{1,0:T(8,128)(2,1)S(1)}, bf16[64,512]{1,0:T(8,128)(2,1)S(1)}, u32[]{:S(2)}, u32[]{:S(2)}) %collective-permute-start.31) | collective-permute-done | bytes 65568 | tf_op jit(solution)/shard_map/ppermute | solution.py:598
  103.3 0.7 assemble.1
  (45 shorter events, 1.3 us)
Async XLA Ops:
  0.0 23.4 %collective-permute-start.14 = (bf16[1024,384]{1,0:T(8,128)(2,1)}, bf16[1024,384]{1,0:T(8,128)(2,1)S(1)}, u32[]{:S(2)}, u32[]{:S(2)}) collective-permute-start(bf16[1024,384]{1,0:T(8,128)(2,1)} %bitcast.5), channel_id=1, source_target_pairs={{0,8},{2,10},{4,12},{6,14},{8,0},{10,2},{12,4},{14,6},{16,24},{18,... | collective-permute-start | bytes 2359304 | tf_op jit(solution)/shard_map/ppermute | solution.py:614
  5.0 18.5 %collective-permute-start.15 = (bf16[1024,384]{1,0:T(8,128)(2,1)}, bf16[1024,384]{1,0:T(8,128)(2,1)S(1)}, u32[]{:S(2)}, u32[]{:S(2)}) collective-permute-start(bf16[1024,384]{1,0:T(8,128)(2,1)} %bitcast.6), channel_id=1, source_target_pairs={{1,9},{3,11},{5,13},{7,15},{9,1},{11,3},{13,5},{15,7},{17,25},{19,... | collective-permute-start | bytes 2359304 | tf_op jit(solution)/shard_map/ppermute | solution.py:614
  23.5 45.8 %collective-permute-start.16 = (bf16[1024,384]{1,0:T(8,128)(2,1)S(1)}, bf16[1024,384]{1,0:T(8,128)(2,1)S(1)}, u32[]{:S(2)}, u32[]{:S(2)}) collective-permute-start(bf16[1024,384]{1,0:T(8,128)(2,1)S(1)} %merge.1.mine_ref), channel_id=1, source_target_pairs={{0,1},{1,0},{2,3},{3,2},{4,5},{5,4},{6,7},{7,6},{8,9},{9,8},{10,11... | collective-permute-start | bytes 2359304 | tf_op jit(solution)/shard_map/ppermute | solution.py:598
  24.5 9.5 %collective-permute-start.4 = (bf16[144,256]{1,0:T(8,128)(2,1)S(1)}, bf16[144,256]{1,0:T(8,128)(2,1)S(1)}, u32[]{:S(2)}, u32[]{:S(2)}) collective-permute-start(bf16[144,256]{1,0:T(8,128)(2,1)S(1)} %get-tuple-element.32.refs_0_), channel_id=1, source_target_pairs={{0,16},{2,18},{4,20},{6,22},{8,24},{10,26},{12,28},{14,30},{16,0},... | collective-permute-start | bytes 221192 | tf_op jit(solution)/shard_map/ppermute | solution.py:592
  27.3 6.3 %collective-permute-start.3 = (bf16[128,256]{1,0:T(8,128)(2,1)S(1)}, bf16[128,256]{1,0:T(8,128)(2,1)S(1)}, u32[]{:S(2)}, u32[]{:S(2)}) collective-permute-start(bf16[128,256]{1,0:T(8,128)(2,1)S(1)} %get-tuple-element.33), channel_id=1, source_target_pairs={{0,8},{2,10},{4,12},{6,14},{8,16},{10,18},{12,20},{14,22},{16,24},... | collective-permute-start | bytes 196616 | tf_op jit(solution)/shard_map/ppermute | solution.py:595
  30.8 3.2 %collective-permute-start.5 = (bf16[128,256]{1,0:T(8,128)(2,1)S(1)}, bf16[128,256]{1,0:T(8,128)(2,1)S(1)}, u32[]{:S(2)}, u32[]{:S(2)}) collective-permute-start(bf16[128,256]{1,0:T(8,128)(2,1)S(1)} %get-tuple-element.33), channel_id=1, source_target_pairs={{0,24},{2,26},{4,28},{6,30},{1,25},{3,27},{5,29},{7,31}} | collective-permute-start | bytes 196616 | tf_op jit(solution)/shard_map/ppermute | solution.py:595
  32.1 5.5 %collective-permute-start = (bf16[144,256]{1,0:T(8,128)(2,1)S(1)}, bf16[144,256]{1,0:T(8,128)(2,1)S(1)}, u32[]{:S(2)}, u32[]{:S(2)}) collective-permute-start(bf16[144,256]{1,0:T(8,128)(2,1)S(1)} %get-tuple-element.32.refs_0_), channel_id=1, source_target_pairs={{0,2},{2,0},{4,6},{6,4},{8,10},{10,8},{12,14},{14,12},{16,18},{18,... | collective-permute-start | bytes 221192 | tf_op jit(solution)/shard_map/ppermute | solution.py:592
  34.0 21.6 %collective-permute-start.6 = (bf16[400,256]{1,0:T(8,128)(2,1)S(1)}, bf16[400,256]{1,0:T(8,128)(2,1)S(1)}, u32[]{:S(2)}, u32[]{:S(2)}) collective-permute-start(bf16[400,256]{1,0:T(8,128)(2,1)S(1)} %join.1.refs_4_), channel_id=1, source_target_pairs={{0,2},{2,0},{4,6},{6,4},{8,10},{10,8},{12,14},{14,12},{16,18},{18,... | collective-permute-start | bytes 614408 | tf_op jit(solution)/shard_map/ppermute | solution.py:592
  35.5 20.0 %collective-permute-start.7 = (bf16[400,256]{1,0:T(8,128)(2,1)S(1)}, bf16[400,256]{1,0:T(8,128)(2,1)S(1)}, u32[]{:S(2)}, u32[]{:S(2)}) collective-permute-start(bf16[400,256]{1,0:T(8,128)(2,1)S(1)} %join.1.refs_4_), channel_id=1, source_target_pairs={{0,4},{2,6},{4,0},{6,2},{8,12},{10,14},{12,8},{14,10},{16,20},{18,... | collective-permute-start | bytes 614408 | tf_op jit(solution)/shard_map/ppermute | solution.py:592
  37.0 10.5 %collective-permute-start.1 = (bf16[144,256]{1,0:T(8,128)(2,1)S(1)}, bf16[144,256]{1,0:T(8,128)(2,1)S(1)}, u32[]{:S(2)}, u32[]{:S(2)}) collective-permute-start(bf16[144,256]{1,0:T(8,128)(2,1)S(1)} %get-tuple-element.32.refs_0_), channel_id=1, source_target_pairs={{0,4},{2,6},{4,0},{6,2},{8,12},{10,14},{12,8},{14,10},{16,20},{18,... | collective-permute-start | bytes 221192 | tf_op jit(solution)/shard_map/ppermute | solution.py:592
  37.6 18.1 %collective-permute-start.8 = (bf16[400,256]{1,0:T(8,128)(2,1)S(1)}, bf16[400,256]{1,0:T(8,128)(2,1)S(1)}, u32[]{:S(2)}, u32[]{:S(2)}) collective-permute-start(bf16[400,256]{1,0:T(8,128)(2,1)S(1)} %join.1.refs_4_), channel_id=1, source_target_pairs={{0,6},{2,4},{4,2},{6,0},{8,14},{10,12},{12,10},{14,8},{16,22},{18,... | collective-permute-start | bytes 614408 | tf_op jit(solution)/shard_map/ppermute | solution.py:592
  47.6 5.3 %collective-permute-start.2 = (bf16[144,256]{1,0:T(8,128)(2,1)S(1)}, bf16[144,256]{1,0:T(8,128)(2,1)S(1)}, u32[]{:S(2)}, u32[]{:S(2)}) collective-permute-start(bf16[144,256]{1,0:T(8,128)(2,1)S(1)} %get-tuple-element.32.refs_0_), channel_id=1, source_target_pairs={{0,6},{2,4},{4,2},{6,0},{8,14},{10,12},{12,10},{14,8},{16,22},{18,... | collective-permute-start | bytes 221192 | tf_op jit(solution)/shard_map/ppermute | solution.py:592
  52.8 2.9 %copy-start.1 = (bf16[1024,1024]{1,0:T(8,128)(2,1)S(1)}, bf16[1024,1024]{1,0:T(8,128)(2,1)}, u32[]{:S(2)}) copy-start(bf16[1024,1024]{1,0:T(8,128)(2,1)} %refs_0_.1) | copy-start | bytes 6291460
  52.8 8.5 %collective-permute-start.19 = (bf16[128,1024]{1,0:T(8,128)(2,1)S(1)}, bf16[128,1024]{1,0:T(8,128)(2,1)S(1)}, u32[]{:S(2)}, u32[]{:S(2)}) collective-permute-start(bf16[128,1024]{1,0:T(8,128)(2,1)S(1)} %get-tuple-element.47), channel_id=1, source_target_pairs={{0,8},{2,10},{4,12},{6,14},{8,0},{10,2},{12,4},{14,6},{16,24},{18,... | collective-permute-start | bytes 786440 | tf_op jit(solution)/shard_map/ppermute | solution.py:592
  55.7 4.9 %copy-start.4 = (bf16[128,1024]{1,0:T(8,128)(2,1)S(1)}, bf16[128,1024]{1,0:T(8,128)(2,1)}, u32[]{:S(2)}) copy-start(bf16[128,1024]{1,0:T(8,128)(2,1)} %hidden_ref.1) | copy-start | bytes 786436
  55.7 4.9 %copy-start.5 = (f32[1024]{0:T(1024)S(1)}, f32[1024]{0:T(1024)}, u32[]{:S(2)}) copy-start(f32[1024]{0:T(1024)} %param.16) | copy-start | bytes 12292
  56.6 13.1 %copy-start.2 = (bf16[1,1024,384]{2,1,0:T(8,128)(2,1)S(1)}, bf16[1,1024,384]{2,1,0:T(8,128)(2,1)}, u32[]{:S(2)}) copy-start(bf16[1,1024,384]{2,1,0:T(8,128)(2,1)} %gate_ref.1) | copy-start | bytes 2359300
  56.6 13.1 %copy-start.3 = (bf16[1,1024,384]{2,1,0:T(8,128)(2,1)S(1)}, bf16[1,1024,384]{2,1,0:T(8,128)(2,1)}, u32[]{:S(2)}) copy-start(bf16[1,1024,384]{2,1,0:T(8,128)(2,1)} %up_ref.1) | copy-start | bytes 2359300
  56.6 4.0 %collective-permute-start.9 = (bf16[64,1024]{1,0:T(8,128)(2,1)S(1)}, bf16[64,1024]{1,0:T(8,128)(2,1)S(1)}, u32[]{:S(2)}, u32[]{:S(2)}) collective-permute-start(bf16[64,1024]{1,0:T(8,128)(2,1)S(1)} %get-tuple-element.41), channel_id=1, source_target_pairs={{0,1},{1,0},{2,3},{3,2},{4,5},{5,4},{6,7},{7,6},{8,9},{9,8},{10,11... | collective-permute-start | bytes 393224 | tf_op jit(solution)/shard_map/ppermute | solution.py:598
  56.7 9.6 %collective-permute-start.17 = (bf16[64,1024]{1,0:T(8,128)(2,1)S(1)}, bf16[64,1024]{1,0:T(8,128)(2,1)S(1)}, u32[]{:S(2)}, u32[]{:S(2)}) collective-permute-start(bf16[64,1024]{1,0:T(8,128)(2,1)S(1)} %get-tuple-element.46), channel_id=1, source_target_pairs={{0,8},{2,10},{4,12},{6,14},{8,0},{10,2},{12,4},{14,6},{16,24},{18,... | collective-permute-start | bytes 393224 | tf_op jit(solution)/shard_map/ppermute | solution.py:592
  60.8 7.1 %collective-permute-start.10 = (bf16[64,1024]{1,0:T(8,128)(2,1)S(1)}, bf16[64,1024]{1,0:T(8,128)(2,1)S(1)}, u32[]{:S(2)}, u32[]{:S(2)}) collective-permute-start(bf16[64,1024]{1,0:T(8,128)(2,1)S(1)} %get-tuple-element.43.refs_0_), channel_id=1, source_target_pairs={{0,2},{2,0},{4,6},{6,4},{8,10},{10,8},{12,14},{14,12},{16,18},{18,... | collective-permute-start | bytes 393224 | tf_op jit(solution)/shard_map/ppermute | solution.py:592
  61.4 17.6 %collective-permute-start.20 = (bf16[128,1024]{1,0:T(8,128)(2,1)S(1)}, bf16[128,1024]{1,0:T(8,128)(2,1)S(1)}, u32[]{:S(2)}, u32[]{:S(2)}) collective-permute-start(bf16[128,1024]{1,0:T(8,128)(2,1)S(1)} %collective-permute-done.19.refs_2_), channel_id=1, source_target_pairs={{0,1},{1,0},{2,3},{3,2},{4,5},{5,4},{6,7},{7,6},{8,9},{9,8},{10,11... | collective-permute-start | bytes 786440 | tf_op jit(solution)/shard_map/ppermute | solution.py:598
  61.4 11.9 %collective-permute-start.13 = (bf16[64,1024]{1,0:T(8,128)(2,1)S(1)}, bf16[64,1024]{1,0:T(8,128)(2,1)S(1)}, u32[]{:S(2)}, u32[]{:S(2)}) collective-permute-start(bf16[64,1024]{1,0:T(8,128)(2,1)S(1)} %get-tuple-element.43.refs_0_), channel_id=1, source_target_pairs={{0,16},{2,18},{4,20},{6,22},{8,24},{10,26},{12,28},{14,30},{16,0},... | collective-permute-start | bytes 393224 | tf_op jit(solution)/shard_map/ppermute | solution.py:592
  66.3 8.5 %collective-permute-start.11 = (bf16[64,1024]{1,0:T(8,128)(2,1)S(1)}, bf16[64,1024]{1,0:T(8,128)(2,1)S(1)}, u32[]{:S(2)}, u32[]{:S(2)}) collective-permute-start(bf16[64,1024]{1,0:T(8,128)(2,1)S(1)} %get-tuple-element.43.refs_0_), channel_id=1, source_target_pairs={{0,4},{2,6},{4,0},{6,2},{8,12},{10,14},{12,8},{14,10},{16,20},{18,... | collective-permute-start | bytes 393224 | tf_op jit(solution)/shard_map/ppermute | solution.py:592
  67.9 8.5 %collective-permute-start.12 = (bf16[64,1024]{1,0:T(8,128)(2,1)S(1)}, bf16[64,1024]{1,0:T(8,128)(2,1)S(1)}, u32[]{:S(2)}, u32[]{:S(2)}) collective-permute-start(bf16[64,1024]{1,0:T(8,128)(2,1)S(1)} %get-tuple-element.43.refs_0_), channel_id=1, source_target_pairs={{0,6},{2,4},{4,2},{6,0},{8,14},{10,12},{12,10},{14,8},{16,22},{18,... | collective-permute-start | bytes 393224 | tf_op jit(solution)/shard_map/ppermute | solution.py:592
  69.3 9.7 %collective-permute-start.18 = (bf16[64,1024]{1,0:T(8,128)(2,1)S(1)}, bf16[64,1024]{1,0:T(8,128)(2,1)S(1)}, u32[]{:S(2)}, u32[]{:S(2)}) collective-permute-start(bf16[64,1024]{1,0:T(8,128)(2,1)S(1)} %collective-permute-done.17.refs_0_), channel_id=1, source_target_pairs={{0,1},{1,0},{2,3},{3,2},{4,5},{5,4},{6,7},{7,6},{8,9},{9,8},{10,11... | collective-permute-start | bytes 393224 | tf_op jit(solution)/shard_map/ppermute | solution.py:598
  73.3 6.9 %collective-permute-start.24 = (bf16[64,1024]{1,0:T(8,128)(2,1)S(1)}, bf16[64,1024]{1,0:T(8,128)(2,1)S(1)}, u32[]{:S(2)}, u32[]{:S(2)}) collective-permute-start(bf16[64,1024]{1,0:T(8,128)(2,1)S(1)} %collective-permute-done.13.refs_4_), channel_id=1, source_target_pairs={{0,2},{2,0},{4,6},{6,4},{8,10},{10,8},{12,14},{14,12},{16,18},{18,... | collective-permute-start | bytes 393224 | tf_op jit(solution)/shard_map/ppermute | solution.py:592
  74.8 7.9 %collective-permute-start.25 = (bf16[64,1024]{1,0:T(8,128)(2,1)S(1)}, bf16[64,1024]{1,0:T(8,128)(2,1)S(1)}, u32[]{:S(2)}, u32[]{:S(2)}) collective-permute-start(bf16[64,1024]{1,0:T(8,128)(2,1)S(1)} %collective-permute-done.13.refs_4_), channel_id=1, source_target_pairs={{0,4},{2,6},{4,0},{6,2},{8,12},{10,14},{12,8},{14,10},{16,20},{18,... | collective-permute-start | bytes 393224 | tf_op jit(solution)/shard_map/ppermute | solution.py:592
  76.3 6.3 %collective-permute-start.26 = (bf16[64,1024]{1,0:T(8,128)(2,1)S(1)}, bf16[64,1024]{1,0:T(8,128)(2,1)S(1)}, u32[]{:S(2)}, u32[]{:S(2)}) collective-permute-start(bf16[64,1024]{1,0:T(8,128)(2,1)S(1)} %collective-permute-done.13.refs_4_), channel_id=1, source_target_pairs={{0,6},{2,4},{4,2},{6,0},{8,14},{10,12},{12,10},{14,8},{16,22},{18,... | collective-permute-start | bytes 393224 | tf_op jit(solution)/shard_map/ppermute | solution.py:592
  77.7 1.3 %copy-start = (bf16[1,384,1024]{2,1,0:T(8,128)(2,1)S(1)}, bf16[1,384,1024]{2,1,0:T(8,128)(2,1)}, u32[]{:S(2)}) copy-start(bf16[1,384,1024]{2,1,0:T(8,128)(2,1)} %down_ref.3) | copy-start | bytes 2359300
  83.8 6.3 %collective-permute-start.27 = (bf16[64,1024]{1,0:T(8,128)(2,1)S(1)}, bf16[64,1024]{1,0:T(8,128)(2,1)S(1)}, u32[]{:S(2)}, u32[]{:S(2)}) collective-permute-start(bf16[64,1024]{1,0:T(8,128)(2,1)S(1)} %get-tuple-element.54), channel_id=1, source_target_pairs={{0,2},{2,0},{4,6},{6,4},{8,10},{10,8},{12,14},{14,12},{16,18},{18,... | collective-permute-start | bytes 393224 | tf_op jit(solution)/shard_map/ppermute | solution.py:592
  85.3 9.1 %collective-permute-start.28 = (bf16[64,1024]{1,0:T(8,128)(2,1)S(1)}, bf16[64,1024]{1,0:T(8,128)(2,1)S(1)}, u32[]{:S(2)}, u32[]{:S(2)}) collective-permute-start(bf16[64,1024]{1,0:T(8,128)(2,1)S(1)} %get-tuple-element.55), channel_id=1, source_target_pairs={{0,4},{2,6},{4,0},{6,2},{8,12},{10,14},{12,8},{14,10},{16,20},{18,... | collective-permute-start | bytes 393224 | tf_op jit(solution)/shard_map/ppermute | solution.py:592
  86.6 7.8 %collective-permute-start.29 = (bf16[64,1024]{1,0:T(8,128)(2,1)S(1)}, bf16[64,1024]{1,0:T(8,128)(2,1)S(1)}, u32[]{:S(2)}, u32[]{:S(2)}) collective-permute-start(bf16[64,1024]{1,0:T(8,128)(2,1)S(1)} %get-tuple-element.56), channel_id=1, source_target_pairs={{0,6},{2,4},{4,2},{6,0},{8,14},{10,12},{12,10},{14,8},{16,22},{18,... | collective-permute-start | bytes 393224 | tf_op jit(solution)/shard_map/ppermute | solution.py:592
  87.4 8.5 %collective-permute-start.21 = (bf16[64,1024]{1,0:T(8,128)(2,1)S(1)}, bf16[64,1024]{1,0:T(8,128)(2,1)S(1)}, u32[]{:S(2)}, u32[]{:S(2)}) collective-permute-start(bf16[64,1024]{1,0:T(8,128)(2,1)S(1)} %get-tuple-element.49), channel_id=1, source_target_pairs={{0,2},{2,0},{4,6},{6,4},{8,10},{10,8},{12,14},{14,12},{16,18},{18,... | collective-permute-start | bytes 393224 | tf_op jit(solution)/shard_map/ppermute | solution.py:592
  88.8 8.9 %collective-permute-start.22 = (bf16[64,1024]{1,0:T(8,128)(2,1)S(1)}, bf16[64,1024]{1,0:T(8,128)(2,1)S(1)}, u32[]{:S(2)}, u32[]{:S(2)}) collective-permute-start(bf16[64,1024]{1,0:T(8,128)(2,1)S(1)} %get-tuple-element.50), channel_id=1, source_target_pairs={{0,4},{2,6},{4,0},{6,2},{8,12},{10,14},{12,8},{14,10},{16,20},{18,... | collective-permute-start | bytes 393224 | tf_op jit(solution)/shard_map/ppermute | solution.py:592
  90.2 7.5 %collective-permute-start.23 = (bf16[64,1024]{1,0:T(8,128)(2,1)S(1)}, bf16[64,1024]{1,0:T(8,128)(2,1)S(1)}, u32[]{:S(2)}, u32[]{:S(2)}) collective-permute-start(bf16[64,1024]{1,0:T(8,128)(2,1)S(1)} %get-tuple-element.51), channel_id=1, source_target_pairs={{0,6},{2,4},{4,2},{6,0},{8,14},{10,12},{12,10},{14,8},{16,22},{18,... | collective-permute-start | bytes 393224 | tf_op jit(solution)/shard_map/ppermute | solution.py:592
  94.5 7.3 %collective-permute-start.30 = (bf16[64,1024]{1,0:T(8,128)(2,1)S(1)}, bf16[64,1024]{1,0:T(8,128)(2,1)S(1)}, u32[]{:S(2)}, u32[]{:S(2)}) collective-permute-start(bf16[64,1024]{1,0:T(8,128)(2,1)S(1)} %gather_sum.1), channel_id=1, source_target_pairs={{0,16},{2,18},{4,20},{6,22},{8,24},{10,26},{12,28},{14,30},{16,0},... | collective-permute-start | bytes 393224 | tf_op jit(solution)/shard_map/ppermute | solution.py:592
  101.9 1.3 %collective-permute-start.31 = (bf16[64,512]{1,0:T(8,128)(2,1)S(1)}, bf16[64,512]{1,0:T(8,128)(2,1)S(1)}, u32[]{:S(2)}, u32[]{:S(2)}) collective-permute-start(bf16[64,512]{1,0:T(8,128)(2,1)S(1)} %get-tuple-element.58), channel_id=1, source_target_pairs={{0,1},{1,0},{2,3},{3,2},{4,5},{5,4},{6,7},{7,6},{8,9},{9,8},{10,11... | collective-permute-start | bytes 196616 | tf_op jit(solution)/shard_map/ppermute | solution.py:598
